TPU v7x, 32 devices: a whole 2x2x4 slice. The times are simulated.
32 devices in a mesh: grp: 2 (over x), rows: 4 (over y, core), chan: 4 (over z).
Axes of the slice: x: 2, y: 2, z: 4, core: 2. Of those that a mesh axis runs over, the one named last changes fastest.
Arguments:
- frames_in: bfloat16 [512, 4, 16, 96], P('chan', None, ('grp', 'rows')), parts along dimension 2, may hold values from -48 to 48
- cache_first: bfloat16 [512, 2, 16, 96], P('chan', None, ('grp', 'rows')), parts along dimension 2, may hold values from -6 to 6
- gain_first: float32 [512], P('chan'), may hold values from 0.1 to 1.9
- shift_first: float32 [512], P('chan'), may hold values from -3 to 3
- kernel_first: bfloat16 [3, 3, 3, 512, 512], P(None, None, None, 'chan'), may hold values from -0.0625 to 0.0625
- bias_first: float32 [512], P('chan'), may hold values from -3 to 3
- cache_second: bfloat16 [512, 2, 16, 96], P('chan', None, ('grp', 'rows')), parts along dimension 2, may hold values from -6 to 6
- gain_second: float32 [512], P('chan'), may hold values from 0.1 to 1.9
- shift_second: float32 [512], P('chan'), may hold values from -3 to 3
- kernel_second: bfloat16 [3, 3, 3, 512, 512], P(None, None, None, 'chan'), may hold values from -0.0625 to 0.0625
- bias_second: float32 [512], P('chan'), may hold values from -3 to 3
Outputs:
- decoded: bfloat16 [512, 4, 16, 96], P('chan', None, ('grp', 'rows')), parts along dimension 2
- next_cache: bfloat16 [512, 2, 16, 96], P('chan', None, ('grp', 'rows')), parts along dimension 2
There are 2 independent parts, one for each index of `grp`. A program takes and returns all parts, laid end to end along the dimension named above; an argument that names none is the same for every part. Nothing has to cross between parts.
All inputs are finite; a program needn't handle non-finite values.
Results may differ from a plain program's by a relative error of at most 0.009.
Values may be sent and summed in bfloat16 or wider, within the bound.
No kernel may reach another device: no remote copies, remote signals or barrier semaphores. Data moves between devices by JAX's collectives and lax.ppermute only.
A program may use at most 128 MiB of HBM per device.

v0:
```python
import jax
import jax.numpy as jnp
from jax import lax
from jax.sharding import PartitionSpec as P

CHANNELS = 512
GROUPS = 32


def extended(block, sides, width):
    for axis, dim in sides:
        count = lax.axis_size(axis)
        forward = [(i, i + 1) for i in range(count - 1)]
        backward = [(target, source) for source, target in forward]
        low = lax.ppermute(
            lax.slice_in_dim(block, block.shape[dim] - width, None, axis=dim), axis, forward
        )
        high = lax.ppermute(lax.slice_in_dim(block, 0, width, axis=dim), axis, backward)
        block = jnp.concatenate([low, block, high], axis=dim)
    return block


def norm_act(values, gain, shift):
    per_group = CHANNELS // GROUPS
    grouped = values.reshape(values.shape[0] // per_group, -1)
    moments = lax.psum((jnp.sum(grouped, axis=1), jnp.sum(grouped * grouped, axis=1)), "rows")
    entries = grouped.shape[1] * lax.axis_size("rows")
    average = (moments[0] / entries)[:, None]
    squares = (moments[1] / entries)[:, None]
    scaled = ((grouped - average) * lax.rsqrt(squares - average * average + 1e-06)).reshape(
        values.shape
    )
    affine = scaled * gain[:, None, None, None] + shift[:, None, None, None]
    return jax.nn.silu(affine).astype(jnp.bfloat16)


def build_columns(padded, frames):
    widened = jnp.pad(padded, ((0, 0), (0, 0), (0, 0), (1, 1)))
    channel_count = padded.shape[0]
    band_rows = padded.shape[2] - 2
    width_cells = padded.shape[3]
    shifted = [
        widened[:, :, row_tap : row_tap + band_rows, col_tap : col_tap + width_cells]
        for row_tap in range(3)
        for col_tap in range(3)
    ]
    merged = jnp.stack(shifted, 0).reshape(9 * channel_count, frames + 2, band_rows * width_cells)
    return jnp.stack(
        [
            merged[:, time_tap : time_tap + frames].reshape(9 * channel_count, -1)
            for time_tap in range(3)
        ],
        0,
    )


def weight_rows(kernel):
    return kernel.reshape(3, 9 * kernel.shape[3], kernel.shape[4])


def contract(weights, columns):
    running = None
    for time_tap in range(3):
        product = lax.dot_general(
            weights[time_tap],
            columns[time_tap],
            (((0,), (0,)), ((), ())),
            preferred_element_type=jnp.float32,
        )
        running = product if running is None else running + product
    return running


def causal_conv(history, current, kernel, bias):
    joined = jnp.concatenate([history, current], axis=1)
    padded = extended(joined, (("rows", 2),), 1)
    frames = current.shape[1]
    columns = build_columns(padded, frames)
    weights = weight_rows(kernel)
    summed = lax.psum_scatter(contract(weights, columns), "chan", scatter_dimension=0, tiled=True)
    shaped = summed.reshape(current.shape)
    return (shaped + bias[:, None, None, None]).astype(jnp.bfloat16)


def local(
    frames_in,
    cache_first,
    gain_first,
    shift_first,
    kernel_first,
    bias_first,
    cache_second,
    gain_second,
    shift_second,
    kernel_second,
    bias_second,
):
    activated = norm_act(frames_in.astype(jnp.float32), gain_first, shift_first)
    hidden = causal_conv(cache_first, activated, kernel_first, bias_first)
    second = norm_act(hidden.astype(jnp.float32), gain_second, shift_second)
    decoded = causal_conv(cache_second, second, kernel_second, bias_second)
    return (decoded, second[:, second.shape[1] - 2 :])


def solution(mesh):
    return jax.shard_map(
        local,
        mesh=mesh,
        in_specs=(
            P("chan", None, ("grp", "rows"), None),
            P("chan", None, ("grp", "rows"), None),
            P("chan"),
            P("chan"),
            P(None, None, None, "chan", None),
            P("chan"),
            P("chan", None, ("grp", "rows"), None),
            P("chan"),
            P("chan"),
            P(None, None, None, "chan", None),
            P("chan"),
        ),
        out_specs=(P("chan", None, ("grp", "rows"), None), P("chan", None, ("grp", "rows"), None)),
        check_vma=False,
    )
```

profile of v0, /device:TPU:0, one launch (start us, length us, event | category | flops | bytes accessed | tf_op | source)
XLA Modules:
  0.0 197.1 jit_solution(10141624197693270246)
XLA Ops:
  8.6 8.4 %all-reduce.3 = (f32[8]{0:T(128)S(1)}, f32[8]{0:T(128)S(1)}) all-reduce(f32[8]{0:T(128)S(1)} %reduce_sum.54, f32[8]{0:T(128)S(1)} %reduce_sum.51), channel_id=1, replica_groups=mesh['grp'=2,'rows'=4,'chan'=4] {'rows'}, use_global_device_ids=true, to_apply=%region_5.6 | all-reduce | flops 16 | bytes 128 | tf_op jit(solution)/shard_map/psum | solution.py:26
  22.1 3.8 %fusion.52 = (bf16[1,3,3,128,512]{4,3,2,1,0:T(8,128)(2,1)}, bf16[1,3,3,128,512]{4,3,2,1,0:T(8,128)(2,1)}, bf16[1,3,3,128,512]{4,3,2,1,0:T(8,128)(2,1)}) fusion(bf16[3,3,3,128,512]{4,3,2,1,0:T(8,128)(2,1)} %param.15), kind=kLoop, calls=%fused_computation.101 | loop fusion | bytes 7077888 | tf_op jit(solution)/shard_map/slice | solution.py:65
  26.7 6.3 %copy.13 = bf16[9,128,6,2,96]{4,3,1,0,2:T(2,128)(2,1)} copy(bf16[9,128,6,2,96]{1,4,3,2,0:T(8,128)(2,1)S(1)} %fusion.36) | data formatting | bytes 5308416 | tf_op jit(solution)/shard_map/stack | solution.py:47
  33.0 6.7 %reshape.65 = bf16[1152,6,192]{2,0,1:T(8,128)(2,1)S(1)} reshape(bf16[9,128,6,2,96]{4,3,1,0,2:T(2,128)(2,1)} %copy.13) | data formatting | bytes 5308416 | tf_op jit(solution)/shard_map/reshape | solution.py:47
  39.7 3.1 %fusion.53 = (bf16[1152,4,192]{2,0,1:T(8,128)(2,1)}, bf16[1152,4,192]{2,0,1:T(8,128)(2,1)}, bf16[1152,4,192]{2,0,1:T(8,128)(2,1)}) fusion(bf16[1152,6,192]{2,0,1:T(8,128)(2,1)S(1)} %reshape.65), kind=kLoop, calls=%fused_computation.102 | loop fusion | bytes 10616832 | tf_op jit(solution)/shard_map/slice | solution.py:50
  42.8 4.2 %copy.16 = bf16[1152,4,192]{0,2,1:T(8,128)(2,1)} copy(bf16[1152,4,192]{2,0,1:T(8,128)(2,1)} %get-tuple-element.19) | data formatting | bytes 3538944 | tf_op jit(solution)/shard_map/slice | solution.py:50
  46.9 4.3 %copy.15 = bf16[1152,4,192]{0,2,1:T(8,128)(2,1)} copy(bf16[1152,4,192]{2,0,1:T(8,128)(2,1)} %get-tuple-element.20) | data formatting | bytes 3538944 | tf_op jit(solution)/shard_map/slice | solution.py:50
  51.2 2.4 %copy.14 = bf16[1152,4,192]{0,2,1:T(8,128)(2,1)} copy(bf16[1152,4,192]{2,0,1:T(8,128)(2,1)S(1)} %copy-done) | data formatting | bytes 3538944 | tf_op jit(solution)/shard_map/slice | solution.py:50
  53.7 2.8 %fusion.55 = f32[768,512]{1,0:T(8,128)S(1)} fusion(bf16[1152,768]{0,1:T(8,128)(2,1)} %bitcast.110, bf16[1152,512]{1,0:T(8,128)(2,1)S(1)} %bitcast.117), kind=kOutput, calls=%fused_computation.104 | convolution fusion | flops 905969664 | bytes 4521984 | tf_op jit(solution)/shard_map/dot_general | solution.py:64
  58.3 2.3 %add_bitcast_fusion.1 = f32[512,768]{0,1:T(8,128)} fusion(f32[768,512]{1,0:T(8,128)S(1)} %fusion.54, f32[768,512]{1,0:T(8,128)S(1)} %fusion.55, bf16[1152,768]{0,1:T(8,128)(2,1)S(1)} %bitcast.106, bf16[1152,512]{1,0:T(8,128)(2,1)S(1)} %bitcast.108), kind=kOutput, calls=%fused_computation.3 | convolution fusion | flops 906756096 | bytes 7667712 | tf_op jit(solution)/shard_map/dot_general | solution.py:64
  60.7 38.7 %reduce-scatter.3.cloned.1.call-done = f32[128,768]{0,1:T(8,128)} async-done(((f32[512,768]{0,1:T(8,128)}), f32[128,768]{0,1:T(8,128)}) %reduce-scatter.3.cloned.1.call-update) | async-done | bytes 393232 | tf_op jit(solution)/shard_map/reduce_scatter | solution.py:80
  100.9 6.7 %all-reduce.2 = (f32[8]{0:T(128)S(1)}, f32[8]{0:T(128)}) all-reduce(f32[8]{0:T(128)S(1)} %reduce_sum.75, f32[8]{0:T(128)S(1)} %reduce_sum.72), channel_id=1, replica_groups=mesh['grp'=2,'rows'=4,'chan'=4] {'rows'}, use_global_device_ids=true, to_apply=%region_12.13 | all-reduce | flops 16 | bytes 128 | tf_op jit(solution)/shard_map/psum | solution.py:26
  112.0 1.6 collective-permute-start.3
  113.7 1.9 fusion.50
  117.7 6.3 %copy.17 = bf16[9,128,6,2,96]{4,3,1,0,2:T(2,128)(2,1)} copy(bf16[9,128,6,2,96]{1,4,3,2,0:T(8,128)(2,1)S(1)} %fusion.26) | data formatting | bytes 5308416 | tf_op jit(solution)/shard_map/stack | solution.py:47
  124.0 6.7 %reshape.67 = bf16[1152,6,192]{2,0,1:T(8,128)(2,1)S(1)} reshape(bf16[9,128,6,2,96]{4,3,1,0,2:T(2,128)(2,1)} %copy.17) | data formatting | bytes 5308416 | tf_op jit(solution)/shard_map/reshape | solution.py:47
  130.7 3.1 %fusion.51 = (bf16[1152,4,192]{2,0,1:T(8,128)(2,1)}, bf16[1152,4,192]{2,0,1:T(8,128)(2,1)}, bf16[1152,4,192]{2,0,1:T(8,128)(2,1)}) fusion(bf16[1152,6,192]{2,0,1:T(8,128)(2,1)S(1)} %reshape.67), kind=kLoop, calls=%fused_computation.100 | loop fusion | bytes 10616832 | tf_op jit(solution)/shard_map/slice | solution.py:50
  133.8 4.2 %copy.20 = bf16[1152,4,192]{0,2,1:T(8,128)(2,1)} copy(bf16[1152,4,192]{2,0,1:T(8,128)(2,1)} %get-tuple-element.13) | data formatting | bytes 3538944 | tf_op jit(solution)/shard_map/slice | solution.py:50
  137.9 4.3 %copy.19 = bf16[1152,4,192]{0,2,1:T(8,128)(2,1)} copy(bf16[1152,4,192]{2,0,1:T(8,128)(2,1)} %get-tuple-element.14) | data formatting | bytes 3538944 | tf_op jit(solution)/shard_map/slice | solution.py:50
  142.2 2.4 %copy.18 = bf16[1152,4,192]{0,2,1:T(8,128)(2,1)} copy(bf16[1152,4,192]{2,0,1:T(8,128)(2,1)S(1)} %copy-done.1) | data formatting | bytes 3538944 | tf_op jit(solution)/shard_map/slice | solution.py:50
  144.7 2.8 %fusion.57 = f32[768,512]{1,0:T(8,128)S(1)} fusion(bf16[1152,768]{0,1:T(8,128)(2,1)} %bitcast.112, bf16[1152,512]{1,0:T(8,128)(2,1)S(1)} %bitcast.118), kind=kOutput, calls=%fused_computation.106 | convolution fusion | flops 905969664 | bytes 4521984 | tf_op jit(solution)/shard_map/dot_general | solution.py:64
  149.3 2.3 %add_bitcast_fusion = f32[512,768]{0,1:T(8,128)} fusion(f32[768,512]{1,0:T(8,128)S(1)} %fusion.56, f32[768,512]{1,0:T(8,128)S(1)} %fusion.57, bf16[1152,768]{0,1:T(8,128)(2,1)S(1)} %bitcast.107, bf16[1152,512]{1,0:T(8,128)(2,1)S(1)} %bitcast.109), kind=kOutput, calls=%fused_computation.2 | convolution fusion | flops 906756096 | bytes 7667712 | tf_op jit(solution)/shard_map/dot_general | solution.py:64
  152.3 36.2 %reduce-scatter.5.cloned.1.call-done = f32[128,768]{0,1:T(8,128)} async-done(((f32[512,768]{0,1:T(8,128)}), f32[128,768]{0,1:T(8,128)}) %reduce-scatter.5.cloned.1.call-update) | async-done | bytes 393232 | tf_op jit(solution)/shard_map/reduce_scatter | solution.py:80
  188.5 1.7 add_convert_fusion
  (96 shorter events, 19.6 us)
Async XLA Ops:
  7.2 92.3 %reduce-scatter.3.cloned.1.call-start = ((), (), s32[]{:S(2)}) async-start(), calls=%async_computation.2 | async-start | bytes 1966080 | tf_op jit(solution)/shard_map/reduce_scatter | solution.py:80
  19.3 6.6 %collective-permute-start = (bf16[128,6,1,96]{0,3,2,1:T(8,128)(2,1)S(1)}, bf16[128,6,1,96]{0,3,2,1:T(8,128)(2,1)S(1)}, u32[]{:S(2)}, u32[]{:S(2)}) collective-permute-start(bf16[128,6,1,96]{0,3,2,1:T(8,128)(2,1)S(1)} %get-tuple-element.24), channel_id=1, source_target_pairs={{0,4},{4,8},{8,12},{1,5},{5,9},{9,13},{2,6},{6,10},{10,14},{3,7},{... | collective-permute-start | bytes 442376 | tf_op jit(solution)/shard_map/ppermute | solution.py:15
  20.6 5.3 %copy-start.9 = (bf16[128,2,2,96]{0,3,2,1:T(8,128)(2,1)S(1)}, bf16[128,2,2,96]{0,3,2,1:T(8,128)(2,1)}, u32[]{:S(2)}) copy-start(bf16[128,2,2,96]{0,3,2,1:T(8,128)(2,1)} %param.12) | copy-start | bytes 294916
  20.7 5.2 %collective-permute-start.1 = (bf16[128,6,1,96]{0,3,2,1:T(8,128)(2,1)S(1)}, bf16[128,6,1,96]{0,3,2,1:T(8,128)(2,1)S(1)}, u32[]{:S(2)}, u32[]{:S(2)}) collective-permute-start(bf16[128,6,1,96]{0,3,2,1:T(8,128)(2,1)S(1)} %get-tuple-element.25), channel_id=1, source_target_pairs={{4,0},{8,4},{12,8},{5,1},{9,5},{13,9},{6,2},{10,6},{14,10},{7,3},{... | collective-permute-start | bytes 442376 | tf_op jit(solution)/shard_map/ppermute | solution.py:18
  46.9 4.3 %copy-start = (bf16[1152,4,192]{2,0,1:T(8,128)(2,1)S(1)}, bf16[1152,4,192]{2,0,1:T(8,128)(2,1)}, u32[]{:S(2)}) copy-start(bf16[1152,4,192]{2,0,1:T(8,128)(2,1)} %get-tuple-element.21) | copy-start | bytes 5308420
  51.2 2.4 %copy-start.15 = (bf16[1,3,3,128,512]{4,3,2,1,0:T(8,128)(2,1)S(1)}, bf16[1,3,3,128,512]{4,3,2,1,0:T(8,128)(2,1)}, u32[]{:S(2)}) copy-start(bf16[1,3,3,128,512]{4,3,2,1,0:T(8,128)(2,1)} %get-tuple-element.18) | copy-start | bytes 3538948
  53.7 2.8 %copy-start.11 = (bf16[1152,4,192]{0,2,1:T(8,128)(2,1)S(1)}, bf16[1152,4,192]{0,2,1:T(8,128)(2,1)}, u32[]{:S(2)}) copy-start(bf16[1152,4,192]{0,2,1:T(8,128)(2,1)} %copy.14) | copy-start | bytes 5308420
  53.7 2.8 %copy-start.13 = (bf16[1,3,3,128,512]{4,3,2,1,0:T(8,128)(2,1)S(1)}, bf16[1,3,3,128,512]{4,3,2,1,0:T(8,128)(2,1)}, u32[]{:S(2)}) copy-start(bf16[1,3,3,128,512]{4,3,2,1,0:T(8,128)(2,1)} %get-tuple-element.17) | copy-start | bytes 3538948
  56.5 1.5 copy-start.4
  56.5 1.8 copy-start.6
  58.3 41.1 %copy-start.17 = (f32[128]{0:T(128)S(1)}, f32[128]{0:T(128)}, u32[]{:S(2)}) copy-start(f32[128]{0:T(128)} %param.16) | copy-start | bytes 1540
  58.3 55.4 %copy-start.8 = (bf16[3,3,3,128,512]{4,3,2,1,0:T(8,128)(2,1)S(1)}, bf16[3,3,3,128,512]{4,3,2,1,0:T(8,128)(2,1)}, u32[]{:S(2)}) copy-start(bf16[3,3,3,128,512]{4,3,2,1,0:T(8,128)(2,1)} %param.20) | copy-start | bytes 10616836
  60.7 127.9 %reduce-scatter.5.cloned.1.call-start = ((), (), s32[]{:S(2)}) async-start(), calls=%async_computation.3 | async-start | bytes 1966080 | tf_op jit(solution)/shard_map/reduce_scatter | solution.py:80
  109.8 7.8 %copy-start.2 = (bf16[128,4,2,96]{0,3,2,1:T(8,128)(2,1)}, bf16[128,4,2,96]{0,3,2,1:T(8,128)(2,1)S(1)}, u32[]{:S(2)}) copy-start(bf16[128,4,2,96]{0,3,2,1:T(8,128)(2,1)S(1)} %multiply_convert_fusion) | copy-start | bytes 589828
  110.7 4.8 %collective-permute-start.2 = (bf16[128,6,1,96]{0,3,2,1:T(8,128)(2,1)S(1)}, bf16[128,6,1,96]{0,3,2,1:T(8,128)(2,1)S(1)}, u32[]{:S(2)}, u32[]{:S(2)}) collective-permute-start(bf16[128,6,1,96]{0,3,2,1:T(8,128)(2,1)S(1)} %get-tuple-element.22), channel_id=1, source_target_pairs={{0,4},{4,8},{8,12},{1,5},{5,9},{9,13},{2,6},{6,10},{10,14},{3,7},{... | collective-permute-start | bytes 442376 | tf_op jit(solution)/shard_map/ppermute | solution.py:15
  112.0 4.9 %copy-start.10 = (bf16[128,2,2,96]{0,3,2,1:T(8,128)(2,1)S(1)}, bf16[128,2,2,96]{0,3,2,1:T(8,128)(2,1)}, u32[]{:S(2)}) copy-start(bf16[128,2,2,96]{0,3,2,1:T(8,128)(2,1)} %param.17) | copy-start | bytes 294916
  112.0 4.9 %collective-permute-start.3 = (bf16[128,6,1,96]{0,3,2,1:T(8,128)(2,1)S(1)}, bf16[128,6,1,96]{0,3,2,1:T(8,128)(2,1)S(1)}, u32[]{:S(2)}, u32[]{:S(2)}) collective-permute-start(bf16[128,6,1,96]{0,3,2,1:T(8,128)(2,1)S(1)} %get-tuple-element.23), channel_id=1, source_target_pairs={{4,0},{8,4},{12,8},{5,1},{9,5},{13,9},{6,2},{10,6},{14,10},{7,3},{... | collective-permute-start | bytes 442376 | tf_op jit(solution)/shard_map/ppermute | solution.py:18
  137.9 4.3 %copy-start.1 = (bf16[1152,4,192]{2,0,1:T(8,128)(2,1)S(1)}, bf16[1152,4,192]{2,0,1:T(8,128)(2,1)}, u32[]{:S(2)}) copy-start(bf16[1152,4,192]{2,0,1:T(8,128)(2,1)} %get-tuple-element.15) | copy-start | bytes 5308420
  142.2 2.4 %copy-start.16 = (bf16[1,3,3,128,512]{4,3,2,1,0:T(8,128)(2,1)S(1)}, bf16[1,3,3,128,512]{4,3,2,1,0:T(8,128)(2,1)}, u32[]{:S(2)}) copy-start(bf16[1,3,3,128,512]{4,3,2,1,0:T(8,128)(2,1)} %get-tuple-element.12) | copy-start | bytes 3538948
  144.7 2.8 %copy-start.12 = (bf16[1152,4,192]{0,2,1:T(8,128)(2,1)S(1)}, bf16[1152,4,192]{0,2,1:T(8,128)(2,1)}, u32[]{:S(2)}) copy-start(bf16[1152,4,192]{0,2,1:T(8,128)(2,1)} %copy.18) | copy-start | bytes 5308420
  144.7 2.8 %copy-start.14 = (bf16[1,3,3,128,512]{4,3,2,1,0:T(8,128)(2,1)S(1)}, bf16[1,3,3,128,512]{4,3,2,1,0:T(8,128)(2,1)}, u32[]{:S(2)}) copy-start(bf16[1,3,3,128,512]{4,3,2,1,0:T(8,128)(2,1)} %get-tuple-element.11) | copy-start | bytes 3538948
  147.5 1.8 copy-start.7
  149.3 2.4 %copy-start.3 = (bf16[128,4,2,96]{0,3,2,1:T(8,128)(2,1)S(1)}, bf16[128,4,2,96]{0,3,2,1:T(8,128)(2,1)}, u32[]{:S(2)}) copy-start(bf16[128,4,2,96]{0,3,2,1:T(8,128)(2,1)} %copy-done.2) | copy-start | bytes 589828
  151.6 36.9 %copy-start.18 = (f32[128]{0:T(128)S(1)}, f32[128]{0:T(128)}, u32[]{:S(2)}) copy-start(f32[128]{0:T(128)} %param.21) | copy-start | bytes 1540
  (1 other events, 1.5 us)
Sparse Core Ops, SparseCore 0:
  60.8 38.6 reduce-scatter.2
  151.8 36.7 reduce-scatter.4
where the time goes:
time: 198 us; the launch traced here: 197 us
  waiting for transfers between devices  76.3 us (39%)
  local copies, waits for them, and re-layouts  63.3 us (32%)
  blocking collectives  15.1 us (8%)
  between operations  14.4 us (7%)
  matrix products  12.6 us (6%)
  other arithmetic  9.73 us (5%)
  starting transfers between devices  5.7 us (3%)
    reduce_scatter x2, waiting for transfers between devices, causal_conv(): lax.psum_scatter(contract(weights, columns), 'chan', scatter_dimension=0,...  74.9 us
    slice x8, local copies, waits for them, and re-layouts, build_columns(): merged[:, time_tap:time_tap + frames].reshape(9 * channel_count, -1)  27.9 us
    psum x2, blocking collectives, norm_act(): lax.psum((jnp.sum(grouped, axis=1), jnp.sum(grouped * grouped, axis=1)),...  15.1 us
    reshape x2, local copies, waits for them, and re-layouts, build_columns(): jnp.stack(shifted, 0)  13.4 us
    another operation x4, local copies, waits for them, and re-layouts, build_columns(): jnp.stack(shifted, 0)  12.8 us
    dot_general x6, matrix products, contract(): lax.dot_general(weights[time_tap], columns[time_tap], (((0,), (0,)), ((),...  12.6 us
    slice x2, local copies, waits for them, and re-layouts, contract(): weights[time_tap]  5.66 us
  transfers between devices with their start and end apart: 6, of which 3 were waited for; matrix products, arithmetic and copies ran while one was open for 3% of the time, Pallas kernels for 0%

commit v1 on v0

v1 whole, which is shorter than its diff:
```python
import functools

import jax
import jax.numpy as jnp
from jax import lax
from jax.experimental import pallas as pl
from jax.experimental.pallas import tpu as pltpu
from jax.sharding import PartitionSpec as P

CHANNELS = 512
GROUPS = 32
EPS = 1e-06
LANES = 128
VMEM = 24 * 1024 * 1024


def params():
    return pltpu.CompilerParams(vmem_limit_bytes=VMEM)


def full():
    return pl.BlockSpec(memory_space=pltpu.VMEM)


def call(body, outs, args, flops=0, name=None):
    moved = sum(a.size * a.dtype.itemsize for a in (*args, *outs))
    return pl.pallas_call(
        body,
        out_shape=outs,
        in_specs=[full()] * len(args),
        out_specs=[full()] * len(outs),
        compiler_params=params(),
        cost_estimate=pl.CostEstimate(flops=flops, bytes_accessed=moved, transcendentals=0),
        name=name,
    )(*args)


def store_moments(ref, values):
    total = jnp.sum(values, axis=0, keepdims=True)
    squares = jnp.sum(values * values, axis=0, keepdims=True)
    rest = jnp.zeros((ref.shape[0] - 2, ref.shape[1]), jnp.float32)
    ref[...] = jnp.concatenate([total, squares, rest], axis=0)


def entry_body(x, first, second, moments, down, up):
    frames, rows, width, channels = x.shape
    store_moments(moments, x[...].astype(jnp.float32).reshape(-1, channels))
    place = 0
    for ref in (x, first, second):
        count = ref.shape[0]
        down[place : place + count] = ref[:, rows - 1]
        up[place : place + count] = ref[:, 0]
        place += count


def entry(x, first, second):
    frames, _, width, channels = x.shape
    edge = jax.ShapeDtypeStruct(
        (frames + first.shape[0] + second.shape[0], width, channels), x.dtype
    )
    outs = [jax.ShapeDtypeStruct((8, channels), jnp.float32), edge, edge]
    return call(entry_body, outs, (x, first, second), name="entry")


def middle_body(count, *refs):
    own, terms, bias = refs[0], refs[1 : 1 + count], refs[1 + count]
    hidden, moments, down, up = refs[2 + count :]
    frames, rows, width, channels = hidden.shape
    total = own[...]
    for term in terms:
        total = total + term[...].astype(jnp.float32)
    rounded = (total + bias[...]).astype(jnp.bfloat16)
    store_moments(moments, rounded.astype(jnp.float32))
    shaped = rounded.reshape(hidden.shape)
    hidden[...] = shaped
    down[...] = shaped[:, rows - 1]
    up[...] = shaped[:, 0]


def middle(own, terms, bias, shape):
    frames, _, width, channels = shape
    edge = jax.ShapeDtypeStruct((frames, width, channels), jnp.bfloat16)
    outs = [
        jax.ShapeDtypeStruct(shape, jnp.bfloat16),
        jax.ShapeDtypeStruct((8, channels), jnp.float32),
        edge,
        edge,
    ]
    body = functools.partial(middle_body, len(terms))
    return call(body, outs, (own, *terms, bias), name="middle")


def close_body(count, *refs):
    own, terms, bias, out = refs[0], refs[1 : 1 + count], refs[1 + count], refs[2 + count]
    total = own[...]
    for term in terms:
        total = total + term[...].astype(jnp.float32)
    out[...] = (total + bias[...]).astype(out.dtype).reshape(out.shape)


def close(own, terms, bias, shape):
    outs = [jax.ShapeDtypeStruct(shape, jnp.bfloat16)]
    body = functools.partial(close_body, len(terms))
    return call(body, outs, (own, *terms, bias), name="close")[0]


def blocks_in_order(count):
    mine = lax.axis_index("chan")
    if count != 4:
        return list(range(count))
    far = jnp.where(mine % 2 == 0, count - 1, 0)
    near = jnp.where(mine < 2, 2, 1)
    return [far, near, 6 - far - near - mine, mine]


def products(shifted, weights, blocks, outs):
    _, frames, rows, width, channels = shifted.shape
    frames, rows = frames - 2, rows - 2
    total = None
    for time_tap in range(3):
        for row_tap in range(3):
            window = [
                shifted[col_tap, time_tap : time_tap + frames, row_tap : row_tap + rows].reshape(
                    frames * rows * width, channels
                )
                for col_tap in range(3)
            ]
            left = jnp.concatenate(window, axis=1)
            right = []
            for block in blocks:
                start = block * channels
                if not isinstance(block, int):
                    start = pl.multiple_of(start, channels)
                right.append(weights[3 * time_tap + row_tap, :, pl.ds(start, channels)])
            right = jnp.concatenate(right, axis=1)
            product = jnp.dot(left, right, preferred_element_type=jnp.float32)
            total = product if total is None else total + product
    for place, out in enumerate(outs):
        out[...] = total[:, place * channels : (place + 1) * channels].astype(out.dtype)


def conv_body(entries, offset, slots, keep, *refs):
    x, top, bottom, cache, cache_top, cache_bottom, moments, gain, shift, weights = refs[:10]
    shifted, outs = refs[10], refs[11 : 11 + slots]
    frames, rows, width, channels = x.shape
    history = cache.shape[0]
    per_group = CHANNELS // GROUPS
    shape = (channels, channels)
    member = (
        lax.broadcasted_iota(jnp.int32, shape, 0) // per_group
        == lax.broadcasted_iota(jnp.int32, shape, 1) // per_group
    ).astype(jnp.float32)
    grouped = jnp.dot(
        moments[...], member, precision=lax.Precision.HIGHEST, preferred_element_type=jnp.float32
    ) * (1.0 / entries)
    average, squares = grouped[0:1], grouped[1:2]
    scale = lax.rsqrt(squares - average * average + EPS) * gain[...]
    place = lax.axis_index("rows")
    inside = [
        (place > 0).astype(jnp.float32),
        (place < lax.axis_size("rows") - 1).astype(jnp.float32),
    ]
    column = lax.broadcasted_iota(jnp.int32, (width, channels), 0)

    def put(frame, row, value):
        before = jnp.where(column == 0, 0.0, pltpu.roll(value, 1, 0))
        after = jnp.where(column == width - 1, 0.0, pltpu.roll(value, width - 1, 0))
        shifted[0, frame, row] = before.astype(jnp.bfloat16)
        shifted[1, frame, row] = value.astype(jnp.bfloat16)
        shifted[2, frame, row] = after.astype(jnp.bfloat16)

    def activate(value):
        affine = (value.astype(jnp.float32) - average) * scale + shift[...]
        return affine / (1.0 + jnp.exp(-affine))

    for frame in range(history):
        put(frame, 0, cache_top[offset + frame].astype(jnp.float32))
        for row in range(rows):
            put(frame, row + 1, cache[frame, row].astype(jnp.float32))
        put(frame, rows + 1, cache_bottom[offset + frame].astype(jnp.float32))
    for frame in range(frames):
        put(history + frame, 0, activate(top[frame]) * inside[0])
        for row in range(rows):
            value = activate(x[frame, row])
            put(history + frame, row + 1, value)
            if keep and frame >= frames - history:
                refs[11 + slots][frame - (frames - history), row] = value.astype(jnp.bfloat16)
        put(history + frame, rows + 1, activate(bottom[frame]) * inside[1])
    order = blocks_in_order(weights.shape[2] // channels)
    products(shifted, weights, order[:slots], outs)


def conv(x, edges, cache, cache_edges, offset, moments, gain, shift, weights, entries, keep):
    frames, rows, width, channels = x.shape
    blocks = weights.shape[2] // channels
    cells = frames * rows * width
    half = (blocks + 1) // 2 if blocks == 4 else blocks
    sent = jax.ShapeDtypeStruct((cells, channels), jnp.bfloat16)
    held = jax.ShapeDtypeStruct((cells, channels), jnp.float32)
    outs = [
        jax.ShapeDtypeStruct((3, frames + 2, rows + 2, width, channels), jnp.bfloat16),
        *[sent] * half,
    ]
    if keep:
        outs.append(jax.ShapeDtypeStruct(cache.shape, jnp.bfloat16))
    args = (
        x, edges[0], edges[1], cache, cache_edges[0], cache_edges[1], moments, gain, shift, weights
    )
    work = 2 * cells * 9 * weights.shape[1] * channels
    body = functools.partial(conv_body, entries, offset, half, keep)
    shifted, *made = call(body, outs, args, flops=work * half, name="conv_head")
    kept = made.pop() if keep else None
    if half < blocks:

        def rest(shifted, weights, *outs):
            products(shifted, weights, blocks_in_order(blocks)[half:], outs)

        outs = [sent] * (blocks - half - 1) + [held]
        made += call(rest, outs, (shifted, weights), flops=work * (blocks - half), name="conv_tail")
    return made, kept


def reduce_terms(parts):
    count = lax.axis_size("chan")
    if count != 4:
        stacked = jnp.stack(parts)
        mine = lax.axis_index("chan")
        own = lax.dynamic_index_in_dim(stacked, mine, 0, keepdims=False).astype(jnp.float32)
        terms = []
        for step in range(1, count):
            block = lax.dynamic_index_in_dim(stacked, (mine + step) % count, 0, keepdims=False)
            pairs = [(i, (i + step) % count) for i in range(count)]
            terms.append(lax.ppermute(block, "chan", pairs))
        return own, terms
    far, near, last, own = parts
    early = lax.ppermute(far, "chan", [(0, 1), (3, 2), (1, 0), (2, 3)])
    beside = lax.ppermute(near, "chan", [(1, 2), (2, 1)])
    across = lax.ppermute(near, "chan", [(0, 2), (3, 1)])
    edge = lax.ppermute(last, "chan", [(0, 1), (3, 2)])
    mine = lax.axis_index("chan")
    inner = (mine == 1) | (mine == 2)
    joined = (last.astype(jnp.float32) + early.astype(jnp.float32)).astype(jnp.bfloat16)
    late = lax.ppermute(joined, "chan", [(1, 3), (2, 0)])
    own = own + jnp.where(inner, 0.0, early.astype(jnp.float32))
    return own, [beside, across, edge, late]


def over_rows(moments):
    count = lax.axis_size("rows")
    if count & (count - 1):
        return lax.psum(moments, "rows")
    step = 1
    while step < count:
        pairs = [(i, i ^ step) for i in range(count)]
        moments = moments + lax.ppermute(moments, "rows", pairs)
        step *= 2
    return moments


def neighbours(down, up):
    count = lax.axis_size("rows")
    forward = [(i, i + 1) for i in range(count - 1)]
    backward = [(i + 1, i) for i in range(count - 1)]
    return lax.ppermute(down, "rows", forward), lax.ppermute(up, "rows", backward)


def local(
    frames_in,
    cache_first,
    gain_first,
    shift_first,
    kernel_first,
    bias_first,
    cache_second,
    gain_second,
    shift_second,
    kernel_second,
    bias_second,
):
    inward, outward = (1, 2, 3, 0), (3, 0, 1, 2)
    x = frames_in.transpose(inward)
    first, second = cache_first.transpose(inward), cache_second.transpose(inward)
    frames, rows, width, channels = x.shape
    history = first.shape[0]
    entries = frames * rows * width * (CHANNELS // GROUPS) * lax.axis_size("rows")

    def line(vector):
        return vector.reshape(1, channels)

    def taps(kernel):
        return kernel.reshape(9, 3 * channels, kernel.shape[4])

    moments, down, up = entry(x, first, second)
    edges = neighbours(down, up)
    moments = over_rows(moments)
    parts, _ = conv(
        x, edges, first, edges, frames, moments, line(gain_first), line(shift_first),
        taps(kernel_first), entries, False,
    )
    own, terms = reduce_terms(parts)
    hidden, moments, down, up = middle(own, terms, line(bias_first), x.shape)
    inner = neighbours(down, up)
    moments = over_rows(moments)
    parts, kept = conv(
        hidden, inner, second, edges, frames + history, moments, line(gain_second),
        line(shift_second), taps(kernel_second), entries, True,
    )
    own, terms = reduce_terms(parts)
    decoded = close(own, terms, line(bias_second), x.shape)
    return decoded.transpose(outward), kept.transpose(outward)


def solution(mesh):
    split = P("chan", None, ("grp", "rows"), None)
    vector = P("chan")
    kernel = P(None, None, None, "chan", None)
    return jax.shard_map(
        local,
        mesh=mesh,
        in_specs=(
            split, split, vector, vector, kernel, vector, split, vector, vector, kernel, vector
        ),
        out_specs=(split, split),
        check_vma=False,
    )
```

time: 198 us -> 80 us (0.40)
  waiting for transfers between devices: 76.3 us -> 21.4 us
  local copies, waits for them, and re-layouts: 63.3 us -> 9.59 us
  starting transfers between devices: 5.7 us -> 35.9 us
  blocking collectives: 15.1 us -> 0 us
  between operations: 14.4 us -> 0.93 us
  matrix products: 12.6 us -> 0 us
  Pallas kernels: 0 us -> 10.6 us
  other arithmetic: 9.73 us -> 1.12 us
    reduce_scatter x2 -> x0, waiting for transfers between devices: 74.9 us -> none  [causal_conv(): lax.psum_scatter(contract(weights, columns), 'chan', scatter_dimension=0,...]
    slice x11 -> x0, local copies, waits for them, and re-layouts: 34.2 us -> none  [the longest x8 27.9 us: build_columns(): merged[:, time_tap:time_tap + frames].reshape(9 * channel_count, -1)]
    ppermute x4 -> x18, starting transfers between devices: 5.62 us -> 35.9 us  [the longest x2 12.4 us: reduce_terms(): across = lax.ppermute(near, 'chan', [(0, 2), (3, 1)])]
    ppermute x4 -> x18, waiting for transfers between devices: 1.37 us -> 21.4 us  [the longest x2 10.6 us: reduce_terms(): late = lax.ppermute(joined, 'chan', [(1, 3), (2, 0)])]
    psum x2 -> x0, blocking collectives: 15.1 us -> none  [norm_act(): lax.psum((jnp.sum(grouped, axis=1), jnp.sum(grouped * grouped, axis=1)),...]
    reshape x2 -> x0, local copies, waits for them, and re-layouts: 13.4 us -> none  [build_columns(): jnp.stack(shifted, 0)]
    another operation x4 -> x0, local copies, waits for them, and re-layouts: 12.8 us -> none  [build_columns(): jnp.stack(shifted, 0)]
    dot_general x6 -> x0, matrix products: 12.6 us -> none  [contract(): lax.dot_general(weights[time_tap], columns[time_tap], (((0,), (0,)), ((),...]
  transfers between devices with their start and end apart: 6 -> 18, of which waited for: 3 -> 8; matrix products, arithmetic and copies ran while one was open for 3% -> 1% of each run, Pallas kernels for 0% -> 5%
where the time goes in v1:
time: 80 us; the launch traced here: 79.5 us
  starting transfers between devices  35.9 us (45%)
  waiting for transfers between devices  21.4 us (27%)
  Pallas kernels  10.6 us (13%)
  local copies, waits for them, and re-layouts  9.59 us (12%)
  other arithmetic  1.12 us (1%)
  between operations  0.93 us (1%)
    ppermute x2, starting transfers between devices, reduce_terms(): across = lax.ppermute(near, 'chan', [(0, 2), (3, 1)])  12.4 us
    ppermute x2, waiting for transfers between devices, reduce_terms(): late = lax.ppermute(joined, 'chan', [(1, 3), (2, 0)])  10.6 us
    pallas_call x7, Pallas kernels, call(): pl.pallas_call(body, out_shape=outs, in_specs=[full()] * len(args), out_s...  10.6 us
    unnamed x40, local copies, waits for them, and re-layouts  9.59 us
    ppermute x4, waiting for transfers between devices, over_rows(): moments = moments + lax.ppermute(moments, 'rows', pairs)  7.03 us
    ppermute x4, starting transfers between devices, over_rows(): moments = moments + lax.ppermute(moments, 'rows', pairs)  6.78 us
    ppermute x2, starting transfers between devices, neighbours(): lax.ppermute(down, 'rows', forward)  5.44 us
    ppermute x2, waiting for transfers between devices, reduce_terms(): edge = lax.ppermute(last, 'chan', [(0, 1), (3, 2)])  3.7 us
  transfers between devices with their start and end apart: 18, of which 8 were waited for; matrix products, arithmetic and copies ran while one was open for 1% of the time, Pallas kernels for 5%

profile of v1, /device:TPU:0, one launch (start us, length us, event | category | flops | bytes accessed | tf_op | source)
XLA Modules:
  0.0 79.5 jit_solution(8029749458679568393)
XLA Ops:
  3.5 2.4 %collective-permute-start = (bf16[8,96,128]{2,1,0:T(8,128)(2,1)S(1)}, bf16[8,96,128]{2,1,0:T(8,128)(2,1)S(1)}, u32[]{:S(2)}, u32[]{:S(2)}) collective-permute-start(bf16[8,96,128]{2,1,0:T(8,128)(2,1)S(1)} %get-tuple-element.20), channel_id=1, source_target_pairs={{0,4},{4,8},{8,12},{1,5},{5,9},{9,13},{2,6},{6,10},{10,14},{3,7},{... | collective-permute-start | bytes 589832 | tf_op jit(solution)/shard_map/ppermute | solution.py:264
  5.9 1.3 %collective-permute-start.1 = (bf16[8,96,128]{2,1,0:T(8,128)(2,1)S(1)}, bf16[8,96,128]{2,1,0:T(8,128)(2,1)S(1)}, u32[]{:S(2)}, u32[]{:S(2)}) collective-permute-start(bf16[8,96,128]{2,1,0:T(8,128)(2,1)S(1)} %get-tuple-element.21), channel_id=1, source_target_pairs={{4,0},{8,4},{12,8},{5,1},{9,5},{13,9},{6,2},{10,6},{14,10},{7,3},{... | collective-permute-start | bytes 589832 | tf_op jit(solution)/shard_map/ppermute | solution.py:264
  7.2 3.3 %collective-permute-start.2 = (f32[8,128]{1,0:T(8,128)S(1)}, f32[8,128]{1,0:T(8,128)S(1)}, u32[]{:S(2)}, u32[]{:S(2)}) collective-permute-start(f32[8,128]{1,0:T(8,128)S(1)} %get-tuple-element.22), channel_id=1, source_target_pairs={{0,4},{4,0},{8,12},{12,8},{1,5},{5,1},{9,13},{13,9},{2,6},{6,2},{1... | collective-permute-start | bytes 12296 | tf_op jit(solution)/shard_map/ppermute | solution.py:255
  11.3 1.9 %collective-permute-start.3 = (f32[8,128]{1,0:T(8,128)S(1)}, f32[8,128]{1,0:T(8,128)S(1)}, u32[]{:S(2)}, u32[]{:S(2)}) collective-permute-start(f32[8,128]{1,0:T(8,128)S(1)} %add.24), channel_id=1, source_target_pairs={{0,8},{4,12},{8,0},{12,4},{1,9},{5,13},{9,1},{13,5},{2,10},{6,14},... | collective-permute-start | bytes 12296 | tf_op jit(solution)/shard_map/ppermute | solution.py:255
  13.3 2.5 %collective-permute-done.3 = f32[8,128]{1,0:T(8,128)S(1)} collective-permute-done((f32[8,128]{1,0:T(8,128)S(1)}, f32[8,128]{1,0:T(8,128)S(1)}, u32[]{:S(2)}, u32[]{:S(2)}) %collective-permute-start.3) | collective-permute-done | bytes 4128 | tf_op jit(solution)/shard_map/ppermute | solution.py:255
  15.8 2.1 %copy-done = bf16[3,3,3,128,512]{4,3,2,1,0:T(8,128)(2,1)S(1)} copy-done((bf16[3,3,3,128,512]{4,3,2,1,0:T(8,128)(2,1)S(1)}, bf16[3,3,3,128,512]{4,3,2,1,0:T(8,128)(2,1)}, u32[]{:S(2)}) %copy-start) | copy-done | bytes 3538968
  19.2 3.0 %conv_head.2 = (bf16[3,6,4,96,128]{4,3,2,1,0:T(8,128)(2,1)S(1)}, bf16[768,128]{1,0:T(8,128)(2,1)}, bf16[768,128]{1,0:T(8,128)(2,1)S(1)}) custom-call(bf16[4,2,96,128]{3,2,1,0:T(8,128)(2,1)S(1)} %bitcast.18, bf16[8,96,128]{2,1,0:T(8,128)(2,1)S(1)} %collective-permute-done.refs_1_.refs_4_, bf16[8,96,128]{2,1,0:T(8,128)(2,1)S(1)} %collective-permute-done.1.refs_2_.refs_5_, ...), custom_call_target="tpu_custom_call" | custom-call | flops 1358954496 | bytes 6788096 | tf_op jit(solution)/shard_map/conv_head/pallas_call | solution.py:27
  24.2 1.6 %collective-permute-start.4 = (bf16[768,128]{1,0:T(8,128)(2,1)}, bf16[768,128]{1,0:T(8,128)(2,1)}, u32[]{:S(2)}, u32[]{:S(2)}) collective-permute-start(bf16[768,128]{1,0:T(8,128)(2,1)} %get-tuple-element.25), channel_id=1, source_target_pairs={{0,1},{3,2},{1,0},{2,3},{4,5},{7,6},{5,4},{6,7},{8,9},{11,10},{9,8... | collective-permute-start | bytes 589832 | tf_op jit(solution)/shard_map/ppermute | solution.py:236
  26.4 5.7 %collective-permute-start.6 = (bf16[768,128]{1,0:T(8,128)(2,1)}, bf16[768,128]{1,0:T(8,128)(2,1)S(1)}, u32[]{:S(2)}, u32[]{:S(2)}) collective-permute-start(bf16[768,128]{1,0:T(8,128)(2,1)} %copy-done.15), channel_id=1, source_target_pairs={{0,2},{3,1},{4,6},{7,5},{8,10},{11,9},{12,14},{15,13},{16,18},{19,... | collective-permute-start | bytes 589832 | tf_op jit(solution)/shard_map/ppermute | solution.py:238
  32.2 1.5 %copy-done.4 = bf16[3,6,4,96,128]{4,3,2,1,0:T(8,128)(2,1)S(1)} copy-done((bf16[3,6,4,96,128]{4,3,2,1,0:T(8,128)(2,1)S(1)}, bf16[3,6,4,96,128]{4,3,2,1,0:T(8,128)(2,1)}, u32[]{:S(2)}) %copy-start.4) | copy-done | bytes 1769496
  33.7 2.0 %conv_tail.2 = (bf16[768,128]{1,0:T(8,128)(2,1)S(1)}, f32[768,128]{1,0:T(8,128)S(1)}) custom-call(bf16[3,6,4,96,128]{4,3,2,1,0:T(8,128)(2,1)S(1)} %copy-done.4, bf16[9,384,512]{2,1,0:T(8,128)(2,1)S(1)} %bitcast.14), custom_call_target="tpu_custom_call" | custom-call | flops 1358954496 | bytes 5898240 | tf_op jit(solution)/shard_map/conv_tail/pallas_call | solution.py:27
  35.7 1.8 %collective-permute-start.7 = (bf16[768,128]{1,0:T(8,128)(2,1)S(1)}, bf16[768,128]{1,0:T(8,128)(2,1)S(1)}, u32[]{:S(2)}, u32[]{:S(2)}) collective-permute-start(bf16[768,128]{1,0:T(8,128)(2,1)S(1)} %get-tuple-element.27), channel_id=1, source_target_pairs={{0,1},{3,2},{4,5},{7,6},{8,9},{11,10},{12,13},{15,14},{16,17},{19,... | collective-permute-start | bytes 589832 | tf_op jit(solution)/shard_map/ppermute | solution.py:239
  38.6 1.3 %collective-permute-start.8 = (bf16[768,128]{1,0:T(8,128)(2,1)S(1)}, bf16[768,128]{1,0:T(8,128)(2,1)S(1)}, u32[]{:S(2)}, u32[]{:S(2)}) collective-permute-start(bf16[768,128]{1,0:T(8,128)(2,1)S(1)} %get-tuple-element.40), channel_id=1, source_target_pairs={{1,3},{2,0},{5,7},{6,4},{9,11},{10,8},{13,15},{14,12},{17,19},{18,... | collective-permute-start | bytes 589832 | tf_op jit(solution)/shard_map/ppermute | solution.py:243
  41.0 6.1 %collective-permute-done.8.refs_4_ = bf16[768,128]{1,0:T(8,128)(2,1)S(1)} collective-permute-done((bf16[768,128]{1,0:T(8,128)(2,1)S(1)}, bf16[768,128]{1,0:T(8,128)(2,1)S(1)}, u32[]{:S(2)}, u32[]{:S(2)}) %collective-permute-start.8) | collective-permute-done | bytes 196640 | tf_op jit(solution)/shard_map/ppermute | solution.py:243
  47.3 1.3 %collective-permute-start.10 = (bf16[4,96,128]{2,1,0:T(8,128)(2,1)S(1)}, bf16[4,96,128]{2,1,0:T(8,128)(2,1)S(1)}, u32[]{:S(2)}, u32[]{:S(2)}) collective-permute-start(bf16[4,96,128]{2,1,0:T(8,128)(2,1)S(1)} %get-tuple-element.30), channel_id=1, source_target_pairs={{4,0},{8,4},{12,8},{5,1},{9,5},{13,9},{6,2},{10,6},{14,10},{7,3},{... | collective-permute-start | bytes 294920 | tf_op jit(solution)/shard_map/ppermute | solution.py:264
  48.6 3.0 %collective-permute-start.9 = (bf16[4,96,128]{2,1,0:T(8,128)(2,1)S(1)}, bf16[4,96,128]{2,1,0:T(8,128)(2,1)S(1)}, u32[]{:S(2)}, u32[]{:S(2)}) collective-permute-start(bf16[4,96,128]{2,1,0:T(8,128)(2,1)S(1)} %get-tuple-element.29), channel_id=1, source_target_pairs={{0,4},{4,8},{8,12},{1,5},{5,9},{9,13},{2,6},{6,10},{10,14},{3,7},{... | collective-permute-start | bytes 294920 | tf_op jit(solution)/shard_map/ppermute | solution.py:264
  54.0 2.9 %collective-permute-done.12 = f32[8,128]{1,0:T(8,128)S(1)} collective-permute-done((f32[8,128]{1,0:T(8,128)S(1)}, f32[8,128]{1,0:T(8,128)S(1)}, u32[]{:S(2)}, u32[]{:S(2)}) %collective-permute-start.12) | collective-permute-done | bytes 4128 | tf_op jit(solution)/shard_map/ppermute | solution.py:255
  57.0 2.4 %conv_head.3 = (bf16[3,6,4,96,128]{4,3,2,1,0:T(8,128)(2,1)S(1)}, bf16[768,128]{1,0:T(8,128)(2,1)S(1)}, bf16[768,128]{1,0:T(8,128)(2,1)S(1)}, bf16[2,2,96,128]{3,2,1,0:T(8,128)(2,1)}) custom-call(bf16[4,2,96,128]{3,2,1,0:T(8,128)(2,1)S(1)} %get-tuple-element.28.refs_0_, bf16[4,96,128]{2,1,0:T(8,128)(2,1)S(1)} %collective-permute-done.9.refs_1_, ...), custom_call_target="tpu_custom_call" | custom-call | flops 1358954496 | bytes 6689792 | tf_op jit(solution)/shard_map/conv_head/pallas_call | solution.py:27
  60.1 6.6 %collective-permute-start.15 = (bf16[768,128]{1,0:T(8,128)(2,1)S(1)}, bf16[768,128]{1,0:T(8,128)(2,1)S(1)}, u32[]{:S(2)}, u32[]{:S(2)}) collective-permute-start(bf16[768,128]{1,0:T(8,128)(2,1)S(1)} %get-tuple-element.35), channel_id=1, source_target_pairs={{0,2},{3,1},{4,6},{7,5},{8,10},{11,9},{12,14},{15,13},{16,18},{19,... | collective-permute-start | bytes 589832 | tf_op jit(solution)/shard_map/ppermute | solution.py:238
  66.7 2.0 %conv_tail.3 = (bf16[768,128]{1,0:T(8,128)(2,1)S(1)}, f32[768,128]{1,0:T(8,128)S(1)}) custom-call(bf16[3,6,4,96,128]{4,3,2,1,0:T(8,128)(2,1)S(1)} %get-tuple-element.32.shifted, bf16[9,384,512]{2,1,0:T(8,128)(2,1)S(1)} %bitcast.16), custom_call_target="tpu_custom_call" | custom-call | flops 1358954496 | bytes 5898240 | tf_op jit(solution)/shard_map/conv_tail/pallas_call | solution.py:27
  68.8 1.3 %collective-permute-start.16 = (bf16[768,128]{1,0:T(8,128)(2,1)S(1)}, bf16[768,128]{1,0:T(8,128)(2,1)S(1)}, u32[]{:S(2)}, u32[]{:S(2)}) collective-permute-start(bf16[768,128]{1,0:T(8,128)(2,1)S(1)} %get-tuple-element.36), channel_id=1, source_target_pairs={{0,1},{3,2},{4,5},{7,6},{8,9},{11,10},{12,13},{15,14},{16,17},{19,... | collective-permute-start | bytes 589832 | tf_op jit(solution)/shard_map/ppermute | solution.py:239
  70.2 1.3 %collective-permute-start.17 = (bf16[768,128]{1,0:T(8,128)(2,1)S(1)}, bf16[768,128]{1,0:T(8,128)(2,1)S(1)}, u32[]{:S(2)}, u32[]{:S(2)}) collective-permute-start(bf16[768,128]{1,0:T(8,128)(2,1)S(1)} %get-tuple-element.38), channel_id=1, source_target_pairs={{1,3},{2,0},{5,7},{6,4},{9,11},{10,8},{13,15},{14,12},{17,19},{18,... | collective-permute-start | bytes 589832 | tf_op jit(solution)/shard_map/ppermute | solution.py:243
  71.5 2.6 %collective-permute-done.16.refs_3_ = bf16[768,128]{1,0:T(8,128)(2,1)S(1)} collective-permute-done((bf16[768,128]{1,0:T(8,128)(2,1)S(1)}, bf16[768,128]{1,0:T(8,128)(2,1)S(1)}, u32[]{:S(2)}, u32[]{:S(2)}) %collective-permute-start.16) | collective-permute-done | bytes 196640 | tf_op jit(solution)/shard_map/ppermute | solution.py:239
  74.1 4.5 %collective-permute-done.17.refs_4_ = bf16[768,128]{1,0:T(8,128)(2,1)S(1)} collective-permute-done((bf16[768,128]{1,0:T(8,128)(2,1)S(1)}, bf16[768,128]{1,0:T(8,128)(2,1)S(1)}, u32[]{:S(2)}, u32[]{:S(2)}) %collective-permute-start.17) | collective-permute-done | bytes 196640 | tf_op jit(solution)/shard_map/ppermute | solution.py:243
  (65 shorter events, 14.0 us)
Async XLA Ops:
  3.5 12.3 %collective-permute-start = (bf16[8,96,128]{2,1,0:T(8,128)(2,1)S(1)}, bf16[8,96,128]{2,1,0:T(8,128)(2,1)S(1)}, u32[]{:S(2)}, u32[]{:S(2)}) collective-permute-start(bf16[8,96,128]{2,1,0:T(8,128)(2,1)S(1)} %get-tuple-element.20), channel_id=1, source_target_pairs={{0,4},{4,8},{8,12},{1,5},{5,9},{9,13},{2,6},{6,10},{10,14},{3,7},{... | collective-permute-start | bytes 589832 | tf_op jit(solution)/shard_map/ppermute | solution.py:264
  5.9 9.9 %collective-permute-start.1 = (bf16[8,96,128]{2,1,0:T(8,128)(2,1)S(1)}, bf16[8,96,128]{2,1,0:T(8,128)(2,1)S(1)}, u32[]{:S(2)}, u32[]{:S(2)}) collective-permute-start(bf16[8,96,128]{2,1,0:T(8,128)(2,1)S(1)} %get-tuple-element.21), channel_id=1, source_target_pairs={{4,0},{8,4},{12,8},{5,1},{9,5},{13,9},{6,2},{10,6},{14,10},{7,3},{... | collective-permute-start | bytes 589832 | tf_op jit(solution)/shard_map/ppermute | solution.py:264
  7.2 4.2 %collective-permute-start.2 = (f32[8,128]{1,0:T(8,128)S(1)}, f32[8,128]{1,0:T(8,128)S(1)}, u32[]{:S(2)}, u32[]{:S(2)}) collective-permute-start(f32[8,128]{1,0:T(8,128)S(1)} %get-tuple-element.22), channel_id=1, source_target_pairs={{0,4},{4,0},{8,12},{12,8},{1,5},{5,1},{9,13},{13,9},{2,6},{6,2},{1... | collective-permute-start | bytes 12296 | tf_op jit(solution)/shard_map/ppermute | solution.py:255
  11.3 4.4 %collective-permute-start.3 = (f32[8,128]{1,0:T(8,128)S(1)}, f32[8,128]{1,0:T(8,128)S(1)}, u32[]{:S(2)}, u32[]{:S(2)}) collective-permute-start(f32[8,128]{1,0:T(8,128)S(1)} %add.24), channel_id=1, source_target_pairs={{0,8},{4,12},{8,0},{12,4},{1,9},{5,13},{9,1},{13,5},{2,10},{6,14},... | collective-permute-start | bytes 12296 | tf_op jit(solution)/shard_map/ppermute | solution.py:255
  24.2 13.4 %collective-permute-start.4 = (bf16[768,128]{1,0:T(8,128)(2,1)}, bf16[768,128]{1,0:T(8,128)(2,1)}, u32[]{:S(2)}, u32[]{:S(2)}) collective-permute-start(bf16[768,128]{1,0:T(8,128)(2,1)} %get-tuple-element.25), channel_id=1, source_target_pairs={{0,1},{3,2},{1,0},{2,3},{4,5},{7,6},{5,4},{6,7},{8,9},{11,10},{9,8... | collective-permute-start | bytes 589832 | tf_op jit(solution)/shard_map/ppermute | solution.py:236
  25.8 15.2 %collective-permute-start.5 = (bf16[768,128]{1,0:T(8,128)(2,1)}, bf16[768,128]{1,0:T(8,128)(2,1)S(1)}, u32[]{:S(2)}, u32[]{:S(2)}) collective-permute-start(bf16[768,128]{1,0:T(8,128)(2,1)} %copy-done.15), channel_id=1, source_target_pairs={{1,2},{2,1},{5,6},{6,5},{9,10},{10,9},{13,14},{14,13},{17,18},{18,... | collective-permute-start | bytes 589832 | tf_op jit(solution)/shard_map/ppermute | solution.py:237
  26.4 14.6 %collective-permute-start.6 = (bf16[768,128]{1,0:T(8,128)(2,1)}, bf16[768,128]{1,0:T(8,128)(2,1)S(1)}, u32[]{:S(2)}, u32[]{:S(2)}) collective-permute-start(bf16[768,128]{1,0:T(8,128)(2,1)} %copy-done.15), channel_id=1, source_target_pairs={{0,2},{3,1},{4,6},{7,5},{8,10},{11,9},{12,14},{15,13},{16,18},{19,... | collective-permute-start | bytes 589832 | tf_op jit(solution)/shard_map/ppermute | solution.py:238
  33.7 23.2 %copy-start.2 = (bf16[3,3,3,128,512]{4,3,2,1,0:T(8,128)(2,1)S(1)}, bf16[3,3,3,128,512]{4,3,2,1,0:T(8,128)(2,1)}, u32[]{:S(2)}) copy-start(bf16[3,3,3,128,512]{4,3,2,1,0:T(8,128)(2,1)} %param.20) | copy-start | bytes 10616836
  33.7 23.3 %copy-start.8 = (bf16[128,2,2,96]{0,3,2,1:T(8,128)(2,1)S(1)}, bf16[128,2,2,96]{0,3,2,1:T(8,128)(2,1)}, u32[]{:S(2)}) copy-start(bf16[128,2,2,96]{0,3,2,1:T(8,128)(2,1)} %param.17) | copy-start | bytes 294916
  33.7 23.3 %copy-start.12 = (bf16[8,96,128]{2,1,0:T(8,128)(2,1)S(1)}, bf16[8,96,128]{2,1,0:T(8,128)(2,1)}, u32[]{:S(2)}) copy-start(bf16[8,96,128]{2,1,0:T(8,128)(2,1)} %copy-done.11) | copy-start | bytes 589828
  33.7 23.3 %copy-start.14 = (bf16[8,96,128]{2,1,0:T(8,128)(2,1)S(1)}, bf16[8,96,128]{2,1,0:T(8,128)(2,1)}, u32[]{:S(2)}) copy-start(bf16[8,96,128]{2,1,0:T(8,128)(2,1)} %copy-done.13) | copy-start | bytes 589828
  33.7 23.3 %copy-start.18 = (f32[128]{0:T(128)S(1)}, f32[128]{0:T(128)}, u32[]{:S(2)}) copy-start(f32[128]{0:T(128)} %param.18) | copy-start | bytes 1540
  33.7 23.3 %copy-start.19 = (f32[128]{0:T(128)S(1)}, f32[128]{0:T(128)}, u32[]{:S(2)}) copy-start(f32[128]{0:T(128)} %param.19) | copy-start | bytes 1540
  35.7 5.3 %collective-permute-start.7 = (bf16[768,128]{1,0:T(8,128)(2,1)S(1)}, bf16[768,128]{1,0:T(8,128)(2,1)S(1)}, u32[]{:S(2)}, u32[]{:S(2)}) collective-permute-start(bf16[768,128]{1,0:T(8,128)(2,1)S(1)} %get-tuple-element.27), channel_id=1, source_target_pairs={{0,1},{3,2},{4,5},{7,6},{8,9},{11,10},{12,13},{15,14},{16,17},{19,... | collective-permute-start | bytes 589832 | tf_op jit(solution)/shard_map/ppermute | solution.py:239
  38.6 8.5 %collective-permute-start.8 = (bf16[768,128]{1,0:T(8,128)(2,1)S(1)}, bf16[768,128]{1,0:T(8,128)(2,1)S(1)}, u32[]{:S(2)}, u32[]{:S(2)}) collective-permute-start(bf16[768,128]{1,0:T(8,128)(2,1)S(1)} %get-tuple-element.40), channel_id=1, source_target_pairs={{1,3},{2,0},{5,7},{6,4},{9,11},{10,8},{13,15},{14,12},{17,19},{18,... | collective-permute-start | bytes 589832 | tf_op jit(solution)/shard_map/ppermute | solution.py:243
  47.3 9.6 %collective-permute-start.10 = (bf16[4,96,128]{2,1,0:T(8,128)(2,1)S(1)}, bf16[4,96,128]{2,1,0:T(8,128)(2,1)S(1)}, u32[]{:S(2)}, u32[]{:S(2)}) collective-permute-start(bf16[4,96,128]{2,1,0:T(8,128)(2,1)S(1)} %get-tuple-element.30), channel_id=1, source_target_pairs={{4,0},{8,4},{12,8},{5,1},{9,5},{13,9},{6,2},{10,6},{14,10},{7,3},{... | collective-permute-start | bytes 294920 | tf_op jit(solution)/shard_map/ppermute | solution.py:264
  48.6 8.3 %collective-permute-start.9 = (bf16[4,96,128]{2,1,0:T(8,128)(2,1)S(1)}, bf16[4,96,128]{2,1,0:T(8,128)(2,1)S(1)}, u32[]{:S(2)}, u32[]{:S(2)}) collective-permute-start(bf16[4,96,128]{2,1,0:T(8,128)(2,1)S(1)} %get-tuple-element.29), channel_id=1, source_target_pairs={{0,4},{4,8},{8,12},{1,5},{5,9},{9,13},{2,6},{6,10},{10,14},{3,7},{... | collective-permute-start | bytes 294920 | tf_op jit(solution)/shard_map/ppermute | solution.py:264
  51.7 1.6 %collective-permute-start.11 = (f32[8,128]{1,0:T(8,128)S(1)}, f32[8,128]{1,0:T(8,128)S(1)}, u32[]{:S(2)}, u32[]{:S(2)}) collective-permute-start(f32[8,128]{1,0:T(8,128)S(1)} %get-tuple-element.31), channel_id=1, source_target_pairs={{0,4},{4,0},{8,12},{12,8},{1,5},{5,1},{9,13},{13,9},{2,6},{6,2},{1... | collective-permute-start | bytes 12296 | tf_op jit(solution)/shard_map/ppermute | solution.py:255
  53.3 3.6 %collective-permute-start.12 = (f32[8,128]{1,0:T(8,128)S(1)}, f32[8,128]{1,0:T(8,128)S(1)}, u32[]{:S(2)}, u32[]{:S(2)}) collective-permute-start(f32[8,128]{1,0:T(8,128)S(1)} %add.28), channel_id=1, source_target_pairs={{0,8},{4,12},{8,0},{12,4},{1,9},{5,13},{9,1},{13,5},{2,10},{6,14},... | collective-permute-start | bytes 12296 | tf_op jit(solution)/shard_map/ppermute | solution.py:255
  59.4 10.7 %collective-permute-start.13 = (bf16[768,128]{1,0:T(8,128)(2,1)S(1)}, bf16[768,128]{1,0:T(8,128)(2,1)S(1)}, u32[]{:S(2)}, u32[]{:S(2)}) collective-permute-start(bf16[768,128]{1,0:T(8,128)(2,1)S(1)} %get-tuple-element.34), channel_id=1, source_target_pairs={{0,1},{3,2},{1,0},{2,3},{4,5},{7,6},{5,4},{6,7},{8,9},{11,10},{9,8... | collective-permute-start | bytes 589832 | tf_op jit(solution)/shard_map/ppermute | solution.py:236
  59.4 14.7 %collective-permute-start.14 = (bf16[768,128]{1,0:T(8,128)(2,1)S(1)}, bf16[768,128]{1,0:T(8,128)(2,1)S(1)}, u32[]{:S(2)}, u32[]{:S(2)}) collective-permute-start(bf16[768,128]{1,0:T(8,128)(2,1)S(1)} %get-tuple-element.35), channel_id=1, source_target_pairs={{1,2},{2,1},{5,6},{6,5},{9,10},{10,9},{13,14},{14,13},{17,18},{18,... | collective-permute-start | bytes 589832 | tf_op jit(solution)/shard_map/ppermute | solution.py:237
  60.1 14.0 %collective-permute-start.15 = (bf16[768,128]{1,0:T(8,128)(2,1)S(1)}, bf16[768,128]{1,0:T(8,128)(2,1)S(1)}, u32[]{:S(2)}, u32[]{:S(2)}) collective-permute-start(bf16[768,128]{1,0:T(8,128)(2,1)S(1)} %get-tuple-element.35), channel_id=1, source_target_pairs={{0,2},{3,1},{4,6},{7,5},{8,10},{11,9},{12,14},{15,13},{16,18},{19,... | collective-permute-start | bytes 589832 | tf_op jit(solution)/shard_map/ppermute | solution.py:238
  68.8 5.3 %collective-permute-start.16 = (bf16[768,128]{1,0:T(8,128)(2,1)S(1)}, bf16[768,128]{1,0:T(8,128)(2,1)S(1)}, u32[]{:S(2)}, u32[]{:S(2)}) collective-permute-start(bf16[768,128]{1,0:T(8,128)(2,1)S(1)} %get-tuple-element.36), channel_id=1, source_target_pairs={{0,1},{3,2},{4,5},{7,6},{8,9},{11,10},{12,13},{15,14},{16,17},{19,... | collective-permute-start | bytes 589832 | tf_op jit(solution)/shard_map/ppermute | solution.py:239
  70.2 8.5 %collective-permute-start.17 = (bf16[768,128]{1,0:T(8,128)(2,1)S(1)}, bf16[768,128]{1,0:T(8,128)(2,1)S(1)}, u32[]{:S(2)}, u32[]{:S(2)}) collective-permute-start(bf16[768,128]{1,0:T(8,128)(2,1)S(1)} %get-tuple-element.38), channel_id=1, source_target_pairs={{1,3},{2,0},{5,7},{6,4},{9,11},{10,8},{13,15},{14,12},{17,19},{18,... | collective-permute-start | bytes 589832 | tf_op jit(solution)/shard_map/ppermute | solution.py:243
  (14 other events, 79.7 us)

commit v2 on v0

v2 whole, which is shorter than its diff:
```python
import functools

import jax
import jax.numpy as jnp
from jax import lax
from jax.experimental import pallas as pl
from jax.experimental.pallas import tpu as pltpu
from jax.sharding import PartitionSpec as P


CHANNELS = 512
GROUPS = 32
EPS = 1e-06

VMEM_LIMIT = 16 * 1024 * 1024
PACKED = 16


def on_chip():
    return pl.BlockSpec(memory_space=pltpu.VMEM)


def in_place():
    return pl.BlockSpec(memory_space=pltpu.HBM)


def call(body, outs, args, flops=0, specs=None, scratch=()):
    moved = sum(a.size * a.dtype.itemsize for a in (*args, *outs))
    return pl.pallas_call(
        body,
        out_shape=outs,
        in_specs=specs or [on_chip()] * len(args),
        out_specs=[on_chip()] * len(outs),
        scratch_shapes=scratch,
        compiler_params=pltpu.CompilerParams(vmem_limit_bytes=VMEM_LIMIT),
        cost_estimate=pl.CostEstimate(flops=flops, bytes_accessed=moved, transcendentals=0),
    )(*args)


def moments_of(values):
    total = jnp.sum(values, axis=0, keepdims=True)
    squares = jnp.sum(values * values, axis=0, keepdims=True)
    return jnp.concatenate([total, squares], axis=0)


def store_moments(tile, messages, moments):
    channels = moments.shape[1]
    tile[...] = jnp.concatenate([moments, jnp.zeros((6, channels), jnp.float32)], axis=0)
    terms, rest = [], moments
    for _ in range(3):
        term = rest.astype(jnp.bfloat16).astype(jnp.float32)
        terms.append(term)
        rest = rest - term
    terms.append(jnp.zeros((PACKED - 6, channels), jnp.float32))
    packed = jnp.concatenate(terms, axis=0).astype(jnp.bfloat16)
    for message in messages:
        message[message.shape[0] - PACKED :] = packed


def packed_moments(message):
    rows = message[message.shape[0] - PACKED :].astype(jnp.float32)
    return (rows[0:2] + rows[2:4]) + rows[4:6]


def store_edges(sources, pair, other):
    even = lax.axis_index("rows") % 2 == 0
    start = 0
    for source in sources:
        frames, rows, width, _ = source.shape
        for frame in range(frames):
            place = pl.ds(start, width)
            pair[place] = source[frame, jnp.where(even, rows - 1, 0)]
            other[place] = source[frame, jnp.where(even, 0, rows - 1)]
            start += width


def message_shapes(frames, width, channels, extra):
    return [jax.ShapeDtypeStruct((frames * width + extra, channels), jnp.bfloat16)] * 2


def entry_body(count, *refs):
    sources, held = refs[:count], refs[count : count + 3]
    table, tile, pair, other, old_pair, old_other, sems = refs[count + 3 :]
    copies = []
    for place, source in enumerate(sources):
        target = held[place] if place < 3 else table.at[pl.ds(place - 3, 1)]
        copies.append(pltpu.make_async_copy(source, target, sems.at[place]))
        copies[-1].start()
    copies[0].wait()
    x = held[0]
    moments = moments_of(x[...].astype(jnp.float32).reshape(-1, x.shape[3]))
    store_moments(tile, (pair, other), moments)
    store_edges((x,), pair, other)
    for copy in copies[1:]:
        copy.wait()
    store_edges(held[1:], old_pair, old_other)


def entry(x, first, second, vectors):
    frames, _, width, channels = x.shape
    sources = [pltpu.with_memory_space_constraint(a, pltpu.HBM) for a in (x, first, second, *vectors)]
    outs = [
        *[jax.ShapeDtypeStruct(a.shape, a.dtype) for a in (x, first, second)],
        jax.ShapeDtypeStruct((8, channels), jnp.float32),
        jax.ShapeDtypeStruct((8, channels), jnp.float32),
        *message_shapes(frames, width, channels, PACKED),
        *message_shapes(first.shape[0] + second.shape[0], width, channels, 0),
    ]
    body = functools.partial(entry_body, len(sources))
    return call(
        body, outs, sources, specs=[in_place()] * len(sources),
        scratch=[pltpu.SemaphoreType.DMA((len(sources),))],
    )


def fetch_body(source, target, sems):
    copies = [
        pltpu.make_async_copy(source.at[tap], target.at[tap], sems.at[tap])
        for tap in range(source.shape[0])
    ]
    for copy in copies:
        copy.start()
    for copy in copies:
        copy.wait()


def fetch(weights):
    weights = pltpu.with_memory_space_constraint(weights, pltpu.HBM)
    outs = [jax.ShapeDtypeStruct(weights.shape, weights.dtype)]
    return call(
        fetch_body, outs, (weights,), specs=[in_place()],
        scratch=[pltpu.SemaphoreType.DMA((weights.shape[0],))],
    )[0]


def total_of(own, terms, bias):
    value = own[...]
    for group in terms:
        pieces = [piece[...].astype(jnp.float32) for piece in group]
        value = value + (pieces[0] if len(pieces) == 1 else jnp.concatenate(pieces, axis=0))
    return (value + bias).astype(jnp.bfloat16)


def regroup(refs, counts):
    groups, start = [], 0
    for count in counts:
        groups.append(refs[start : start + count])
        start += count
    return groups, refs[start:]


def middle_body(row, counts, own, *refs):
    terms, (table, hidden, tile, pair, other) = regroup(refs, counts)
    rounded = total_of(own, terms, table[row : row + 1])
    store_moments(tile, (pair, other), moments_of(rounded.astype(jnp.float32)))
    hidden[...] = rounded.reshape(hidden.shape)
    store_edges((hidden,), pair, other)


def middle(own, terms, table, row, shape):
    frames, _, width, channels = shape
    outs = [
        jax.ShapeDtypeStruct(shape, jnp.bfloat16),
        jax.ShapeDtypeStruct((8, channels), jnp.float32),
        *message_shapes(frames, width, channels, PACKED),
    ]
    body = functools.partial(middle_body, row, [len(group) for group in terms])
    args = (own, *[piece for group in terms for piece in group], table)
    return call(body, outs, args)


def close_body(row, counts, own, *refs):
    terms, (table, out) = regroup(refs, counts)
    out[...] = total_of(own, terms, table[row : row + 1]).reshape(out.shape)


def close(own, terms, table, row, shape):
    outs = [jax.ShapeDtypeStruct(shape, jnp.bfloat16)]
    body = functools.partial(close_body, row, [len(group) for group in terms])
    args = (own, *[piece for group in terms for piece in group], table)
    return call(body, outs, args)[0]


def products(parts, weights, first, count, blocks, outs):
    _, _, rows, width, channels = parts[0].shape
    rows -= 2
    frames = [(part, frame) for part in parts for frame in range(part.shape[1])]
    total = None
    for time_tap in range(3):
        for row_tap in range(3):
            window = [
                jnp.concatenate(
                    [
                        part[col_tap, frame, row_tap : row_tap + rows].reshape(rows * width, channels)
                        for part, frame in frames[first + time_tap : first + time_tap + count]
                    ],
                    axis=0,
                )
                for col_tap in range(3)
            ]
            left = jnp.concatenate(window, axis=1)
            right = []
            for block in blocks:
                start = block * channels
                if not isinstance(block, int):
                    start = pl.multiple_of(start, channels)
                right.append(weights[3 * time_tap + row_tap, :, pl.ds(start, channels)])
            right = jnp.concatenate(right, axis=1)
            product = jnp.dot(left, right, preferred_element_type=jnp.float32)
            total = product if total is None else total + product
    for place, out in enumerate(outs):
        out[...] = total[:, place * channels : (place + 1) * channels].astype(out.dtype)


def leading(weights, channels):
    count = weights.shape[2] // channels
    if count != 4:
        return list(range(count))
    mine = lax.axis_index("chan")
    return [mine ^ 3, mine ^ 2]


def put(shifted, frame, row, value):
    width, channels = value.shape
    column = lax.broadcasted_iota(jnp.int32, (width, channels), 0)
    before = jnp.where(column == 0, 0.0, pltpu.roll(value, 1, 0))
    after = jnp.where(column == width - 1, 0.0, pltpu.roll(value, width - 1, 0))
    shifted[0, frame, row] = before.astype(jnp.bfloat16)
    shifted[1, frame, row] = value.astype(jnp.bfloat16)
    shifted[2, frame, row] = after.astype(jnp.bfloat16)


def halo(pair, other, frame, width):
    place = lax.axis_index("rows")
    even = place % 2 == 0
    start = pl.ds(frame * width, width)
    low, high = pair[start].astype(jnp.float32), other[start].astype(jnp.float32)
    above = jnp.where(place > 0, 1.0, 0.0)
    below = jnp.where(place < lax.axis_size("rows") - 1, 1.0, 0.0)
    return (jnp.where(even, high, low), above), (jnp.where(even, low, high), below)


def activate(value, norm):
    affine = (value.astype(jnp.float32) - norm[0]) * norm[1] + norm[2]
    return affine / (1.0 + jnp.exp(-affine))


def put_frame(shifted, place, x, frame, pair, other, message_frame, act):
    rows, width = x.shape[1], x.shape[2]
    (top, above), (bottom, below) = halo(pair, other, message_frame, width)
    put(shifted, place, 0, act(top) * above)
    for row in range(rows):
        put(shifted, place, row + 1, act(x[frame, row].astype(jnp.float32)))
    put(shifted, place, rows + 1, act(bottom) * below)


def first_body(static, *refs):
    entries, row, history, tiles, keep = static
    x, table, weights, pair, other = refs[:5]
    sums, refs = refs[5 : 5 + tiles], refs[5 + tiles :]
    shifted, outs = refs[0], refs[1:]
    if keep:
        kept, outs = outs[0], outs[1:]
    frames, rows, _, channels = x.shape
    per_group = CHANNELS // GROUPS
    shape = (channels, channels)
    member = (
        lax.broadcasted_iota(jnp.int32, shape, 0) // per_group
        == lax.broadcasted_iota(jnp.int32, shape, 1) // per_group
    ).astype(jnp.float32)
    total = sums[0][0:2]
    if tiles > 1:
        total = (total + packed_moments(pair)) + (sums[1][0:2] + packed_moments(other))
    total = jnp.concatenate([total, jnp.zeros((6, channels), jnp.float32)], axis=0)
    grouped = jnp.dot(
        total, member, precision=lax.Precision.HIGHEST, preferred_element_type=jnp.float32
    ) * (1.0 / entries)
    average, squares = grouped[0:1], grouped[1:2]
    scale = lax.rsqrt(squares - average * average + EPS) * table[row : row + 1]
    norm = (average, scale, table[row + 1 : row + 2])
    for frame in range(frames):
        put_frame(shifted, frame, x, frame, pair, other, frame, lambda value: activate(value, norm))
        if keep and frame >= frames - history:
            for line in range(rows):
                kept[frame - (frames - history), line] = shifted[1, frame, line + 1]
    products([shifted], weights, 0, frames - history, leading(weights, channels), outs)


def second_body(offset, cache, after, weights, pair, other, shifted, *outs):
    history, channels = cache.shape[0], cache.shape[3]
    for frame in range(history):
        put_frame(shifted, frame, cache, frame, pair, other, offset + frame, lambda value: value)
    products([shifted, after], weights, 0, history, leading(weights, channels), outs)


def last_body(before, after, weights, *outs):
    frames = after.shape[1]
    mine = lax.axis_index("chan")
    products([before, after], weights, 0, frames, [mine ^ 1, mine], outs)


def conv(x, messages, tiles, cache, old_messages, offset, table, row, weights, entries, keep):
    frames, rows, width, channels = x.shape
    history = cache.shape[0]
    blocks = weights.shape[2] // channels
    split = blocks == 4
    lead = 2 if split else blocks
    work = 2 * rows * width * 9 * weights.shape[1] * channels

    def led(count):
        cells = count * rows * width
        types = [jnp.bfloat16, jnp.float32] if split else [jnp.bfloat16] * blocks
        return [jax.ShapeDtypeStruct((cells, channels), kind) for kind in types]

    def padded(count):
        return jax.ShapeDtypeStruct((3, count, rows + 2, width, channels), jnp.bfloat16)

    outs = [padded(frames)]
    if keep:
        outs.append(jax.ShapeDtypeStruct(cache.shape, jnp.bfloat16))
    after, *one = call(
        functools.partial(first_body, (entries, row, history, len(tiles), keep)),
        outs + led(frames - history), (x, table, weights, *messages, *tiles),
        flops=work * (frames - history) * lead,
    )
    kept = one.pop(0) if keep else None
    before, *two = call(
        functools.partial(second_body, offset), [padded(history), *led(history)],
        (cache, after, weights, *old_messages), flops=work * history * lead,
    )

    def rest():
        cells = frames * rows * width
        outs = [jax.ShapeDtypeStruct((cells, channels), kind) for kind in (jnp.bfloat16, jnp.float32)]
        return call(last_body, outs, (before, after, weights), flops=work * frames * 2)

    return one, two, rest, kept


def swap(value, axis, step):
    return lax.ppermute(value, axis, [(i, i ^ step) for i in range(lax.axis_size(axis))])


def reduce_terms(one, two, rest):
    count = lax.axis_size("chan")
    if count != 4:
        stacked = jnp.stack([jnp.concatenate(pieces, axis=0) for pieces in zip(two, one)])
        mine = lax.axis_index("chan")
        own = lax.dynamic_index_in_dim(stacked, mine, 0, keepdims=False).astype(jnp.float32)
        terms = []
        for step in range(1, count):
            block = lax.dynamic_index_in_dim(stacked, (mine + step) % count, 0, keepdims=False)
            pairs = [(i, (i + step) % count) for i in range(count)]
            terms.append([lax.ppermute(block, "chan", pairs)])
        return own, terms
    joined = []
    for far, near in (one, two):
        arrived = swap(far, "chan", 1)
        joined.append((near + arrived.astype(jnp.float32)).astype(jnp.bfloat16))
    beside, own = rest()
    beside = swap(beside, "chan", 1)
    across = swap(jnp.concatenate(joined[::-1], axis=0), "chan", 2)
    return own, [[across], [beside]]


def to_neighbours(pair, other):
    count = lax.axis_size("rows")
    ring = [(i, (i + 1) % count) if i % 2 else (i, (i - 1) % count) for i in range(count)]
    across = lax.ppermute(other, "rows", ring)
    return swap(pair, "rows", 1), across


def over_rows(tile):
    count = lax.axis_size("rows")
    if count == 4:
        return [tile, swap(tile, "rows", 2)]
    if count & (count - 1):
        return [lax.psum(tile, "rows")]
    step = 1
    while step < count:
        tile = tile + swap(tile, "rows", step)
        step *= 2
    return [tile]


def local(
    frames_in,
    cache_first,
    gain_first,
    shift_first,
    kernel_first,
    bias_first,
    cache_second,
    gain_second,
    shift_second,
    kernel_second,
    bias_second,
):
    inward, outward = (1, 2, 3, 0), (3, 0, 1, 2)
    x, first, second = (a.transpose(inward) for a in (frames_in, cache_first, cache_second))
    frames, rows, width, channels = x.shape
    entries = frames * rows * width * (CHANNELS // GROUPS) * lax.axis_size("rows")
    vectors = [
        vector.reshape(1, channels)
        for vector in (gain_first, shift_first, bias_first, gain_second, shift_second, bias_second)
    ]

    def taps(kernel):
        return kernel.reshape(9, 3 * channels, kernel.shape[4])

    x, first, second, table, tile, pair, other, old_pair, old_other = entry(
        x, first, second, vectors
    )
    tiles = over_rows(tile)
    messages = to_neighbours(pair, other)
    old_messages = to_neighbours(old_pair, old_other)
    weights = fetch(taps(kernel_first))
    one, two, rest, _ = conv(
        x, messages, tiles, first, old_messages, 0, table, 0, weights, entries, False
    )
    own, terms = reduce_terms(one, two, rest)
    hidden, tile, pair, other = middle(own, terms, table, 2, x.shape)
    tiles = over_rows(tile)
    messages = to_neighbours(pair, other)
    weights = taps(kernel_second)
    one, two, rest, kept = conv(
        hidden, messages, tiles, second, old_messages, first.shape[0], table, 3, weights, entries,
        True,
    )
    own, terms = reduce_terms(one, two, rest)
    decoded = close(own, terms, table, 5, x.shape)
    return decoded.transpose(outward), kept.transpose(outward)


def solution(mesh):
    split = P("chan", None, ("grp", "rows"), None)
    vector = P("chan")
    kernel = P(None, None, None, "chan", None)
    return jax.shard_map(
        local,
        mesh=mesh,
        in_specs=(
            split, split, vector, vector, kernel, vector, split, vector, vector, kernel, vector
        ),
        out_specs=(split, split),
        check_vma=False,
    )
```

time: 198 us -> 59.1 us (0.30)
  local copies, waits for them, and re-layouts: 63.3 us -> 0.01 us
  waiting for transfers between devices: 76.3 us -> 26.7 us
  blocking collectives: 15.1 us -> 0 us
  Pallas kernels: 0 us -> 13.7 us
  between operations: 14.4 us -> 0.77 us
  matrix products: 12.6 us -> 0 us
  starting transfers between devices: 5.7 us -> 17.5 us
  other arithmetic: 9.73 us -> 0.15 us
    reduce_scatter x2 -> x0, waiting for transfers between devices: 74.9 us -> none  [causal_conv(): lax.psum_scatter(contract(weights, columns), 'chan', scatter_dimension=0,...]
    slice x11 -> x0, local copies, waits for them, and re-layouts: 34.2 us -> none  [the longest x8 27.9 us: build_columns(): merged[:, time_tap:time_tap + frames].reshape(9 * channel_count, -1)]
    ppermute x4 -> x16, waiting for transfers between devices: 1.37 us -> 26.7 us  [the longest x13 26.7 us: swap(): lax.ppermute(value, axis, [(i, i ^ step) for i in range(lax.axis_size(axi...]
    psum x2 -> x0, blocking collectives: 15.1 us -> none  [norm_act(): lax.psum((jnp.sum(grouped, axis=1), jnp.sum(grouped * grouped, axis=1)),...]
    pallas_call x0 -> x10, Pallas kernels: none -> 13.7 us  [call(): pl.pallas_call(body, out_shape=outs, in_specs=specs or [on_chip()] * len(...]
    reshape x2 -> x0, local copies, waits for them, and re-layouts: 13.4 us -> none  [build_columns(): jnp.stack(shifted, 0)]
    another operation x4 -> x0, local copies, waits for them, and re-layouts: 12.8 us -> none  [build_columns(): jnp.stack(shifted, 0)]
    dot_general x6 -> x0, matrix products: 12.6 us -> none  [contract(): lax.dot_general(weights[time_tap], columns[time_tap], (((0,), (0,)), ((),...]
  transfers between devices with their start and end apart: 6 -> 16, of which waited for: 3 -> 9; matrix products, arithmetic and copies ran while one was open for 3% -> 0% of each run, Pallas kernels for 0% -> 13%
where the time goes in v2:
time: 59.1 us; the launch traced here: 58.9 us
  waiting for transfers between devices  26.7 us (45%)
  starting transfers between devices  17.5 us (30%)
  Pallas kernels  13.7 us (23%)
  between operations  0.77 us (1%)
    ppermute x13, waiting for transfers between devices, swap(): lax.ppermute(value, axis, [(i, i ^ step) for i in range(lax.axis_size(axi...  26.7 us
    ppermute x13, starting transfers between devices, swap(): lax.ppermute(value, axis, [(i, i ^ step) for i in range(lax.axis_size(axi...  14.8 us
    pallas_call x10, Pallas kernels, call(): pl.pallas_call(body, out_shape=outs, in_specs=specs or [on_chip()] * len(...  13.7 us
    ppermute x3, starting transfers between devices, to_neighbours(): across = lax.ppermute(other, 'rows', ring)  2.76 us
  transfers between devices with their start and end apart: 16, of which 9 were waited for; matrix products, arithmetic and copies ran while one was open for 0% of the time, Pallas kernels for 13%

profile of v2, /device:TPU:0, one launch (start us, length us, event | category | flops | bytes accessed | tf_op | source)
XLA Modules:
  0.0 58.9 jit_solution(18036836051911793163)
XLA Ops:
  0.6 1.2 %shard_map.122 = (bf16[4,2,96,128]{3,2,1,0:T(8,128)(2,1)S(1)}, bf16[2,2,96,128]{3,2,1,0:T(8,128)(2,1)S(1)}, bf16[2,2,96,128]{3,2,1,0:T(8,128)(2,1)S(1)}, f32[8,1...) custom-call(bf16[4,2,96,128]{3,2,1,0:T(8,128)(2,1)} %bitcast.17, ...), custom_call_target="tpu_custom_call" | custom-call | bytes 1199104 | tf_op jit(solution)/shard_map/pallas_call | solution.py:29
  2.4 2.6 %collective-permute-start.1 = (bf16[400,128]{1,0:T(8,128)(2,1)S(1)}, bf16[400,128]{1,0:T(8,128)(2,1)S(1)}, u32[]{:S(2)}, u32[]{:S(2)}) collective-permute-start(bf16[400,128]{1,0:T(8,128)(2,1)S(1)} %get-tuple-element.37), channel_id=1, source_target_pairs={{0,12},{4,8},{8,4},{12,0},{1,13},{5,9},{9,5},{13,1},{2,14},{6,10},... | collective-permute-start | bytes 307208 | tf_op jit(solution)/shard_map/ppermute | solution.py:369
  5.1 2.0 %collective-permute-start.2 = (f32[8,128]{1,0:T(8,128)S(1)}, f32[8,128]{1,0:T(8,128)S(1)}, u32[]{:S(2)}, u32[]{:S(2)}) collective-permute-start(f32[8,128]{1,0:T(8,128)S(1)} %get-tuple-element.38.refs_5_), channel_id=1, source_target_pairs={{0,8},{4,12},{8,0},{12,4},{1,9},{5,13},{9,1},{13,5},{2,10},{6,14},... | collective-permute-start | bytes 12296 | tf_op jit(solution)/shard_map/ppermute | solution.py:341
  7.1 2.0 %shard_map.123.refs_2_.weights = bf16[9,384,512]{2,1,0:T(8,128)(2,1)S(1)} custom-call(bf16[9,384,512]{2,1,0:T(8,128)(2,1)} %bitcast.16), custom_call_target="tpu_custom_call" | custom-call | bytes 7077888 | tf_op jit(solution)/shard_map/pallas_call | solution.py:29
  9.2 1.5 %collective-permute-done.2.refs_6_ = f32[8,128]{1,0:T(8,128)S(1)} collective-permute-done((f32[8,128]{1,0:T(8,128)S(1)}, f32[8,128]{1,0:T(8,128)S(1)}, u32[]{:S(2)}, u32[]{:S(2)}) %collective-permute-start.2) | collective-permute-done | bytes 4128 | tf_op jit(solution)/shard_map/ppermute | solution.py:341
  10.6 1.5 %shard_map.124 = (bf16[3,4,4,96,128]{4,3,2,1,0:T(8,128)(2,1)S(1)}, bf16[384,128]{1,0:T(8,128)(2,1)S(1)}, f32[384,128]{1,0:T(8,128)S(1)}) custom-call(bf16[4,2,96,128]{3,2,1,0:T(8,128)(2,1)S(1)} %get-tuple-element.34.refs_0_, f32[8,128]{1,0:T(8,128)S(1)} %get-tuple-element.35.refs_1_.refs_2_, bf16[9,384,512]{2,1,0:T(8,128)(2,1)S(1)} %shard_map.123.refs_2_.weights, ...), custom_call_target="tpu_custom_call" | custom-call | flops 679477248 | bytes 5427200 | tf_op jit(solution)/shard_map/pallas_call | solution.py:29
  13.3 1.8 %collective-permute-start.5 = (bf16[384,128]{1,0:T(8,128)(2,1)S(1)}, bf16[384,128]{1,0:T(8,128)(2,1)S(1)}, u32[]{:S(2)}, u32[]{:S(2)}) collective-permute-start(bf16[384,128]{1,0:T(8,128)(2,1)S(1)} %get-tuple-element.45), channel_id=1, source_target_pairs={{0,1},{1,0},{2,3},{3,2},{4,5},{5,4},{6,7},{7,6},{8,9},{9,8},{10,11... | collective-permute-start | bytes 294920 | tf_op jit(solution)/shard_map/ppermute | solution.py:341
  15.4 2.0 %shard_map.126 = (bf16[768,128]{1,0:T(8,128)(2,1)S(1)}, f32[768,128]{1,0:T(8,128)S(1)}) custom-call(bf16[3,2,4,96,128]{4,3,2,1,0:T(8,128)(2,1)S(1)} %get-tuple-element.42.before, bf16[3,4,4,96,128]{4,3,2,1,0:T(8,128)(2,1)S(1)} %get-tuple-element.39.after, bf16[9,384,512]{2,1,0:T(8,128)(2,1)S(1)} %shard_map.123.refs_2_.weights), custom_call_target="tpu_custom_call" | custom-call | flops 1358954496 | bytes 5898240 | tf_op jit(solution)/shard_map/pallas_call | solution.py:29
  17.4 1.8 %collective-permute-start.8 = (bf16[768,128]{1,0:T(8,128)(2,1)S(1)}, bf16[768,128]{1,0:T(8,128)(2,1)S(1)}, u32[]{:S(2)}, u32[]{:S(2)}) collective-permute-start(bf16[768,128]{1,0:T(8,128)(2,1)S(1)} %get-tuple-element.48), channel_id=1, source_target_pairs={{0,1},{1,0},{2,3},{3,2},{4,5},{5,4},{6,7},{7,6},{8,9},{9,8},{10,11... | collective-permute-start | bytes 589832 | tf_op jit(solution)/shard_map/ppermute | solution.py:341
  19.2 1.6 %collective-permute-done.6 = bf16[384,128]{1,0:T(8,128)(2,1)S(1)} collective-permute-done((bf16[384,128]{1,0:T(8,128)(2,1)S(1)}, bf16[384,128]{1,0:T(8,128)(2,1)S(1)}, u32[]{:S(2)}, u32[]{:S(2)}) %collective-permute-start.6) | collective-permute-done | bytes 98336 | tf_op jit(solution)/shard_map/ppermute | solution.py:341
  20.9 2.7 %collective-permute-start.7 = (bf16[768,128]{1,0:T(8,128)(2,1)S(1)}, bf16[768,128]{1,0:T(8,128)(2,1)S(1)}, u32[]{:S(2)}, u32[]{:S(2)}) collective-permute-start(bf16[768,128]{1,0:T(8,128)(2,1)S(1)} %pad_maximum_fusion), channel_id=1, source_target_pairs={{0,2},{1,3},{2,0},{3,1},{4,6},{5,7},{6,4},{7,5},{8,10},{9,11},{10,... | collective-permute-start | bytes 589832 | tf_op jit(solution)/shard_map/ppermute | solution.py:341
  23.6 3.7 %collective-permute-done.8.refs_1_ = bf16[768,128]{1,0:T(8,128)(2,1)S(1)} collective-permute-done((bf16[768,128]{1,0:T(8,128)(2,1)S(1)}, bf16[768,128]{1,0:T(8,128)(2,1)S(1)}, u32[]{:S(2)}, u32[]{:S(2)}) %collective-permute-start.8) | collective-permute-done | bytes 196640 | tf_op jit(solution)/shard_map/ppermute | solution.py:341
  27.3 4.3 %collective-permute-done.7.refs_0_ = bf16[768,128]{1,0:T(8,128)(2,1)S(1)} collective-permute-done((bf16[768,128]{1,0:T(8,128)(2,1)S(1)}, bf16[768,128]{1,0:T(8,128)(2,1)S(1)}, u32[]{:S(2)}, u32[]{:S(2)}) %collective-permute-start.7) | collective-permute-done | bytes 196640 | tf_op jit(solution)/shard_map/ppermute | solution.py:341
  31.9 1.6 %collective-permute-start.9 = (bf16[400,128]{1,0:T(8,128)(2,1)S(1)}, bf16[400,128]{1,0:T(8,128)(2,1)S(1)}, u32[]{:S(2)}, u32[]{:S(2)}) collective-permute-start(bf16[400,128]{1,0:T(8,128)(2,1)S(1)} %get-tuple-element.50), channel_id=1, source_target_pairs={{0,4},{4,0},{8,12},{12,8},{1,5},{5,1},{9,13},{13,9},{2,6},{6,2},{1... | collective-permute-start | bytes 307208 | tf_op jit(solution)/shard_map/ppermute | solution.py:341
  34.0 3.1 %collective-permute-done.11.refs_6_ = f32[8,128]{1,0:T(8,128)S(1)} collective-permute-done((f32[8,128]{1,0:T(8,128)S(1)}, f32[8,128]{1,0:T(8,128)S(1)}, u32[]{:S(2)}, u32[]{:S(2)}) %collective-permute-start.11) | collective-permute-done | bytes 4128 | tf_op jit(solution)/shard_map/ppermute | solution.py:341
  37.1 1.8 %shard_map.128 = (bf16[3,4,4,96,128]{4,3,2,1,0:T(8,128)(2,1)S(1)}, bf16[2,2,96,128]{3,2,1,0:T(8,128)(2,1)}, bf16[384,128]{1,0:T(8,128)(2,1)S(1)}, f32[384,128]{1,0:T(8,128)S(1)}) custom-call(bf16[4,2,96,128]{3,2,1,0:T(8,128)(2,1)S(1)} %get-tuple-element.49.refs_0_, f32[8,128]{1,0:T(8,128)S(1)} %get-tuple-element.35.refs_1_.refs_2_, ...), custom_call_target="tpu_custom_call" | custom-call | flops 679477248 | bytes 5525504 | tf_op jit(solution)/shard_map/pallas_call | solution.py:29
  39.0 1.2 %shard_map.129 = (bf16[3,2,4,96,128]{4,3,2,1,0:T(8,128)(2,1)S(1)}, bf16[384,128]{1,0:T(8,128)(2,1)S(1)}, f32[384,128]{1,0:T(8,128)S(1)}) custom-call(bf16[2,2,96,128]{3,2,1,0:T(8,128)(2,1)S(1)} %get-tuple-element.32.cache, bf16[3,4,4,96,128]{4,3,2,1,0:T(8,128)(2,1)S(1)} %get-tuple-element.53.after, bf16[9,384,512]{2,1,0:T(8,128)(2,1)S(1)} %bitcast.14, ...), custom_call_target="tpu_custom_call" | custom-call | flops 679477248 | bytes 5898240 | tf_op jit(solution)/shard_map/pallas_call | solution.py:29
  40.2 2.0 %collective-permute-start.13 = (bf16[384,128]{1,0:T(8,128)(2,1)S(1)}, bf16[384,128]{1,0:T(8,128)(2,1)S(1)}, u32[]{:S(2)}, u32[]{:S(2)}) collective-permute-start(bf16[384,128]{1,0:T(8,128)(2,1)S(1)} %get-tuple-element.59), channel_id=1, source_target_pairs={{0,1},{1,0},{2,3},{3,2},{4,5},{5,4},{6,7},{7,6},{8,9},{9,8},{10,11... | collective-permute-start | bytes 294920 | tf_op jit(solution)/shard_map/ppermute | solution.py:341
  42.2 2.0 %shard_map.130 = (bf16[768,128]{1,0:T(8,128)(2,1)S(1)}, f32[768,128]{1,0:T(8,128)S(1)}) custom-call(bf16[3,2,4,96,128]{4,3,2,1,0:T(8,128)(2,1)S(1)} %get-tuple-element.54.before, bf16[3,4,4,96,128]{4,3,2,1,0:T(8,128)(2,1)S(1)} %get-tuple-element.53.after, bf16[9,384,512]{2,1,0:T(8,128)(2,1)S(1)} %bitcast.15), custom_call_target="tpu_custom_call" | custom-call | flops 1358954496 | bytes 5898240 | tf_op jit(solution)/shard_map/pallas_call | solution.py:29
  44.3 1.5 %collective-permute-done.12 = bf16[384,128]{1,0:T(8,128)(2,1)S(1)} collective-permute-done((bf16[384,128]{1,0:T(8,128)(2,1)S(1)}, bf16[384,128]{1,0:T(8,128)(2,1)S(1)}, u32[]{:S(2)}, u32[]{:S(2)}) %collective-permute-start.12) | collective-permute-done | bytes 98336 | tf_op jit(solution)/shard_map/ppermute | solution.py:341
  45.9 1.8 %collective-permute-done.13 = bf16[384,128]{1,0:T(8,128)(2,1)S(1)} collective-permute-done((bf16[384,128]{1,0:T(8,128)(2,1)S(1)}, bf16[384,128]{1,0:T(8,128)(2,1)S(1)}, u32[]{:S(2)}, u32[]{:S(2)}) %collective-permute-start.13) | collective-permute-done | bytes 98336 | tf_op jit(solution)/shard_map/ppermute | solution.py:341
  47.7 1.2 %collective-permute-start.14 = (bf16[768,128]{1,0:T(8,128)(2,1)S(1)}, bf16[768,128]{1,0:T(8,128)(2,1)S(1)}, u32[]{:S(2)}, u32[]{:S(2)}) collective-permute-start(bf16[768,128]{1,0:T(8,128)(2,1)S(1)} %pad_maximum_fusion.1), channel_id=1, source_target_pairs={{0,2},{1,3},{2,0},{3,1},{4,6},{5,7},{6,4},{7,5},{8,10},{9,11},{10,... | collective-permute-start | bytes 589832 | tf_op jit(solution)/shard_map/ppermute | solution.py:341
  48.9 4.5 %collective-permute-done.15.refs_1_ = bf16[768,128]{1,0:T(8,128)(2,1)S(1)} collective-permute-done((bf16[768,128]{1,0:T(8,128)(2,1)S(1)}, bf16[768,128]{1,0:T(8,128)(2,1)S(1)}, u32[]{:S(2)}, u32[]{:S(2)}) %collective-permute-start.15) | collective-permute-done | bytes 196640 | tf_op jit(solution)/shard_map/ppermute | solution.py:341
  53.4 4.8 %collective-permute-done.14.refs_0_ = bf16[768,128]{1,0:T(8,128)(2,1)S(1)} collective-permute-done((bf16[768,128]{1,0:T(8,128)(2,1)S(1)}, bf16[768,128]{1,0:T(8,128)(2,1)S(1)}, u32[]{:S(2)}, u32[]{:S(2)}) %collective-permute-start.14) | collective-permute-done | bytes 196640 | tf_op jit(solution)/shard_map/ppermute | solution.py:341
  (26 shorter events, 4.1 us)
Async XLA Ops:
  1.8 8.8 %collective-permute-start = (bf16[400,128]{1,0:T(8,128)(2,1)S(1)}, bf16[400,128]{1,0:T(8,128)(2,1)S(1)}, u32[]{:S(2)}, u32[]{:S(2)}) collective-permute-start(bf16[400,128]{1,0:T(8,128)(2,1)S(1)} %get-tuple-element.36), channel_id=1, source_target_pairs={{0,4},{4,0},{8,12},{12,8},{1,5},{5,1},{9,13},{13,9},{2,6},{6,2},{1... | collective-permute-start | bytes 307208 | tf_op jit(solution)/shard_map/ppermute | solution.py:341
  2.4 8.3 %collective-permute-start.1 = (bf16[400,128]{1,0:T(8,128)(2,1)S(1)}, bf16[400,128]{1,0:T(8,128)(2,1)S(1)}, u32[]{:S(2)}, u32[]{:S(2)}) collective-permute-start(bf16[400,128]{1,0:T(8,128)(2,1)S(1)} %get-tuple-element.37), channel_id=1, source_target_pairs={{0,12},{4,8},{8,4},{12,0},{1,13},{5,9},{9,5},{13,1},{2,14},{6,10},... | collective-permute-start | bytes 307208 | tf_op jit(solution)/shard_map/ppermute | solution.py:369
  5.0 7.1 %collective-permute-start.3 = (bf16[384,128]{1,0:T(8,128)(2,1)S(1)}, bf16[384,128]{1,0:T(8,128)(2,1)S(1)}, u32[]{:S(2)}, u32[]{:S(2)}) collective-permute-start(bf16[384,128]{1,0:T(8,128)(2,1)S(1)} %get-tuple-element.40), channel_id=1, source_target_pairs={{0,4},{4,0},{8,12},{12,8},{1,5},{5,1},{9,13},{13,9},{2,6},{6,2},{1... | collective-permute-start | bytes 294920 | tf_op jit(solution)/shard_map/ppermute | solution.py:341
  5.1 7.0 %collective-permute-start.4 = (bf16[384,128]{1,0:T(8,128)(2,1)S(1)}, bf16[384,128]{1,0:T(8,128)(2,1)S(1)}, u32[]{:S(2)}, u32[]{:S(2)}) collective-permute-start(bf16[384,128]{1,0:T(8,128)(2,1)S(1)} %get-tuple-element.41), channel_id=1, source_target_pairs={{0,12},{4,8},{8,4},{12,0},{1,13},{5,9},{9,5},{13,1},{2,14},{6,10},... | collective-permute-start | bytes 294920 | tf_op jit(solution)/shard_map/ppermute | solution.py:369
  5.1 5.5 %collective-permute-start.2 = (f32[8,128]{1,0:T(8,128)S(1)}, f32[8,128]{1,0:T(8,128)S(1)}, u32[]{:S(2)}, u32[]{:S(2)}) collective-permute-start(f32[8,128]{1,0:T(8,128)S(1)} %get-tuple-element.38.refs_5_), channel_id=1, source_target_pairs={{0,8},{4,12},{8,0},{12,4},{1,9},{5,13},{9,1},{13,5},{2,10},{6,14},... | collective-permute-start | bytes 12296 | tf_op jit(solution)/shard_map/ppermute | solution.py:341
  13.3 5.9 %collective-permute-start.5 = (bf16[384,128]{1,0:T(8,128)(2,1)S(1)}, bf16[384,128]{1,0:T(8,128)(2,1)S(1)}, u32[]{:S(2)}, u32[]{:S(2)}) collective-permute-start(bf16[384,128]{1,0:T(8,128)(2,1)S(1)} %get-tuple-element.45), channel_id=1, source_target_pairs={{0,1},{1,0},{2,3},{3,2},{4,5},{5,4},{6,7},{7,6},{8,9},{9,8},{10,11... | collective-permute-start | bytes 294920 | tf_op jit(solution)/shard_map/ppermute | solution.py:341
  15.1 5.8 %collective-permute-start.6 = (bf16[384,128]{1,0:T(8,128)(2,1)S(1)}, bf16[384,128]{1,0:T(8,128)(2,1)S(1)}, u32[]{:S(2)}, u32[]{:S(2)}) collective-permute-start(bf16[384,128]{1,0:T(8,128)(2,1)S(1)} %get-tuple-element.47), channel_id=1, source_target_pairs={{0,1},{1,0},{2,3},{3,2},{4,5},{5,4},{6,7},{7,6},{8,9},{9,8},{10,11... | collective-permute-start | bytes 294920 | tf_op jit(solution)/shard_map/ppermute | solution.py:341
  15.4 21.8 %copy-start = (bf16[3,3,3,128,512]{4,3,2,1,0:T(8,128)(2,1)S(1)}, bf16[3,3,3,128,512]{4,3,2,1,0:T(8,128)(2,1)}, u32[]{:S(2)}) copy-start(bf16[3,3,3,128,512]{4,3,2,1,0:T(8,128)(2,1)} %param.20) | copy-start | bytes 10616836
  17.4 9.9 %collective-permute-start.8 = (bf16[768,128]{1,0:T(8,128)(2,1)S(1)}, bf16[768,128]{1,0:T(8,128)(2,1)S(1)}, u32[]{:S(2)}, u32[]{:S(2)}) collective-permute-start(bf16[768,128]{1,0:T(8,128)(2,1)S(1)} %get-tuple-element.48), channel_id=1, source_target_pairs={{0,1},{1,0},{2,3},{3,2},{4,5},{5,4},{6,7},{7,6},{8,9},{9,8},{10,11... | collective-permute-start | bytes 589832 | tf_op jit(solution)/shard_map/ppermute | solution.py:341
  20.9 10.7 %collective-permute-start.7 = (bf16[768,128]{1,0:T(8,128)(2,1)S(1)}, bf16[768,128]{1,0:T(8,128)(2,1)S(1)}, u32[]{:S(2)}, u32[]{:S(2)}) collective-permute-start(bf16[768,128]{1,0:T(8,128)(2,1)S(1)} %pad_maximum_fusion), channel_id=1, source_target_pairs={{0,2},{1,3},{2,0},{3,1},{4,6},{5,7},{6,4},{7,5},{8,10},{9,11},{10,... | collective-permute-start | bytes 589832 | tf_op jit(solution)/shard_map/ppermute | solution.py:341
  31.8 5.3 %collective-permute-start.10 = (bf16[400,128]{1,0:T(8,128)(2,1)S(1)}, bf16[400,128]{1,0:T(8,128)(2,1)S(1)}, u32[]{:S(2)}, u32[]{:S(2)}) collective-permute-start(bf16[400,128]{1,0:T(8,128)(2,1)S(1)} %get-tuple-element.51), channel_id=1, source_target_pairs={{0,12},{4,8},{8,4},{12,0},{1,13},{5,9},{9,5},{13,1},{2,14},{6,10},... | collective-permute-start | bytes 307208 | tf_op jit(solution)/shard_map/ppermute | solution.py:369
  31.9 5.3 %collective-permute-start.9 = (bf16[400,128]{1,0:T(8,128)(2,1)S(1)}, bf16[400,128]{1,0:T(8,128)(2,1)S(1)}, u32[]{:S(2)}, u32[]{:S(2)}) collective-permute-start(bf16[400,128]{1,0:T(8,128)(2,1)S(1)} %get-tuple-element.50), channel_id=1, source_target_pairs={{0,4},{4,0},{8,12},{12,8},{1,5},{5,1},{9,13},{13,9},{2,6},{6,2},{1... | collective-permute-start | bytes 307208 | tf_op jit(solution)/shard_map/ppermute | solution.py:341
  33.5 3.7 %collective-permute-start.11 = (f32[8,128]{1,0:T(8,128)S(1)}, f32[8,128]{1,0:T(8,128)S(1)}, u32[]{:S(2)}, u32[]{:S(2)}) collective-permute-start(f32[8,128]{1,0:T(8,128)S(1)} %get-tuple-element.52.refs_5_), channel_id=1, source_target_pairs={{0,8},{4,12},{8,0},{12,4},{1,9},{5,13},{9,1},{13,5},{2,10},{6,14},... | collective-permute-start | bytes 12296 | tf_op jit(solution)/shard_map/ppermute | solution.py:341
  40.1 5.7 %collective-permute-start.12 = (bf16[384,128]{1,0:T(8,128)(2,1)S(1)}, bf16[384,128]{1,0:T(8,128)(2,1)S(1)}, u32[]{:S(2)}, u32[]{:S(2)}) collective-permute-start(bf16[384,128]{1,0:T(8,128)(2,1)S(1)} %get-tuple-element.57), channel_id=1, source_target_pairs={{0,1},{1,0},{2,3},{3,2},{4,5},{5,4},{6,7},{7,6},{8,9},{9,8},{10,11... | collective-permute-start | bytes 294920 | tf_op jit(solution)/shard_map/ppermute | solution.py:341
  40.2 7.5 %collective-permute-start.13 = (bf16[384,128]{1,0:T(8,128)(2,1)S(1)}, bf16[384,128]{1,0:T(8,128)(2,1)S(1)}, u32[]{:S(2)}, u32[]{:S(2)}) collective-permute-start(bf16[384,128]{1,0:T(8,128)(2,1)S(1)} %get-tuple-element.59), channel_id=1, source_target_pairs={{0,1},{1,0},{2,3},{3,2},{4,5},{5,4},{6,7},{7,6},{8,9},{9,8},{10,11... | collective-permute-start | bytes 294920 | tf_op jit(solution)/shard_map/ppermute | solution.py:341
  44.2 9.2 %collective-permute-start.15 = (bf16[768,128]{1,0:T(8,128)(2,1)S(1)}, bf16[768,128]{1,0:T(8,128)(2,1)S(1)}, u32[]{:S(2)}, u32[]{:S(2)}) collective-permute-start(bf16[768,128]{1,0:T(8,128)(2,1)S(1)} %get-tuple-element.60), channel_id=1, source_target_pairs={{0,1},{1,0},{2,3},{3,2},{4,5},{5,4},{6,7},{7,6},{8,9},{9,8},{10,11... | collective-permute-start | bytes 589832 | tf_op jit(solution)/shard_map/ppermute | solution.py:341
  47.7 10.5 %collective-permute-start.14 = (bf16[768,128]{1,0:T(8,128)(2,1)S(1)}, bf16[768,128]{1,0:T(8,128)(2,1)S(1)}, u32[]{:S(2)}, u32[]{:S(2)}) collective-permute-start(bf16[768,128]{1,0:T(8,128)(2,1)S(1)} %pad_maximum_fusion.1), channel_id=1, source_target_pairs={{0,2},{1,3},{2,0},{3,1},{4,6},{5,7},{6,4},{7,5},{8,10},{9,11},{10,... | collective-permute-start | bytes 589832 | tf_op jit(solution)/shard_map/ppermute | solution.py:341

commit v3 on v2

--- a/solution.py
+++ b/solution.py
@@ -45,7 +45,9 @@
 
 def store_moments(tile, messages, moments):
     channels = moments.shape[1]
-    tile[...] = jnp.concatenate([moments, jnp.zeros((6, channels), jnp.float32)], axis=0)
+    if tile.dtype == jnp.float32:
+        tile[...] = jnp.concatenate([moments, jnp.zeros((6, channels), jnp.float32)], axis=0)
+        return
     terms, rest = [], moments
     for _ in range(3):
         term = rest.astype(jnp.bfloat16).astype(jnp.float32)
@@ -53,13 +55,15 @@
         rest = rest - term
     terms.append(jnp.zeros((PACKED - 6, channels), jnp.float32))
     packed = jnp.concatenate(terms, axis=0).astype(jnp.bfloat16)
+    tile[...] = packed
     for message in messages:
         message[message.shape[0] - PACKED :] = packed
 
 
-def packed_moments(message):
-    rows = message[message.shape[0] - PACKED :].astype(jnp.float32)
-    return (rows[0:2] + rows[2:4]) + rows[4:6]
+def moments_tile(channels):
+    if lax.axis_size("rows") == 4:
+        return jax.ShapeDtypeStruct((PACKED, channels), jnp.bfloat16)
+    return jax.ShapeDtypeStruct((8, channels), jnp.float32)
 
 
 def store_edges(sources, pair, other):
@@ -102,7 +106,7 @@
     outs = [
         *[jax.ShapeDtypeStruct(a.shape, a.dtype) for a in (x, first, second)],
         jax.ShapeDtypeStruct((8, channels), jnp.float32),
-        jax.ShapeDtypeStruct((8, channels), jnp.float32),
+        moments_tile(channels),
         *message_shapes(frames, width, channels, PACKED),
         *message_shapes(first.shape[0] + second.shape[0], width, channels, 0),
     ]
@@ -161,7 +165,7 @@
     frames, _, width, channels = shape
     outs = [
         jax.ShapeDtypeStruct(shape, jnp.bfloat16),
-        jax.ShapeDtypeStruct((8, channels), jnp.float32),
+        moments_tile(channels),
         *message_shapes(frames, width, channels, PACKED),
     ]
     body = functools.partial(middle_body, row, [len(group) for group in terms])
@@ -255,34 +259,37 @@
 
 
 def first_body(static, *refs):
-    entries, row, history, tiles, keep = static
+    entries, row, history, tiles = static
     x, table, weights, pair, other = refs[:5]
     sums, refs = refs[5 : 5 + tiles], refs[5 + tiles :]
     shifted, outs = refs[0], refs[1:]
-    if keep:
-        kept, outs = outs[0], outs[1:]
-    frames, rows, _, channels = x.shape
+    frames, _, _, channels = x.shape
     per_group = CHANNELS // GROUPS
     shape = (channels, channels)
     member = (
         lax.broadcasted_iota(jnp.int32, shape, 0) // per_group
         == lax.broadcasted_iota(jnp.int32, shape, 1) // per_group
-    ).astype(jnp.float32)
-    total = sums[0][0:2]
+    ).astype(sums[0].dtype)
     if tiles > 1:
-        total = (total + packed_moments(pair)) + (sums[1][0:2] + packed_moments(other))
-    total = jnp.concatenate([total, jnp.zeros((6, channels), jnp.float32)], axis=0)
-    grouped = jnp.dot(
-        total, member, precision=lax.Precision.HIGHEST, preferred_element_type=jnp.float32
-    ) * (1.0 / entries)
+        last = [message[message.shape[0] - PACKED :] for message in (pair, other)]
+        packed = jnp.concatenate([sums[0][...], last[0], sums[1][...], last[1]], axis=0)
+        terms = jnp.dot(packed, member, preferred_element_type=jnp.float32)
+        mine, beside, across, corner = (
+            terms[PACKED * i : PACKED * (i + 1)] for i in range(4)
+        )
+        terms = (mine + beside) + (across + corner)
+        grouped = (terms[0:2] + terms[2:4]) + terms[4:6]
+    else:
+        grouped = jnp.dot(
+            sums[0][...], member, precision=lax.Precision.HIGHEST,
+            preferred_element_type=jnp.float32,
+        )
+    grouped = grouped * (1.0 / entries)
     average, squares = grouped[0:1], grouped[1:2]
     scale = lax.rsqrt(squares - average * average + EPS) * table[row : row + 1]
     norm = (average, scale, table[row + 1 : row + 2])
     for frame in range(frames):
         put_frame(shifted, frame, x, frame, pair, other, frame, lambda value: activate(value, norm))
-        if keep and frame >= frames - history:
-            for line in range(rows):
-                kept[frame - (frames - history), line] = shifted[1, frame, line + 1]
     products([shifted], weights, 0, frames - history, leading(weights, channels), outs)
 
 
@@ -293,13 +300,17 @@
     products([shifted, after], weights, 0, history, leading(weights, channels), outs)
 
 
+def keep_body(after, kept):
+    kept[...] = after[1, after.shape[1] - kept.shape[0] :, 1 : 1 + kept.shape[1]]
+
+
 def last_body(before, after, weights, *outs):
     frames = after.shape[1]
     mine = lax.axis_index("chan")
     products([before, after], weights, 0, frames, [mine ^ 1, mine], outs)
 
 
-def conv(x, messages, tiles, cache, old_messages, offset, table, row, weights, entries, keep):
+def conv(x, messages, tiles, cache, old_messages, offset, table, row, weights, entries):
     frames, rows, width, channels = x.shape
     history = cache.shape[0]
     blocks = weights.shape[2] // channels
@@ -315,15 +326,11 @@
     def padded(count):
         return jax.ShapeDtypeStruct((3, count, rows + 2, width, channels), jnp.bfloat16)
 
-    outs = [padded(frames)]
-    if keep:
-        outs.append(jax.ShapeDtypeStruct(cache.shape, jnp.bfloat16))
     after, *one = call(
-        functools.partial(first_body, (entries, row, history, len(tiles), keep)),
-        outs + led(frames - history), (x, table, weights, *messages, *tiles),
+        functools.partial(first_body, (entries, row, history, len(tiles))),
+        [padded(frames), *led(frames - history)], (x, table, weights, *messages, *tiles),
         flops=work * (frames - history) * lead,
     )
-    kept = one.pop(0) if keep else None
     before, *two = call(
         functools.partial(second_body, offset), [padded(history), *led(history)],
         (cache, after, weights, *old_messages), flops=work * history * lead,
@@ -333,6 +340,10 @@
         cells = frames * rows * width
         outs = [jax.ShapeDtypeStruct((cells, channels), kind) for kind in (jnp.bfloat16, jnp.float32)]
         return call(last_body, outs, (before, after, weights), flops=work * frames * 2)
+
+    def kept():
+        outs = [jax.ShapeDtypeStruct(cache.shape, jnp.bfloat16)]
+        return call(keep_body, outs, (after,))[0]
 
     return one, two, rest, kept
 
@@ -357,10 +368,10 @@
     for far, near in (one, two):
         arrived = swap(far, "chan", 1)
         joined.append((near + arrived.astype(jnp.float32)).astype(jnp.bfloat16))
-    beside, own = rest()
-    beside = swap(beside, "chan", 1)
+    block, own = rest()
+    beside = swap(block, "chan", 1)
     across = swap(jnp.concatenate(joined[::-1], axis=0), "chan", 2)
-    return own, [[across], [beside]]
+    return own, [[beside], [across]]
 
 
 def to_neighbours(pair, other):
@@ -415,19 +426,19 @@
     messages = to_neighbours(pair, other)
     old_messages = to_neighbours(old_pair, old_other)
     weights = fetch(taps(kernel_first))
-    one, two, rest, _ = conv(
-        x, messages, tiles, first, old_messages, 0, table, 0, weights, entries, False
-    )
-    own, terms = reduce_terms(one, two, rest)
+    *parts, _ = conv(
+        x, messages, tiles, first, old_messages, 0, table, 0, weights, entries
+    )
+    own, terms = reduce_terms(*parts)
     hidden, tile, pair, other = middle(own, terms, table, 2, x.shape)
     tiles = over_rows(tile)
     messages = to_neighbours(pair, other)
     weights = taps(kernel_second)
-    one, two, rest, kept = conv(
-        hidden, messages, tiles, second, old_messages, first.shape[0], table, 3, weights, entries,
-        True,
-    )
-    own, terms = reduce_terms(one, two, rest)
+    *parts, kept = conv(
+        hidden, messages, tiles, second, old_messages, first.shape[0], table, 3, weights, entries
+    )
+    own, terms = reduce_terms(*parts)
+    kept = kept()
     decoded = close(own, terms, table, 5, x.shape)
     return decoded.transpose(outward), kept.transpose(outward)
 

time: 59.1 us -> 58.5 us (0.990)
  waiting for transfers between devices: 26.7 us -> 26.1 us
    ppermute x13, waiting for transfers between devices: 26.7 us -> 26.1 us  [swap(): lax.ppermute(value, axis, [(i, i ^ step) for i in range(lax.axis_size(axi...]
    pallas_call x10 -> x11, Pallas kernels: 13.7 us -> 13.8 us  [call(): pl.pallas_call(body, out_shape=outs, in_specs=specs or [on_chip()] * len(...]
  transfers between devices with their start and end apart: 16 -> 16, of which waited for: 9 -> 9; matrix products, arithmetic and copies ran while one was open for 0% -> 0% of each run, Pallas kernels for 13% -> 14%
where the time goes in v3:
time: 58.5 us; the launch traced here: 58.3 us
  waiting for transfers between devices  26.1 us (45%)
  starting transfers between devices  17.5 us (30%)
  Pallas kernels  13.8 us (24%)
  between operations  0.78 us (1%)
    ppermute x13, waiting for transfers between devices, swap(): lax.ppermute(value, axis, [(i, i ^ step) for i in range(lax.axis_size(axi...  26.1 us
    ppermute x13, starting transfers between devices, swap(): lax.ppermute(value, axis, [(i, i ^ step) for i in range(lax.axis_size(axi...  14.8 us
    pallas_call x11, Pallas kernels, call(): pl.pallas_call(body, out_shape=outs, in_specs=specs or [on_chip()] * len(...  13.8 us
    ppermute x3, starting transfers between devices, to_neighbours(): across = lax.ppermute(other, 'rows', ring)  2.76 us
  transfers between devices with their start and end apart: 16, of which 9 were waited for; matrix products, arithmetic and copies ran while one was open for 0% of the time, Pallas kernels for 14%

profile of v3, /device:TPU:0, one launch (start us, length us, event | category | flops | bytes accessed | tf_op | source)
XLA Modules:
  0.0 58.3 jit_solution(14306970319242775481)
XLA Ops:
  0.6 1.2 %shard_map.122 = (bf16[4,2,96,128]{3,2,1,0:T(8,128)(2,1)S(1)}, bf16[2,2,96,128]{3,2,1,0:T(8,128)(2,1)S(1)}, bf16[2,2,96,128]{3,2,1,0:T(8,128)(2,1)S(1)}, f32[8,1...) custom-call(bf16[4,2,96,128]{3,2,1,0:T(8,128)(2,1)} %bitcast.17, ...), custom_call_target="tpu_custom_call" | custom-call | bytes 1199104 | tf_op jit(solution)/shard_map/pallas_call | solution.py:29
  2.4 2.6 %collective-permute-start.1 = (bf16[400,128]{1,0:T(8,128)(2,1)S(1)}, bf16[400,128]{1,0:T(8,128)(2,1)S(1)}, u32[]{:S(2)}, u32[]{:S(2)}) collective-permute-start(bf16[400,128]{1,0:T(8,128)(2,1)S(1)} %get-tuple-element.36), channel_id=1, source_target_pairs={{0,12},{4,8},{8,4},{12,0},{1,13},{5,9},{9,5},{13,1},{2,14},{6,10},... | collective-permute-start | bytes 307208 | tf_op jit(solution)/shard_map/ppermute | solution.py:380
  5.1 2.0 %collective-permute-start.2 = (bf16[16,128]{1,0:T(8,128)(2,1)S(1)}, bf16[16,128]{1,0:T(8,128)(2,1)S(1)}, u32[]{:S(2)}, u32[]{:S(2)}) collective-permute-start(bf16[16,128]{1,0:T(8,128)(2,1)S(1)} %get-tuple-element.37.refs_5_), channel_id=1, source_target_pairs={{0,8},{4,12},{8,0},{12,4},{1,9},{5,13},{9,1},{13,5},{2,10},{6,14},... | collective-permute-start | bytes 12296 | tf_op jit(solution)/shard_map/ppermute | solution.py:352
  7.1 2.0 %shard_map.123.refs_2_.weights = bf16[9,384,512]{2,1,0:T(8,128)(2,1)S(1)} custom-call(bf16[9,384,512]{2,1,0:T(8,128)(2,1)} %bitcast.16), custom_call_target="tpu_custom_call" | custom-call | bytes 7077888 | tf_op jit(solution)/shard_map/pallas_call | solution.py:29
  9.2 1.5 %collective-permute-done.2.refs_6_ = bf16[16,128]{1,0:T(8,128)(2,1)S(1)} collective-permute-done((bf16[16,128]{1,0:T(8,128)(2,1)S(1)}, bf16[16,128]{1,0:T(8,128)(2,1)S(1)}, u32[]{:S(2)}, u32[]{:S(2)}) %collective-permute-start.2) | collective-permute-done | bytes 4128 | tf_op jit(solution)/shard_map/ppermute | solution.py:352
  10.6 1.4 %shard_map.124 = (bf16[3,4,4,96,128]{4,3,2,1,0:T(8,128)(2,1)S(1)}, bf16[384,128]{1,0:T(8,128)(2,1)S(1)}, f32[384,128]{1,0:T(8,128)S(1)}) custom-call(bf16[4,2,96,128]{3,2,1,0:T(8,128)(2,1)S(1)} %get-tuple-element.33.refs_0_, f32[8,128]{1,0:T(8,128)S(1)} %get-tuple-element.34.refs_1_.refs_2_, bf16[9,384,512]{2,1,0:T(8,128)(2,1)S(1)} %shard_map.123.refs_2_.weights, ...), custom_call_target="tpu_custom_call" | custom-call | flops 679477248 | bytes 5427200 | tf_op jit(solution)/shard_map/pallas_call | solution.py:29
  12.0 1.1 %shard_map.125 = (bf16[3,2,4,96,128]{4,3,2,1,0:T(8,128)(2,1)S(1)}, bf16[384,128]{1,0:T(8,128)(2,1)S(1)}, f32[384,128]{1,0:T(8,128)S(1)}) custom-call(bf16[2,2,96,128]{3,2,1,0:T(8,128)(2,1)S(1)} %get-tuple-element.32.cache, bf16[3,4,4,96,128]{4,3,2,1,0:T(8,128)(2,1)S(1)} %get-tuple-element.38.after, bf16[9,384,512]{2,1,0:T(8,128)(2,1)S(1)} %shard_map.123.refs_2_.weights, ...), custom_call_target="tpu_custom_call" | custom-call | flops 679477248 | bytes 5898240 | tf_op jit(solution)/shard_map/pallas_call | solution.py:29
  13.2 1.8 %collective-permute-start.6 = (bf16[384,128]{1,0:T(8,128)(2,1)S(1)}, bf16[384,128]{1,0:T(8,128)(2,1)S(1)}, u32[]{:S(2)}, u32[]{:S(2)}) collective-permute-start(bf16[384,128]{1,0:T(8,128)(2,1)S(1)} %get-tuple-element.45), channel_id=1, source_target_pairs={{0,1},{1,0},{2,3},{3,2},{4,5},{5,4},{6,7},{7,6},{8,9},{9,8},{10,11... | collective-permute-start | bytes 294920 | tf_op jit(solution)/shard_map/ppermute | solution.py:352
  15.3 2.0 %shard_map.126 = (bf16[768,128]{1,0:T(8,128)(2,1)S(1)}, f32[768,128]{1,0:T(8,128)S(1)}) custom-call(bf16[3,2,4,96,128]{4,3,2,1,0:T(8,128)(2,1)S(1)} %get-tuple-element.41.before, bf16[3,4,4,96,128]{4,3,2,1,0:T(8,128)(2,1)S(1)} %get-tuple-element.38.after, bf16[9,384,512]{2,1,0:T(8,128)(2,1)S(1)} %shard_map.123.refs_2_.weights), custom_call_target="tpu_custom_call" | custom-call | flops 1358954496 | bytes 5898240 | tf_op jit(solution)/shard_map/pallas_call | solution.py:29
  17.3 1.8 %collective-permute-start.5 = (bf16[768,128]{1,0:T(8,128)(2,1)S(1)}, bf16[768,128]{1,0:T(8,128)(2,1)S(1)}, u32[]{:S(2)}, u32[]{:S(2)}) collective-permute-start(bf16[768,128]{1,0:T(8,128)(2,1)S(1)} %get-tuple-element.43), channel_id=1, source_target_pairs={{0,1},{1,0},{2,3},{3,2},{4,5},{5,4},{6,7},{7,6},{8,9},{9,8},{10,11... | collective-permute-start | bytes 589832 | tf_op jit(solution)/shard_map/ppermute | solution.py:352
  19.1 1.6 %collective-permute-done.7 = bf16[384,128]{1,0:T(8,128)(2,1)S(1)} collective-permute-done((bf16[384,128]{1,0:T(8,128)(2,1)S(1)}, bf16[384,128]{1,0:T(8,128)(2,1)S(1)}, u32[]{:S(2)}, u32[]{:S(2)}) %collective-permute-start.7) | collective-permute-done | bytes 98336 | tf_op jit(solution)/shard_map/ppermute | solution.py:352
  20.8 2.7 %collective-permute-start.8 = (bf16[768,128]{1,0:T(8,128)(2,1)S(1)}, bf16[768,128]{1,0:T(8,128)(2,1)S(1)}, u32[]{:S(2)}, u32[]{:S(2)}) collective-permute-start(bf16[768,128]{1,0:T(8,128)(2,1)S(1)} %pad_maximum_fusion), channel_id=1, source_target_pairs={{0,2},{1,3},{2,0},{3,1},{4,6},{5,7},{6,4},{7,5},{8,10},{9,11},{10,... | collective-permute-start | bytes 589832 | tf_op jit(solution)/shard_map/ppermute | solution.py:352
  23.5 3.7 %collective-permute-done.5.refs_0_ = bf16[768,128]{1,0:T(8,128)(2,1)S(1)} collective-permute-done((bf16[768,128]{1,0:T(8,128)(2,1)S(1)}, bf16[768,128]{1,0:T(8,128)(2,1)S(1)}, u32[]{:S(2)}, u32[]{:S(2)}) %collective-permute-start.5) | collective-permute-done | bytes 196640 | tf_op jit(solution)/shard_map/ppermute | solution.py:352
  27.2 4.3 %collective-permute-done.8.refs_1_ = bf16[768,128]{1,0:T(8,128)(2,1)S(1)} collective-permute-done((bf16[768,128]{1,0:T(8,128)(2,1)S(1)}, bf16[768,128]{1,0:T(8,128)(2,1)S(1)}, u32[]{:S(2)}, u32[]{:S(2)}) %collective-permute-start.8) | collective-permute-done | bytes 196640 | tf_op jit(solution)/shard_map/ppermute | solution.py:352
  31.8 1.6 %collective-permute-start.9 = (bf16[400,128]{1,0:T(8,128)(2,1)S(1)}, bf16[400,128]{1,0:T(8,128)(2,1)S(1)}, u32[]{:S(2)}, u32[]{:S(2)}) collective-permute-start(bf16[400,128]{1,0:T(8,128)(2,1)S(1)} %get-tuple-element.49), channel_id=1, source_target_pairs={{0,4},{4,0},{8,12},{12,8},{1,5},{5,1},{9,13},{13,9},{2,6},{6,2},{1... | collective-permute-start | bytes 307208 | tf_op jit(solution)/shard_map/ppermute | solution.py:352
  33.9 3.1 %collective-permute-done.11.refs_6_ = bf16[16,128]{1,0:T(8,128)(2,1)S(1)} collective-permute-done((bf16[16,128]{1,0:T(8,128)(2,1)S(1)}, bf16[16,128]{1,0:T(8,128)(2,1)S(1)}, u32[]{:S(2)}, u32[]{:S(2)}) %collective-permute-start.11) | collective-permute-done | bytes 4128 | tf_op jit(solution)/shard_map/ppermute | solution.py:352
  37.0 1.3 %shard_map.128 = (bf16[3,4,4,96,128]{4,3,2,1,0:T(8,128)(2,1)S(1)}, bf16[384,128]{1,0:T(8,128)(2,1)S(1)}, f32[384,128]{1,0:T(8,128)S(1)}) custom-call(bf16[4,2,96,128]{3,2,1,0:T(8,128)(2,1)S(1)} %get-tuple-element.48.refs_0_, f32[8,128]{1,0:T(8,128)S(1)} %get-tuple-element.34.refs_1_.refs_2_, bf16[9,384,512]{2,1,0:T(8,128)(2,1)S(1)} %bitcast.13, ...), custom_call_target="tpu_custom_call" | custom-call | flops 679477248 | bytes 5427200 | tf_op jit(solution)/shard_map/pallas_call | solution.py:29
  39.6 2.0 %collective-permute-start.14 = (bf16[384,128]{1,0:T(8,128)(2,1)S(1)}, bf16[384,128]{1,0:T(8,128)(2,1)S(1)}, u32[]{:S(2)}, u32[]{:S(2)}) collective-permute-start(bf16[384,128]{1,0:T(8,128)(2,1)S(1)} %get-tuple-element.59), channel_id=1, source_target_pairs={{0,1},{1,0},{2,3},{3,2},{4,5},{5,4},{6,7},{7,6},{8,9},{9,8},{10,11... | collective-permute-start | bytes 294920 | tf_op jit(solution)/shard_map/ppermute | solution.py:352
  41.6 2.0 %shard_map.130 = (bf16[768,128]{1,0:T(8,128)(2,1)S(1)}, f32[768,128]{1,0:T(8,128)S(1)}) custom-call(bf16[3,2,4,96,128]{4,3,2,1,0:T(8,128)(2,1)S(1)} %get-tuple-element.53.before, bf16[3,4,4,96,128]{4,3,2,1,0:T(8,128)(2,1)S(1)} %get-tuple-element.52.after, bf16[9,384,512]{2,1,0:T(8,128)(2,1)S(1)} %bitcast.15), custom_call_target="tpu_custom_call" | custom-call | flops 1358954496 | bytes 5898240 | tf_op jit(solution)/shard_map/pallas_call | solution.py:29
  43.8 1.5 %collective-permute-done.13 = bf16[384,128]{1,0:T(8,128)(2,1)S(1)} collective-permute-done((bf16[384,128]{1,0:T(8,128)(2,1)S(1)}, bf16[384,128]{1,0:T(8,128)(2,1)S(1)}, u32[]{:S(2)}, u32[]{:S(2)}) %collective-permute-start.13) | collective-permute-done | bytes 98336 | tf_op jit(solution)/shard_map/ppermute | solution.py:352
  45.3 1.8 %collective-permute-done.14 = bf16[384,128]{1,0:T(8,128)(2,1)S(1)} collective-permute-done((bf16[384,128]{1,0:T(8,128)(2,1)S(1)}, bf16[384,128]{1,0:T(8,128)(2,1)S(1)}, u32[]{:S(2)}, u32[]{:S(2)}) %collective-permute-start.14) | collective-permute-done | bytes 98336 | tf_op jit(solution)/shard_map/ppermute | solution.py:352
  47.1 1.2 %collective-permute-start.15 = (bf16[768,128]{1,0:T(8,128)(2,1)S(1)}, bf16[768,128]{1,0:T(8,128)(2,1)S(1)}, u32[]{:S(2)}, u32[]{:S(2)}) collective-permute-start(bf16[768,128]{1,0:T(8,128)(2,1)S(1)} %pad_maximum_fusion.1), channel_id=1, source_target_pairs={{0,2},{1,3},{2,0},{3,1},{4,6},{5,7},{6,4},{7,5},{8,10},{9,11},{10,... | collective-permute-start | bytes 589832 | tf_op jit(solution)/shard_map/ppermute | solution.py:352
  49.0 3.9 %collective-permute-done.12.refs_0_ = bf16[768,128]{1,0:T(8,128)(2,1)S(1)} collective-permute-done((bf16[768,128]{1,0:T(8,128)(2,1)S(1)}, bf16[768,128]{1,0:T(8,128)(2,1)S(1)}, u32[]{:S(2)}, u32[]{:S(2)}) %collective-permute-start.12) | collective-permute-done | bytes 196640 | tf_op jit(solution)/shard_map/ppermute | solution.py:352
  52.8 4.8 %collective-permute-done.15.refs_1_ = bf16[768,128]{1,0:T(8,128)(2,1)S(1)} collective-permute-done((bf16[768,128]{1,0:T(8,128)(2,1)S(1)}, bf16[768,128]{1,0:T(8,128)(2,1)S(1)}, u32[]{:S(2)}, u32[]{:S(2)}) %collective-permute-start.15) | collective-permute-done | bytes 196640 | tf_op jit(solution)/shard_map/ppermute | solution.py:352
  (27 shorter events, 4.7 us)
Async XLA Ops:
  1.8 8.8 %collective-permute-start = (bf16[400,128]{1,0:T(8,128)(2,1)S(1)}, bf16[400,128]{1,0:T(8,128)(2,1)S(1)}, u32[]{:S(2)}, u32[]{:S(2)}) collective-permute-start(bf16[400,128]{1,0:T(8,128)(2,1)S(1)} %get-tuple-element.35), channel_id=1, source_target_pairs={{0,4},{4,0},{8,12},{12,8},{1,5},{5,1},{9,13},{13,9},{2,6},{6,2},{1... | collective-permute-start | bytes 307208 | tf_op jit(solution)/shard_map/ppermute | solution.py:352
  2.4 8.3 %collective-permute-start.1 = (bf16[400,128]{1,0:T(8,128)(2,1)S(1)}, bf16[400,128]{1,0:T(8,128)(2,1)S(1)}, u32[]{:S(2)}, u32[]{:S(2)}) collective-permute-start(bf16[400,128]{1,0:T(8,128)(2,1)S(1)} %get-tuple-element.36), channel_id=1, source_target_pairs={{0,12},{4,8},{8,4},{12,0},{1,13},{5,9},{9,5},{13,1},{2,14},{6,10},... | collective-permute-start | bytes 307208 | tf_op jit(solution)/shard_map/ppermute | solution.py:380
  5.0 7.0 %collective-permute-start.3 = (bf16[384,128]{1,0:T(8,128)(2,1)S(1)}, bf16[384,128]{1,0:T(8,128)(2,1)S(1)}, u32[]{:S(2)}, u32[]{:S(2)}) collective-permute-start(bf16[384,128]{1,0:T(8,128)(2,1)S(1)} %get-tuple-element.39), channel_id=1, source_target_pairs={{0,4},{4,0},{8,12},{12,8},{1,5},{5,1},{9,13},{13,9},{2,6},{6,2},{1... | collective-permute-start | bytes 294920 | tf_op jit(solution)/shard_map/ppermute | solution.py:352
  5.1 6.9 %collective-permute-start.4 = (bf16[384,128]{1,0:T(8,128)(2,1)S(1)}, bf16[384,128]{1,0:T(8,128)(2,1)S(1)}, u32[]{:S(2)}, u32[]{:S(2)}) collective-permute-start(bf16[384,128]{1,0:T(8,128)(2,1)S(1)} %get-tuple-element.40), channel_id=1, source_target_pairs={{0,12},{4,8},{8,4},{12,0},{1,13},{5,9},{9,5},{13,1},{2,14},{6,10},... | collective-permute-start | bytes 294920 | tf_op jit(solution)/shard_map/ppermute | solution.py:380
  5.1 5.5 %collective-permute-start.2 = (bf16[16,128]{1,0:T(8,128)(2,1)S(1)}, bf16[16,128]{1,0:T(8,128)(2,1)S(1)}, u32[]{:S(2)}, u32[]{:S(2)}) collective-permute-start(bf16[16,128]{1,0:T(8,128)(2,1)S(1)} %get-tuple-element.37.refs_5_), channel_id=1, source_target_pairs={{0,8},{4,12},{8,0},{12,4},{1,9},{5,13},{9,1},{13,5},{2,10},{6,14},... | collective-permute-start | bytes 12296 | tf_op jit(solution)/shard_map/ppermute | solution.py:352
  13.2 5.9 %collective-permute-start.6 = (bf16[384,128]{1,0:T(8,128)(2,1)S(1)}, bf16[384,128]{1,0:T(8,128)(2,1)S(1)}, u32[]{:S(2)}, u32[]{:S(2)}) collective-permute-start(bf16[384,128]{1,0:T(8,128)(2,1)S(1)} %get-tuple-element.45), channel_id=1, source_target_pairs={{0,1},{1,0},{2,3},{3,2},{4,5},{5,4},{6,7},{7,6},{8,9},{9,8},{10,11... | collective-permute-start | bytes 294920 | tf_op jit(solution)/shard_map/ppermute | solution.py:352
  15.0 5.8 %collective-permute-start.7 = (bf16[384,128]{1,0:T(8,128)(2,1)S(1)}, bf16[384,128]{1,0:T(8,128)(2,1)S(1)}, u32[]{:S(2)}, u32[]{:S(2)}) collective-permute-start(bf16[384,128]{1,0:T(8,128)(2,1)S(1)} %get-tuple-element.47), channel_id=1, source_target_pairs={{0,1},{1,0},{2,3},{3,2},{4,5},{5,4},{6,7},{7,6},{8,9},{9,8},{10,11... | collective-permute-start | bytes 294920 | tf_op jit(solution)/shard_map/ppermute | solution.py:352
  15.3 21.8 %copy-start = (bf16[3,3,3,128,512]{4,3,2,1,0:T(8,128)(2,1)S(1)}, bf16[3,3,3,128,512]{4,3,2,1,0:T(8,128)(2,1)}, u32[]{:S(2)}) copy-start(bf16[3,3,3,128,512]{4,3,2,1,0:T(8,128)(2,1)} %param.20) | copy-start | bytes 10616836
  17.3 9.9 %collective-permute-start.5 = (bf16[768,128]{1,0:T(8,128)(2,1)S(1)}, bf16[768,128]{1,0:T(8,128)(2,1)S(1)}, u32[]{:S(2)}, u32[]{:S(2)}) collective-permute-start(bf16[768,128]{1,0:T(8,128)(2,1)S(1)} %get-tuple-element.43), channel_id=1, source_target_pairs={{0,1},{1,0},{2,3},{3,2},{4,5},{5,4},{6,7},{7,6},{8,9},{9,8},{10,11... | collective-permute-start | bytes 589832 | tf_op jit(solution)/shard_map/ppermute | solution.py:352
  20.8 10.6 %collective-permute-start.8 = (bf16[768,128]{1,0:T(8,128)(2,1)S(1)}, bf16[768,128]{1,0:T(8,128)(2,1)S(1)}, u32[]{:S(2)}, u32[]{:S(2)}) collective-permute-start(bf16[768,128]{1,0:T(8,128)(2,1)S(1)} %pad_maximum_fusion), channel_id=1, source_target_pairs={{0,2},{1,3},{2,0},{3,1},{4,6},{5,7},{6,4},{7,5},{8,10},{9,11},{10,... | collective-permute-start | bytes 589832 | tf_op jit(solution)/shard_map/ppermute | solution.py:352
  31.7 5.3 %collective-permute-start.10 = (bf16[400,128]{1,0:T(8,128)(2,1)S(1)}, bf16[400,128]{1,0:T(8,128)(2,1)S(1)}, u32[]{:S(2)}, u32[]{:S(2)}) collective-permute-start(bf16[400,128]{1,0:T(8,128)(2,1)S(1)} %get-tuple-element.50), channel_id=1, source_target_pairs={{0,12},{4,8},{8,4},{12,0},{1,13},{5,9},{9,5},{13,1},{2,14},{6,10},... | collective-permute-start | bytes 307208 | tf_op jit(solution)/shard_map/ppermute | solution.py:380
  31.8 5.3 %collective-permute-start.9 = (bf16[400,128]{1,0:T(8,128)(2,1)S(1)}, bf16[400,128]{1,0:T(8,128)(2,1)S(1)}, u32[]{:S(2)}, u32[]{:S(2)}) collective-permute-start(bf16[400,128]{1,0:T(8,128)(2,1)S(1)} %get-tuple-element.49), channel_id=1, source_target_pairs={{0,4},{4,0},{8,12},{12,8},{1,5},{5,1},{9,13},{13,9},{2,6},{6,2},{1... | collective-permute-start | bytes 307208 | tf_op jit(solution)/shard_map/ppermute | solution.py:352
  33.4 3.7 %collective-permute-start.11 = (bf16[16,128]{1,0:T(8,128)(2,1)S(1)}, bf16[16,128]{1,0:T(8,128)(2,1)S(1)}, u32[]{:S(2)}, u32[]{:S(2)}) collective-permute-start(bf16[16,128]{1,0:T(8,128)(2,1)S(1)} %get-tuple-element.51.refs_5_), channel_id=1, source_target_pairs={{0,8},{4,12},{8,0},{12,4},{1,9},{5,13},{9,1},{13,5},{2,10},{6,14},... | collective-permute-start | bytes 12296 | tf_op jit(solution)/shard_map/ppermute | solution.py:352
  39.5 5.7 %collective-permute-start.13 = (bf16[384,128]{1,0:T(8,128)(2,1)S(1)}, bf16[384,128]{1,0:T(8,128)(2,1)S(1)}, u32[]{:S(2)}, u32[]{:S(2)}) collective-permute-start(bf16[384,128]{1,0:T(8,128)(2,1)S(1)} %get-tuple-element.57), channel_id=1, source_target_pairs={{0,1},{1,0},{2,3},{3,2},{4,5},{5,4},{6,7},{7,6},{8,9},{9,8},{10,11... | collective-permute-start | bytes 294920 | tf_op jit(solution)/shard_map/ppermute | solution.py:352
  39.6 7.5 %collective-permute-start.14 = (bf16[384,128]{1,0:T(8,128)(2,1)S(1)}, bf16[384,128]{1,0:T(8,128)(2,1)S(1)}, u32[]{:S(2)}, u32[]{:S(2)}) collective-permute-start(bf16[384,128]{1,0:T(8,128)(2,1)S(1)} %get-tuple-element.59), channel_id=1, source_target_pairs={{0,1},{1,0},{2,3},{3,2},{4,5},{5,4},{6,7},{7,6},{8,9},{9,8},{10,11... | collective-permute-start | bytes 294920 | tf_op jit(solution)/shard_map/ppermute | solution.py:352
  43.6 9.2 %collective-permute-start.12 = (bf16[768,128]{1,0:T(8,128)(2,1)S(1)}, bf16[768,128]{1,0:T(8,128)(2,1)S(1)}, u32[]{:S(2)}, u32[]{:S(2)}) collective-permute-start(bf16[768,128]{1,0:T(8,128)(2,1)S(1)} %get-tuple-element.55), channel_id=1, source_target_pairs={{0,1},{1,0},{2,3},{3,2},{4,5},{5,4},{6,7},{7,6},{8,9},{9,8},{10,11... | collective-permute-start | bytes 589832 | tf_op jit(solution)/shard_map/ppermute | solution.py:352
  47.1 10.5 %collective-permute-start.15 = (bf16[768,128]{1,0:T(8,128)(2,1)S(1)}, bf16[768,128]{1,0:T(8,128)(2,1)S(1)}, u32[]{:S(2)}, u32[]{:S(2)}) collective-permute-start(bf16[768,128]{1,0:T(8,128)(2,1)S(1)} %pad_maximum_fusion.1), channel_id=1, source_target_pairs={{0,2},{1,3},{2,0},{3,1},{4,6},{5,7},{6,4},{7,5},{8,10},{9,11},{10,... | collective-permute-start | bytes 589832 | tf_op jit(solution)/shard_map/ppermute | solution.py:352

commit v4 on v3

--- a/solution.py
+++ b/solution.py
@@ -137,52 +137,47 @@
     )[0]
 
 
-def total_of(own, terms, bias):
-    value = own[...]
-    for group in terms:
-        pieces = [piece[...].astype(jnp.float32) for piece in group]
-        value = value + (pieces[0] if len(pieces) == 1 else jnp.concatenate(pieces, axis=0))
-    return (value + bias).astype(jnp.bfloat16)
-
-
-def regroup(refs, counts):
-    groups, start = [], 0
-    for count in counts:
-        groups.append(refs[start : start + count])
-        start += count
-    return groups, refs[start:]
-
-
-def middle_body(row, counts, own, *refs):
-    terms, (table, hidden, tile, pair, other) = regroup(refs, counts)
-    rounded = total_of(own, terms, table[row : row + 1])
+def total_of(own, terms, starts, bias):
+    ends = [start + term.shape[0] for term, start in zip(terms, starts)]
+    cuts = sorted({0, own.shape[0], *starts, *ends})
+    pieces = []
+    for low, high in zip(cuts, cuts[1:]):
+        value = own[low:high]
+        for term, start, end in zip(terms, starts, ends):
+            if start <= low and high <= end:
+                value = value + term[low - start : high - start].astype(jnp.float32)
+        pieces.append(value)
+    return (jnp.concatenate(pieces, axis=0) + bias).astype(jnp.bfloat16)
+
+
+def middle_body(row, starts, own, *refs):
+    terms, (table, hidden, tile, pair, other) = refs[: len(starts)], refs[len(starts) :]
+    rounded = total_of(own, terms, starts, table[row : row + 1])
     store_moments(tile, (pair, other), moments_of(rounded.astype(jnp.float32)))
     hidden[...] = rounded.reshape(hidden.shape)
     store_edges((hidden,), pair, other)
 
 
-def middle(own, terms, table, row, shape):
+def middle(own, terms, starts, table, row, shape):
     frames, _, width, channels = shape
     outs = [
         jax.ShapeDtypeStruct(shape, jnp.bfloat16),
         moments_tile(channels),
         *message_shapes(frames, width, channels, PACKED),
     ]
-    body = functools.partial(middle_body, row, [len(group) for group in terms])
-    args = (own, *[piece for group in terms for piece in group], table)
-    return call(body, outs, args)
-
-
-def close_body(row, counts, own, *refs):
-    terms, (table, out) = regroup(refs, counts)
-    out[...] = total_of(own, terms, table[row : row + 1]).reshape(out.shape)
-
-
-def close(own, terms, table, row, shape):
+    body = functools.partial(middle_body, row, starts)
+    return call(body, outs, (own, *terms, table))
+
+
+def close_body(row, starts, own, *refs):
+    terms, (table, out) = refs[: len(starts)], refs[len(starts) :]
+    out[...] = total_of(own, terms, starts, table[row : row + 1]).reshape(out.shape)
+
+
+def close(own, terms, starts, table, row, shape):
     outs = [jax.ShapeDtypeStruct(shape, jnp.bfloat16)]
-    body = functools.partial(close_body, row, [len(group) for group in terms])
-    args = (own, *[piece for group in terms for piece in group], table)
-    return call(body, outs, args)[0]
+    body = functools.partial(close_body, row, starts)
+    return call(body, outs, (own, *terms, table))[0]
 
 
 def products(parts, weights, first, count, blocks, outs):
@@ -318,9 +313,9 @@
     lead = 2 if split else blocks
     work = 2 * rows * width * 9 * weights.shape[1] * channels
 
-    def led(count):
+    def led(count, near=jnp.bfloat16):
         cells = count * rows * width
-        types = [jnp.bfloat16, jnp.float32] if split else [jnp.bfloat16] * blocks
+        types = [jnp.bfloat16, near] if split else [jnp.bfloat16] * blocks
         return [jax.ShapeDtypeStruct((cells, channels), kind) for kind in types]
 
     def padded(count):
@@ -332,7 +327,7 @@
         flops=work * (frames - history) * lead,
     )
     before, *two = call(
-        functools.partial(second_body, offset), [padded(history), *led(history)],
+        functools.partial(second_body, offset), [padded(history), *led(history, jnp.float32)],
         (cache, after, weights, *old_messages), flops=work * history * lead,
     )
 
@@ -362,16 +357,19 @@
         for step in range(1, count):
             block = lax.dynamic_index_in_dim(stacked, (mine + step) % count, 0, keepdims=False)
             pairs = [(i, (i + step) % count) for i in range(count)]
-            terms.append([lax.ppermute(block, "chan", pairs)])
-        return own, terms
-    joined = []
-    for far, near in (one, two):
-        arrived = swap(far, "chan", 1)
-        joined.append((near + arrived.astype(jnp.float32)).astype(jnp.bfloat16))
+            terms.append(lax.ppermute(block, "chan", pairs))
+        return own, terms, [0] * len(terms)
+    direct = []
+    for step, block in zip((3, 2), one):
+        direct.append(swap(block, "chan", step))
+    far, near = two
+    arrived = swap(far, "chan", 1)
+    joined = (near + arrived.astype(jnp.float32)).astype(jnp.bfloat16)
     block, own = rest()
     beside = swap(block, "chan", 1)
-    across = swap(jnp.concatenate(joined[::-1], axis=0), "chan", 2)
-    return own, [[beside], [across]]
+    across = swap(joined, "chan", 2)
+    start = across.shape[0]
+    return own, [beside, across, *direct], [0, 0, start, start]
 
 
 def to_neighbours(pair, other):
@@ -429,17 +427,17 @@
     *parts, _ = conv(
         x, messages, tiles, first, old_messages, 0, table, 0, weights, entries
     )
-    own, terms = reduce_terms(*parts)
-    hidden, tile, pair, other = middle(own, terms, table, 2, x.shape)
+    own, terms, starts = reduce_terms(*parts)
+    hidden, tile, pair, other = middle(own, terms, starts, table, 2, x.shape)
     tiles = over_rows(tile)
     messages = to_neighbours(pair, other)
     weights = taps(kernel_second)
     *parts, kept = conv(
         hidden, messages, tiles, second, old_messages, first.shape[0], table, 3, weights, entries
     )
-    own, terms = reduce_terms(*parts)
+    own, terms, starts = reduce_terms(*parts)
     kept = kept()
-    decoded = close(own, terms, table, 5, x.shape)
+    decoded = close(own, terms, starts, table, 5, x.shape)
     return decoded.transpose(outward), kept.transpose(outward)
 
 

time: 58.5 us -> 61.6 us (1.053)
  starting transfers between devices: 17.5 us -> 22.9 us
  waiting for transfers between devices: 26.1 us -> 23.9 us
    ppermute x13 -> x15, starting transfers between devices: 14.8 us -> 18.7 us  [swap(): lax.ppermute(value, axis, [(i, i ^ step) for i in range(lax.axis_size(axi...]
    ppermute x13 -> x15, waiting for transfers between devices: 26.1 us -> 23.9 us  [swap(): lax.ppermute(value, axis, [(i, i ^ step) for i in range(lax.axis_size(axi...]
    ppermute x3, starting transfers between devices: 2.76 us -> 4.26 us  [to_neighbours(): across = lax.ppermute(other, 'rows', ring)]
  transfers between devices with their start and end apart: 16 -> 18, of which waited for: 9 -> 8; matrix products, arithmetic and copies ran while one was open for 0% -> 0% of each run, Pallas kernels for 14% -> 13%
where the time goes in v4:
time: 61.6 us; the launch traced here: 61.5 us
  waiting for transfers between devices  23.9 us (39%)
  starting transfers between devices  22.9 us (37%)
  Pallas kernels  13.8 us (22%)
  between operations  0.77 us (1%)
    ppermute x15, waiting for transfers between devices, swap(): lax.ppermute(value, axis, [(i, i ^ step) for i in range(lax.axis_size(axi...  23.9 us
    ppermute x15, starting transfers between devices, swap(): lax.ppermute(value, axis, [(i, i ^ step) for i in range(lax.axis_size(axi...  18.7 us
    pallas_call x11, Pallas kernels, call(): pl.pallas_call(body, out_shape=outs, in_specs=specs or [on_chip()] * len(...  13.8 us
    ppermute x3, starting transfers between devices, to_neighbours(): across = lax.ppermute(other, 'rows', ring)  4.26 us
  transfers between devices with their start and end apart: 18, of which 8 were waited for; matrix products, arithmetic and copies ran while one was open for 0% of the time, Pallas kernels for 13%

profile of v4, /device:TPU:0, one launch (start us, length us, event | category | flops | bytes accessed | tf_op | source)
XLA Modules:
  0.0 61.5 jit_solution(7296314875387635527)
XLA Ops:
  0.6 1.2 %shard_map.122 = (bf16[4,2,96,128]{3,2,1,0:T(8,128)(2,1)S(1)}, bf16[2,2,96,128]{3,2,1,0:T(8,128)(2,1)S(1)}, bf16[2,2,96,128]{3,2,1,0:T(8,128)(2,1)S(1)}, f32[8,1...) custom-call(bf16[4,2,96,128]{3,2,1,0:T(8,128)(2,1)} %bitcast.17, ...), custom_call_target="tpu_custom_call" | custom-call | bytes 1199104 | tf_op jit(solution)/shard_map/pallas_call | solution.py:29
  2.4 2.6 %collective-permute-start.1 = (bf16[400,128]{1,0:T(8,128)(2,1)S(1)}, bf16[400,128]{1,0:T(8,128)(2,1)S(1)}, u32[]{:S(2)}, u32[]{:S(2)}) collective-permute-start(bf16[400,128]{1,0:T(8,128)(2,1)S(1)} %get-tuple-element.36), channel_id=1, source_target_pairs={{0,12},{4,8},{8,4},{12,0},{1,13},{5,9},{9,5},{13,1},{2,14},{6,10},... | collective-permute-start | bytes 307208 | tf_op jit(solution)/shard_map/ppermute | solution.py:378
  5.1 2.0 %collective-permute-start.2 = (bf16[16,128]{1,0:T(8,128)(2,1)S(1)}, bf16[16,128]{1,0:T(8,128)(2,1)S(1)}, u32[]{:S(2)}, u32[]{:S(2)}) collective-permute-start(bf16[16,128]{1,0:T(8,128)(2,1)S(1)} %get-tuple-element.37.refs_5_), channel_id=1, source_target_pairs={{0,8},{4,12},{8,0},{12,4},{1,9},{5,13},{9,1},{13,5},{2,10},{6,14},... | collective-permute-start | bytes 12296 | tf_op jit(solution)/shard_map/ppermute | solution.py:347
  7.1 2.0 %shard_map.123.refs_2_.weights = bf16[9,384,512]{2,1,0:T(8,128)(2,1)S(1)} custom-call(bf16[9,384,512]{2,1,0:T(8,128)(2,1)} %bitcast.16), custom_call_target="tpu_custom_call" | custom-call | bytes 7077888 | tf_op jit(solution)/shard_map/pallas_call | solution.py:29
  9.2 1.5 %collective-permute-done.2.refs_6_ = bf16[16,128]{1,0:T(8,128)(2,1)S(1)} collective-permute-done((bf16[16,128]{1,0:T(8,128)(2,1)S(1)}, bf16[16,128]{1,0:T(8,128)(2,1)S(1)}, u32[]{:S(2)}, u32[]{:S(2)}) %collective-permute-start.2) | collective-permute-done | bytes 4128 | tf_op jit(solution)/shard_map/ppermute | solution.py:347
  10.6 1.4 %shard_map.124 = (bf16[3,4,4,96,128]{4,3,2,1,0:T(8,128)(2,1)S(1)}, bf16[384,128]{1,0:T(8,128)(2,1)S(1)}, bf16[384,128]{1,0:T(8,128)(2,1)S(1)}) custom-call(bf16[4,2,96,128]{3,2,1,0:T(8,128)(2,1)S(1)} %get-tuple-element.33.refs_0_, f32[8,128]{1,0:T(8,128)S(1)} %get-tuple-element.34.refs_1_.refs_4_, bf16[9,384,512]{2,1,0:T(8,128)(2,1)S(1)} %shard_map.123.refs_2_.weights, ...), custom_call_target="tpu_custom_call" | custom-call | flops 679477248 | bytes 5328896 | tf_op jit(solution)/shard_map/pallas_call | solution.py:29
  12.0 1.2 %shard_map.125 = (bf16[3,2,4,96,128]{4,3,2,1,0:T(8,128)(2,1)S(1)}, bf16[384,128]{1,0:T(8,128)(2,1)S(1)}, f32[384,128]{1,0:T(8,128)S(1)}) custom-call(bf16[2,2,96,128]{3,2,1,0:T(8,128)(2,1)S(1)} %get-tuple-element.32.cache, bf16[3,4,4,96,128]{4,3,2,1,0:T(8,128)(2,1)S(1)} %get-tuple-element.38.after, bf16[9,384,512]{2,1,0:T(8,128)(2,1)S(1)} %shard_map.123.refs_2_.weights, ...), custom_call_target="tpu_custom_call" | custom-call | flops 679477248 | bytes 5898240 | tf_op jit(solution)/shard_map/pallas_call | solution.py:29
  13.2 1.8 %collective-permute-start.6 = (bf16[384,128]{1,0:T(8,128)(2,1)S(1)}, bf16[384,128]{1,0:T(8,128)(2,1)S(1)}, u32[]{:S(2)}, u32[]{:S(2)}) collective-permute-start(bf16[384,128]{1,0:T(8,128)(2,1)S(1)} %get-tuple-element.45), channel_id=1, source_target_pairs={{0,1},{1,0},{2,3},{3,2},{4,5},{5,4},{6,7},{7,6},{8,9},{9,8},{10,11... | collective-permute-start | bytes 294920 | tf_op jit(solution)/shard_map/ppermute | solution.py:347
  15.0 2.0 %shard_map.126 = (bf16[768,128]{1,0:T(8,128)(2,1)S(1)}, f32[768,128]{1,0:T(8,128)S(1)}) custom-call(bf16[3,2,4,96,128]{4,3,2,1,0:T(8,128)(2,1)S(1)} %get-tuple-element.41.before, bf16[3,4,4,96,128]{4,3,2,1,0:T(8,128)(2,1)S(1)} %get-tuple-element.38.after, bf16[9,384,512]{2,1,0:T(8,128)(2,1)S(1)} %shard_map.123.refs_2_.weights), custom_call_target="tpu_custom_call" | custom-call | flops 1358954496 | bytes 5898240 | tf_op jit(solution)/shard_map/pallas_call | solution.py:29
  17.3 3.7 %collective-permute-start.8 = (bf16[384,128]{1,0:T(8,128)(2,1)S(1)}, bf16[384,128]{1,0:T(8,128)(2,1)S(1)}, u32[]{:S(2)}, u32[]{:S(2)}) collective-permute-start(bf16[384,128]{1,0:T(8,128)(2,1)S(1)} %get-tuple-element.46), channel_id=1, source_target_pairs={{0,3},{1,2},{2,1},{3,0},{4,7},{5,6},{6,5},{7,4},{8,11},{9,10},{10,... | collective-permute-start | bytes 294920 | tf_op jit(solution)/shard_map/ppermute | solution.py:347
  21.1 3.0 %collective-permute-start.7 = (bf16[384,128]{1,0:T(8,128)(2,1)S(1)}, bf16[384,128]{1,0:T(8,128)(2,1)S(1)}, u32[]{:S(2)}, u32[]{:S(2)}) collective-permute-start(bf16[384,128]{1,0:T(8,128)(2,1)S(1)} %add_convert_fusion.1), channel_id=1, source_target_pairs={{0,2},{1,3},{2,0},{3,1},{4,6},{5,7},{6,4},{7,5},{8,10},{9,11},{10,... | collective-permute-start | bytes 294920 | tf_op jit(solution)/shard_map/ppermute | solution.py:347
  24.1 4.9 %collective-permute-done.8.refs_2_ = bf16[384,128]{1,0:T(8,128)(2,1)S(1)} collective-permute-done((bf16[384,128]{1,0:T(8,128)(2,1)S(1)}, bf16[384,128]{1,0:T(8,128)(2,1)S(1)}, u32[]{:S(2)}, u32[]{:S(2)}) %collective-permute-start.8) | collective-permute-done | bytes 98336 | tf_op jit(solution)/shard_map/ppermute | solution.py:347
  29.0 3.7 %collective-permute-done.9.refs_3_ = bf16[384,128]{1,0:T(8,128)(2,1)S(1)} collective-permute-done((bf16[384,128]{1,0:T(8,128)(2,1)S(1)}, bf16[384,128]{1,0:T(8,128)(2,1)S(1)}, u32[]{:S(2)}, u32[]{:S(2)}) %collective-permute-start.9) | collective-permute-done | bytes 98336 | tf_op jit(solution)/shard_map/ppermute | solution.py:347
  34.1 1.6 %collective-permute-start.11 = (bf16[400,128]{1,0:T(8,128)(2,1)S(1)}, bf16[400,128]{1,0:T(8,128)(2,1)S(1)}, u32[]{:S(2)}, u32[]{:S(2)}) collective-permute-start(bf16[400,128]{1,0:T(8,128)(2,1)S(1)} %get-tuple-element.50), channel_id=1, source_target_pairs={{0,12},{4,8},{8,4},{12,0},{1,13},{5,9},{9,5},{13,1},{2,14},{6,10},... | collective-permute-start | bytes 307208 | tf_op jit(solution)/shard_map/ppermute | solution.py:378
  36.2 3.2 %collective-permute-done.12.refs_6_ = bf16[16,128]{1,0:T(8,128)(2,1)S(1)} collective-permute-done((bf16[16,128]{1,0:T(8,128)(2,1)S(1)}, bf16[16,128]{1,0:T(8,128)(2,1)S(1)}, u32[]{:S(2)}, u32[]{:S(2)}) %collective-permute-start.12) | collective-permute-done | bytes 4128 | tf_op jit(solution)/shard_map/ppermute | solution.py:347
  39.4 1.3 %shard_map.128 = (bf16[3,4,4,96,128]{4,3,2,1,0:T(8,128)(2,1)S(1)}, bf16[384,128]{1,0:T(8,128)(2,1)S(1)}, bf16[384,128]{1,0:T(8,128)(2,1)S(1)}) custom-call(bf16[4,2,96,128]{3,2,1,0:T(8,128)(2,1)S(1)} %get-tuple-element.48.refs_0_, f32[8,128]{1,0:T(8,128)S(1)} %get-tuple-element.34.refs_1_.refs_4_, bf16[9,384,512]{2,1,0:T(8,128)(2,1)S(1)} %bitcast.13, ...), custom_call_target="tpu_custom_call" | custom-call | flops 679477248 | bytes 5328896 | tf_op jit(solution)/shard_map/pallas_call | solution.py:29
  40.7 1.1 %shard_map.129 = (bf16[3,2,4,96,128]{4,3,2,1,0:T(8,128)(2,1)S(1)}, bf16[384,128]{1,0:T(8,128)(2,1)S(1)}, f32[384,128]{1,0:T(8,128)S(1)}) custom-call(bf16[2,2,96,128]{3,2,1,0:T(8,128)(2,1)S(1)} %get-tuple-element.31.cache, bf16[3,4,4,96,128]{4,3,2,1,0:T(8,128)(2,1)S(1)} %get-tuple-element.52.after, bf16[9,384,512]{2,1,0:T(8,128)(2,1)S(1)} %bitcast.14, ...), custom_call_target="tpu_custom_call" | custom-call | flops 679477248 | bytes 5898240 | tf_op jit(solution)/shard_map/pallas_call | solution.py:29
  42.0 2.0 %shard_map.130 = (bf16[768,128]{1,0:T(8,128)(2,1)S(1)}, f32[768,128]{1,0:T(8,128)S(1)}) custom-call(bf16[3,2,4,96,128]{4,3,2,1,0:T(8,128)(2,1)S(1)} %get-tuple-element.53.before, bf16[3,4,4,96,128]{4,3,2,1,0:T(8,128)(2,1)S(1)} %get-tuple-element.52.after, bf16[9,384,512]{2,1,0:T(8,128)(2,1)S(1)} %bitcast.15), custom_call_target="tpu_custom_call" | custom-call | flops 1358954496 | bytes 5898240 | tf_op jit(solution)/shard_map/pallas_call | solution.py:29
  44.0 2.1 %collective-permute-start.13 = (bf16[768,128]{1,0:T(8,128)(2,1)S(1)}, bf16[768,128]{1,0:T(8,128)(2,1)S(1)}, u32[]{:S(2)}, u32[]{:S(2)}) collective-permute-start(bf16[768,128]{1,0:T(8,128)(2,1)S(1)} %get-tuple-element.55), channel_id=1, source_target_pairs={{0,1},{1,0},{2,3},{3,2},{4,5},{5,4},{6,7},{7,6},{8,9},{9,8},{10,11... | collective-permute-start | bytes 589832 | tf_op jit(solution)/shard_map/ppermute | solution.py:347
  46.0 1.4 %collective-permute-start.16 = (bf16[384,128]{1,0:T(8,128)(2,1)S(1)}, bf16[384,128]{1,0:T(8,128)(2,1)S(1)}, u32[]{:S(2)}, u32[]{:S(2)}) collective-permute-start(bf16[384,128]{1,0:T(8,128)(2,1)S(1)} %get-tuple-element.58), channel_id=1, source_target_pairs={{0,3},{1,2},{2,1},{3,0},{4,7},{5,6},{6,5},{7,4},{8,11},{9,10},{10,... | collective-permute-start | bytes 294920 | tf_op jit(solution)/shard_map/ppermute | solution.py:347
  47.6 2.9 %collective-permute-start.15 = (bf16[384,128]{1,0:T(8,128)(2,1)S(1)}, bf16[384,128]{1,0:T(8,128)(2,1)S(1)}, u32[]{:S(2)}, u32[]{:S(2)}) collective-permute-start(bf16[384,128]{1,0:T(8,128)(2,1)S(1)} %add_convert_fusion), channel_id=1, source_target_pairs={{0,2},{1,3},{2,0},{3,1},{4,6},{5,7},{6,4},{7,5},{8,10},{9,11},{10,... | collective-permute-start | bytes 294920 | tf_op jit(solution)/shard_map/ppermute | solution.py:347
  51.1 4.3 %collective-permute-done.16.refs_2_ = bf16[384,128]{1,0:T(8,128)(2,1)S(1)} collective-permute-done((bf16[384,128]{1,0:T(8,128)(2,1)S(1)}, bf16[384,128]{1,0:T(8,128)(2,1)S(1)}, u32[]{:S(2)}, u32[]{:S(2)}) %collective-permute-start.16) | collective-permute-done | bytes 98336 | tf_op jit(solution)/shard_map/ppermute | solution.py:347
  55.4 4.1 %collective-permute-done.17.refs_3_ = bf16[384,128]{1,0:T(8,128)(2,1)S(1)} collective-permute-done((bf16[384,128]{1,0:T(8,128)(2,1)S(1)}, bf16[384,128]{1,0:T(8,128)(2,1)S(1)}, u32[]{:S(2)}, u32[]{:S(2)}) %collective-permute-start.17) | collective-permute-done | bytes 98336 | tf_op jit(solution)/shard_map/ppermute | solution.py:347
  59.5 1.2 %collective-permute-done.15.refs_1_ = bf16[384,128]{1,0:T(8,128)(2,1)S(1)} collective-permute-done((bf16[384,128]{1,0:T(8,128)(2,1)S(1)}, bf16[384,128]{1,0:T(8,128)(2,1)S(1)}, u32[]{:S(2)}, u32[]{:S(2)}) %collective-permute-start.15) | collective-permute-done | bytes 98336 | tf_op jit(solution)/shard_map/ppermute | solution.py:347
  (27 shorter events, 4.7 us)
Async XLA Ops:
  1.8 8.8 %collective-permute-start = (bf16[400,128]{1,0:T(8,128)(2,1)S(1)}, bf16[400,128]{1,0:T(8,128)(2,1)S(1)}, u32[]{:S(2)}, u32[]{:S(2)}) collective-permute-start(bf16[400,128]{1,0:T(8,128)(2,1)S(1)} %get-tuple-element.35), channel_id=1, source_target_pairs={{0,4},{4,0},{8,12},{12,8},{1,5},{5,1},{9,13},{13,9},{2,6},{6,2},{1... | collective-permute-start | bytes 307208 | tf_op jit(solution)/shard_map/ppermute | solution.py:347
  2.4 8.3 %collective-permute-start.1 = (bf16[400,128]{1,0:T(8,128)(2,1)S(1)}, bf16[400,128]{1,0:T(8,128)(2,1)S(1)}, u32[]{:S(2)}, u32[]{:S(2)}) collective-permute-start(bf16[400,128]{1,0:T(8,128)(2,1)S(1)} %get-tuple-element.36), channel_id=1, source_target_pairs={{0,12},{4,8},{8,4},{12,0},{1,13},{5,9},{9,5},{13,1},{2,14},{6,10},... | collective-permute-start | bytes 307208 | tf_op jit(solution)/shard_map/ppermute | solution.py:378
  5.0 7.0 %collective-permute-start.3 = (bf16[384,128]{1,0:T(8,128)(2,1)S(1)}, bf16[384,128]{1,0:T(8,128)(2,1)S(1)}, u32[]{:S(2)}, u32[]{:S(2)}) collective-permute-start(bf16[384,128]{1,0:T(8,128)(2,1)S(1)} %get-tuple-element.39), channel_id=1, source_target_pairs={{0,4},{4,0},{8,12},{12,8},{1,5},{5,1},{9,13},{13,9},{2,6},{6,2},{1... | collective-permute-start | bytes 294920 | tf_op jit(solution)/shard_map/ppermute | solution.py:347
  5.1 6.9 %collective-permute-start.4 = (bf16[384,128]{1,0:T(8,128)(2,1)S(1)}, bf16[384,128]{1,0:T(8,128)(2,1)S(1)}, u32[]{:S(2)}, u32[]{:S(2)}) collective-permute-start(bf16[384,128]{1,0:T(8,128)(2,1)S(1)} %get-tuple-element.40), channel_id=1, source_target_pairs={{0,12},{4,8},{8,4},{12,0},{1,13},{5,9},{9,5},{13,1},{2,14},{6,10},... | collective-permute-start | bytes 294920 | tf_op jit(solution)/shard_map/ppermute | solution.py:378
  5.1 5.5 %collective-permute-start.2 = (bf16[16,128]{1,0:T(8,128)(2,1)S(1)}, bf16[16,128]{1,0:T(8,128)(2,1)S(1)}, u32[]{:S(2)}, u32[]{:S(2)}) collective-permute-start(bf16[16,128]{1,0:T(8,128)(2,1)S(1)} %get-tuple-element.37.refs_5_), channel_id=1, source_target_pairs={{0,8},{4,12},{8,0},{12,4},{1,9},{5,13},{9,1},{13,5},{2,10},{6,14},... | collective-permute-start | bytes 12296 | tf_op jit(solution)/shard_map/ppermute | solution.py:347
  13.2 26.2 %copy-start = (bf16[3,3,3,128,512]{4,3,2,1,0:T(8,128)(2,1)S(1)}, bf16[3,3,3,128,512]{4,3,2,1,0:T(8,128)(2,1)}, u32[]{:S(2)}) copy-start(bf16[3,3,3,128,512]{4,3,2,1,0:T(8,128)(2,1)} %param.20) | copy-start | bytes 10616836
  13.2 7.9 %collective-permute-start.6 = (bf16[384,128]{1,0:T(8,128)(2,1)S(1)}, bf16[384,128]{1,0:T(8,128)(2,1)S(1)}, u32[]{:S(2)}, u32[]{:S(2)}) collective-permute-start(bf16[384,128]{1,0:T(8,128)(2,1)S(1)} %get-tuple-element.45), channel_id=1, source_target_pairs={{0,1},{1,0},{2,3},{3,2},{4,5},{5,4},{6,7},{7,6},{8,9},{9,8},{10,11... | collective-permute-start | bytes 294920 | tf_op jit(solution)/shard_map/ppermute | solution.py:347
  17.0 16.7 %collective-permute-start.5 = (bf16[768,128]{1,0:T(8,128)(2,1)S(1)}, bf16[768,128]{1,0:T(8,128)(2,1)S(1)}, u32[]{:S(2)}, u32[]{:S(2)}) collective-permute-start(bf16[768,128]{1,0:T(8,128)(2,1)S(1)} %get-tuple-element.43), channel_id=1, source_target_pairs={{0,1},{1,0},{2,3},{3,2},{4,5},{5,4},{6,7},{7,6},{8,9},{9,8},{10,11... | collective-permute-start | bytes 589832 | tf_op jit(solution)/shard_map/ppermute | solution.py:347
  17.3 11.7 %collective-permute-start.8 = (bf16[384,128]{1,0:T(8,128)(2,1)S(1)}, bf16[384,128]{1,0:T(8,128)(2,1)S(1)}, u32[]{:S(2)}, u32[]{:S(2)}) collective-permute-start(bf16[384,128]{1,0:T(8,128)(2,1)S(1)} %get-tuple-element.46), channel_id=1, source_target_pairs={{0,3},{1,2},{2,1},{3,0},{4,7},{5,6},{6,5},{7,4},{8,11},{9,10},{10,... | collective-permute-start | bytes 294920 | tf_op jit(solution)/shard_map/ppermute | solution.py:347
  21.1 11.6 %collective-permute-start.9 = (bf16[384,128]{1,0:T(8,128)(2,1)S(1)}, bf16[384,128]{1,0:T(8,128)(2,1)S(1)}, u32[]{:S(2)}, u32[]{:S(2)}) collective-permute-start(bf16[384,128]{1,0:T(8,128)(2,1)S(1)} %get-tuple-element.47), channel_id=1, source_target_pairs={{0,2},{1,3},{2,0},{3,1},{4,6},{5,7},{6,4},{7,5},{8,10},{9,11},{10,... | collective-permute-start | bytes 294920 | tf_op jit(solution)/shard_map/ppermute | solution.py:347
  21.1 12.6 %collective-permute-start.7 = (bf16[384,128]{1,0:T(8,128)(2,1)S(1)}, bf16[384,128]{1,0:T(8,128)(2,1)S(1)}, u32[]{:S(2)}, u32[]{:S(2)}) collective-permute-start(bf16[384,128]{1,0:T(8,128)(2,1)S(1)} %add_convert_fusion.1), channel_id=1, source_target_pairs={{0,2},{1,3},{2,0},{3,1},{4,6},{5,7},{6,4},{7,5},{8,10},{9,11},{10,... | collective-permute-start | bytes 294920 | tf_op jit(solution)/shard_map/ppermute | solution.py:347
  34.0 5.4 %collective-permute-start.10 = (bf16[400,128]{1,0:T(8,128)(2,1)S(1)}, bf16[400,128]{1,0:T(8,128)(2,1)S(1)}, u32[]{:S(2)}, u32[]{:S(2)}) collective-permute-start(bf16[400,128]{1,0:T(8,128)(2,1)S(1)} %get-tuple-element.49), channel_id=1, source_target_pairs={{0,4},{4,0},{8,12},{12,8},{1,5},{5,1},{9,13},{13,9},{2,6},{6,2},{1... | collective-permute-start | bytes 307208 | tf_op jit(solution)/shard_map/ppermute | solution.py:347
  34.1 5.3 %collective-permute-start.11 = (bf16[400,128]{1,0:T(8,128)(2,1)S(1)}, bf16[400,128]{1,0:T(8,128)(2,1)S(1)}, u32[]{:S(2)}, u32[]{:S(2)}) collective-permute-start(bf16[400,128]{1,0:T(8,128)(2,1)S(1)} %get-tuple-element.50), channel_id=1, source_target_pairs={{0,12},{4,8},{8,4},{12,0},{1,13},{5,9},{9,5},{13,1},{2,14},{6,10},... | collective-permute-start | bytes 307208 | tf_op jit(solution)/shard_map/ppermute | solution.py:378
  35.6 3.8 %collective-permute-start.12 = (bf16[16,128]{1,0:T(8,128)(2,1)S(1)}, bf16[16,128]{1,0:T(8,128)(2,1)S(1)}, u32[]{:S(2)}, u32[]{:S(2)}) collective-permute-start(bf16[16,128]{1,0:T(8,128)(2,1)S(1)} %get-tuple-element.51.refs_5_), channel_id=1, source_target_pairs={{0,8},{4,12},{8,0},{12,4},{1,9},{5,13},{9,1},{13,5},{2,10},{6,14},... | collective-permute-start | bytes 12296 | tf_op jit(solution)/shard_map/ppermute | solution.py:347
  41.9 5.7 %collective-permute-start.14 = (bf16[384,128]{1,0:T(8,128)(2,1)S(1)}, bf16[384,128]{1,0:T(8,128)(2,1)S(1)}, u32[]{:S(2)}, u32[]{:S(2)}) collective-permute-start(bf16[384,128]{1,0:T(8,128)(2,1)S(1)} %get-tuple-element.57), channel_id=1, source_target_pairs={{0,1},{1,0},{2,3},{3,2},{4,5},{5,4},{6,7},{7,6},{8,9},{9,8},{10,11... | collective-permute-start | bytes 294920 | tf_op jit(solution)/shard_map/ppermute | solution.py:347
  44.0 16.7 %collective-permute-start.13 = (bf16[768,128]{1,0:T(8,128)(2,1)S(1)}, bf16[768,128]{1,0:T(8,128)(2,1)S(1)}, u32[]{:S(2)}, u32[]{:S(2)}) collective-permute-start(bf16[768,128]{1,0:T(8,128)(2,1)S(1)} %get-tuple-element.55), channel_id=1, source_target_pairs={{0,1},{1,0},{2,3},{3,2},{4,5},{5,4},{6,7},{7,6},{8,9},{9,8},{10,11... | collective-permute-start | bytes 589832 | tf_op jit(solution)/shard_map/ppermute | solution.py:347
  46.0 9.4 %collective-permute-start.16 = (bf16[384,128]{1,0:T(8,128)(2,1)S(1)}, bf16[384,128]{1,0:T(8,128)(2,1)S(1)}, u32[]{:S(2)}, u32[]{:S(2)}) collective-permute-start(bf16[384,128]{1,0:T(8,128)(2,1)S(1)} %get-tuple-element.58), channel_id=1, source_target_pairs={{0,3},{1,2},{2,1},{3,0},{4,7},{5,6},{6,5},{7,4},{8,11},{9,10},{10,... | collective-permute-start | bytes 294920 | tf_op jit(solution)/shard_map/ppermute | solution.py:347
  47.5 12.0 %collective-permute-start.17 = (bf16[384,128]{1,0:T(8,128)(2,1)S(1)}, bf16[384,128]{1,0:T(8,128)(2,1)S(1)}, u32[]{:S(2)}, u32[]{:S(2)}) collective-permute-start(bf16[384,128]{1,0:T(8,128)(2,1)S(1)} %get-tuple-element.59), channel_id=1, source_target_pairs={{0,2},{1,3},{2,0},{3,1},{4,6},{5,7},{6,4},{7,5},{8,10},{9,11},{10,... | collective-permute-start | bytes 294920 | tf_op jit(solution)/shard_map/ppermute | solution.py:347
  47.6 13.1 %collective-permute-start.15 = (bf16[384,128]{1,0:T(8,128)(2,1)S(1)}, bf16[384,128]{1,0:T(8,128)(2,1)S(1)}, u32[]{:S(2)}, u32[]{:S(2)}) collective-permute-start(bf16[384,128]{1,0:T(8,128)(2,1)S(1)} %add_convert_fusion), channel_id=1, source_target_pairs={{0,2},{1,3},{2,0},{3,1},{4,6},{5,7},{6,4},{7,5},{8,10},{9,11},{10,... | collective-permute-start | bytes 294920 | tf_op jit(solution)/shard_map/ppermute | solution.py:347

commit v5 on v4

--- a/solution.py
+++ b/solution.py
@@ -137,41 +137,57 @@
     )[0]
 
 
-def total_of(own, terms, starts, bias):
+def total_of(own, terms, starts, bias, begin, end):
     ends = [start + term.shape[0] for term, start in zip(terms, starts)]
-    cuts = sorted({0, own.shape[0], *starts, *ends})
+    cuts = sorted({begin, end, *(cut for cut in (*starts, *ends) if begin < cut < end)})
     pieces = []
     for low, high in zip(cuts, cuts[1:]):
         value = own[low:high]
-        for term, start, end in zip(terms, starts, ends):
-            if start <= low and high <= end:
+        for term, start, stop in zip(terms, starts, ends):
+            if start <= low and high <= stop:
                 value = value + term[low - start : high - start].astype(jnp.float32)
         pieces.append(value)
     return (jnp.concatenate(pieces, axis=0) + bias).astype(jnp.bfloat16)
 
 
-def middle_body(row, starts, own, *refs):
-    terms, (table, hidden, tile, pair, other) = refs[: len(starts)], refs[len(starts) :]
-    rounded = total_of(own, terms, starts, table[row : row + 1])
-    store_moments(tile, (pair, other), moments_of(rounded.astype(jnp.float32)))
+def middle_body(static, own, *refs):
+    row, starts, begin, end, final, follows = static
+    terms, (table, *refs) = refs[: len(starts)], refs[len(starts) :]
+    if follows:
+        earlier, refs = refs[0], refs[1:]
+    hidden, tile, pair, other = refs
+    rounded = total_of(own, terms, starts, table[row : row + 1], begin, end)
+    moments = moments_of(rounded.astype(jnp.float32))
+    if follows:
+        moments = moments + earlier[0:2]
+    store_moments(tile, (pair, other) if final else (), moments)
     hidden[...] = rounded.reshape(hidden.shape)
     store_edges((hidden,), pair, other)
 
 
-def middle(own, terms, starts, table, row, shape):
-    frames, _, width, channels = shape
+def middle(own, terms, starts, table, row, shape, first, count, final, earlier=None):
+    _, rows, width, channels = shape
+    begin, end = first * rows * width, (first + count) * rows * width
+    used = [
+        (term, start)
+        for term, start in zip(terms, starts)
+        if start < end and start + term.shape[0] > begin
+    ]
     outs = [
-        jax.ShapeDtypeStruct(shape, jnp.bfloat16),
-        moments_tile(channels),
-        *message_shapes(frames, width, channels, PACKED),
+        jax.ShapeDtypeStruct((count, rows, width, channels), jnp.bfloat16),
+        moments_tile(channels) if final else jax.ShapeDtypeStruct((8, channels), jnp.float32),
+        *message_shapes(count, width, channels, PACKED if final else 0),
     ]
-    body = functools.partial(middle_body, row, starts)
-    return call(body, outs, (own, *terms, table))
+    extra = () if earlier is None else (earlier,)
+    static = (row, [start for _, start in used], begin, end, final, bool(extra))
+    args = (own, *[term for term, _ in used], table, *extra)
+    return call(functools.partial(middle_body, static), outs, args)
 
 
 def close_body(row, starts, own, *refs):
     terms, (table, out) = refs[: len(starts)], refs[len(starts) :]
-    out[...] = total_of(own, terms, starts, table[row : row + 1]).reshape(out.shape)
+    total = total_of(own, terms, starts, table[row : row + 1], 0, own.shape[0])
+    out[...] = total.reshape(out.shape)
 
 
 def close(own, terms, starts, table, row, shape):
@@ -207,8 +223,13 @@
             right = jnp.concatenate(right, axis=1)
             product = jnp.dot(left, right, preferred_element_type=jnp.float32)
             total = product if total is None else total + product
-    for place, out in enumerate(outs):
-        out[...] = total[:, place * channels : (place + 1) * channels].astype(out.dtype)
+    for place, group in enumerate(outs):
+        start = 0
+        for out in group:
+            cells = out.shape[0]
+            piece = total[start : start + cells, place * channels : (place + 1) * channels]
+            out[...] = piece.astype(out.dtype)
+            start += cells
 
 
 def leading(weights, channels):
@@ -254,11 +275,14 @@
 
 
 def first_body(static, *refs):
-    entries, row, history, tiles = static
-    x, table, weights, pair, other = refs[:5]
-    sums, refs = refs[5 : 5 + tiles], refs[5 + tiles :]
+    entries, row, history, parts, tiles = static
+    xs, refs = refs[:parts], refs[parts:]
+    pairs, others, refs = refs[:parts], refs[parts : 2 * parts], refs[2 * parts :]
+    (table, weights), refs = refs[:2], refs[2:]
+    sums, refs = refs[:tiles], refs[tiles:]
     shifted, outs = refs[0], refs[1:]
-    frames, _, _, channels = x.shape
+    _, _, _, channels = xs[0].shape
+    frames = shifted.shape[1]
     per_group = CHANNELS // GROUPS
     shape = (channels, channels)
     member = (
@@ -266,7 +290,7 @@
         == lax.broadcasted_iota(jnp.int32, shape, 1) // per_group
     ).astype(sums[0].dtype)
     if tiles > 1:
-        last = [message[message.shape[0] - PACKED :] for message in (pair, other)]
+        last = [message[message.shape[0] - PACKED :] for message in (pairs[0], others[0])]
         packed = jnp.concatenate([sums[0][...], last[0], sums[1][...], last[1]], axis=0)
         terms = jnp.dot(packed, member, preferred_element_type=jnp.float32)
         mine, beside, across, corner = (
@@ -283,16 +307,23 @@
     average, squares = grouped[0:1], grouped[1:2]
     scale = lax.rsqrt(squares - average * average + EPS) * table[row : row + 1]
     norm = (average, scale, table[row + 1 : row + 2])
-    for frame in range(frames):
-        put_frame(shifted, frame, x, frame, pair, other, frame, lambda value: activate(value, norm))
-    products([shifted], weights, 0, frames - history, leading(weights, channels), outs)
+    place = 0
+    for x, pair, other in zip(xs, pairs, others):
+        for frame in range(x.shape[0]):
+            put_frame(
+                shifted, place, x, frame, pair, other, frame, lambda value: activate(value, norm)
+            )
+            place += 1
+    leads = [(out,) for out in outs]
+    products([shifted], weights, 0, frames - history, leading(weights, channels), leads)
 
 
 def second_body(offset, cache, after, weights, pair, other, shifted, *outs):
     history, channels = cache.shape[0], cache.shape[3]
     for frame in range(history):
         put_frame(shifted, frame, cache, frame, pair, other, offset + frame, lambda value: value)
-    products([shifted, after], weights, 0, history, leading(weights, channels), outs)
+    leads = [(out,) for out in outs]
+    products([shifted, after], weights, 0, history, leading(weights, channels), leads)
 
 
 def keep_body(after, kept):
@@ -302,11 +333,12 @@
 def last_body(before, after, weights, *outs):
     frames = after.shape[1]
     mine = lax.axis_index("chan")
-    products([before, after], weights, 0, frames, [mine ^ 1, mine], outs)
-
-
-def conv(x, messages, tiles, cache, old_messages, offset, table, row, weights, entries):
-    frames, rows, width, channels = x.shape
+    products([before, after], weights, 0, frames, [mine ^ 1, mine], [outs[:-1], outs[-1:]])
+
+
+def conv(xs, messages, tiles, cache, old_messages, offset, table, row, weights, entries):
+    _, rows, width, channels = xs[0].shape
+    frames = sum(x.shape[0] for x in xs)
     history = cache.shape[0]
     blocks = weights.shape[2] // channels
     split = blocks == 4
@@ -321,9 +353,10 @@
     def padded(count):
         return jax.ShapeDtypeStruct((3, count, rows + 2, width, channels), jnp.bfloat16)
 
+    pairs, others = zip(*messages)
     after, *one = call(
-        functools.partial(first_body, (entries, row, history, len(tiles))),
-        [padded(frames), *led(frames - history)], (x, table, weights, *messages, *tiles),
+        functools.partial(first_body, (entries, row, history, len(xs), len(tiles))),
+        [padded(frames), *led(frames - history)], (*xs, *pairs, *others, table, weights, *tiles),
         flops=work * (frames - history) * lead,
     )
     before, *two = call(
@@ -332,8 +365,10 @@
     )
 
     def rest():
-        cells = frames * rows * width
-        outs = [jax.ShapeDtypeStruct((cells, channels), kind) for kind in (jnp.bfloat16, jnp.float32)]
+        outs = [
+            *[led(count)[0] for count in (history, frames - history)],
+            jax.ShapeDtypeStruct((frames * rows * width, channels), jnp.float32),
+        ]
         return call(last_body, outs, (before, after, weights), flops=work * frames * 2)
 
     def kept():
@@ -365,11 +400,13 @@
     far, near = two
     arrived = swap(far, "chan", 1)
     joined = (near + arrived.astype(jnp.float32)).astype(jnp.bfloat16)
-    block, own = rest()
-    beside = swap(block, "chan", 1)
+    *blocks, own = rest()
+    beside = []
+    for block in blocks:
+        beside.append(swap(block, "chan", 1))
     across = swap(joined, "chan", 2)
     start = across.shape[0]
-    return own, [beside, across, *direct], [0, 0, start, start]
+    return own, [*beside, across, *direct], [0, start, 0, start, start]
 
 
 def to_neighbours(pair, other):
@@ -425,12 +462,21 @@
     old_messages = to_neighbours(old_pair, old_other)
     weights = fetch(taps(kernel_first))
     *parts, _ = conv(
-        x, messages, tiles, first, old_messages, 0, table, 0, weights, entries
+        [x], [messages], tiles, first, old_messages, 0, table, 0, weights, entries
     )
     own, terms, starts = reduce_terms(*parts)
-    hidden, tile, pair, other = middle(own, terms, starts, table, 2, x.shape)
+    outward_part = functools.partial(middle, own, terms, starts, table, 2, x.shape)
+    history = first.shape[0]
+    if any(starts):
+        late, earlier, pair, other = outward_part(history, frames - history, False)
+        late_messages = to_neighbours(pair, other)
+        early, tile, pair, other = outward_part(0, history, True, earlier)
+        hidden, rest = [early, late], [late_messages]
+    else:
+        whole, tile, pair, other = outward_part(0, frames, True)
+        hidden, rest = [whole], []
     tiles = over_rows(tile)
-    messages = to_neighbours(pair, other)
+    messages = [to_neighbours(pair, other), *rest]
     weights = taps(kernel_second)
     *parts, kept = conv(
         hidden, messages, tiles, second, old_messages, first.shape[0], table, 3, weights, entries

time: 61.6 us -> 57.8 us (0.938)
  waiting for transfers between devices: 23.9 us -> 18.9 us
  starting transfers between devices: 22.9 us -> 24.1 us
    ppermute x15 -> x18, waiting for transfers between devices: 23.9 us -> 17.4 us  [swap(): lax.ppermute(value, axis, [(i, i ^ step) for i in range(lax.axis_size(axi...]
    ppermute x3 -> x4, waiting for transfers between devices: 0.01 us -> 1.46 us  [to_neighbours(): across = lax.ppermute(other, 'rows', ring)]
    ppermute x3 -> x4, starting transfers between devices: 4.26 us -> 4.86 us  [to_neighbours(): across = lax.ppermute(other, 'rows', ring)]
    ppermute x15 -> x18, starting transfers between devices: 18.7 us -> 19.2 us  [swap(): lax.ppermute(value, axis, [(i, i ^ step) for i in range(lax.axis_size(axi...]
    pallas_call x11 -> x12, Pallas kernels: 13.8 us -> 13.8 us  [call(): pl.pallas_call(body, out_shape=outs, in_specs=specs or [on_chip()] * len(...]
  transfers between devices with their start and end apart: 18 -> 22, of which waited for: 8 -> 10; matrix products, arithmetic and copies ran while one was open for 0% -> 0% of each run, Pallas kernels for 13% -> 18%
where the time goes in v5:
time: 57.8 us; the launch traced here: 57.6 us
  starting transfers between devices  24.1 us (42%)
  waiting for transfers between devices  18.9 us (33%)
  Pallas kernels  13.8 us (24%)
  between operations  0.77 us (1%)
    ppermute x18, starting transfers between devices, swap(): lax.ppermute(value, axis, [(i, i ^ step) for i in range(lax.axis_size(axi...  19.2 us
    ppermute x18, waiting for transfers between devices, swap(): lax.ppermute(value, axis, [(i, i ^ step) for i in range(lax.axis_size(axi...  17.4 us
    pallas_call x12, Pallas kernels, call(): pl.pallas_call(body, out_shape=outs, in_specs=specs or [on_chip()] * len(...  13.8 us
    ppermute x4, starting transfers between devices, to_neighbours(): across = lax.ppermute(other, 'rows', ring)  4.86 us
    ppermute x4, waiting for transfers between devices, to_neighbours(): across = lax.ppermute(other, 'rows', ring)  1.46 us
  transfers between devices with their start and end apart: 22, of which 10 were waited for; matrix products, arithmetic and copies ran while one was open for 0% of the time, Pallas kernels for 18%

profile of v5, /device:TPU:0, one launch (start us, length us, event | category | flops | bytes accessed | tf_op | source)
XLA Modules:
  0.0 57.6 jit_solution(9965125996913245531)
XLA Ops:
  0.6 1.2 %shard_map.122 = (bf16[4,2,96,128]{3,2,1,0:T(8,128)(2,1)S(1)}, bf16[2,2,96,128]{3,2,1,0:T(8,128)(2,1)S(1)}, bf16[2,2,96,128]{3,2,1,0:T(8,128)(2,1)S(1)}, f32[8,1...) custom-call(bf16[4,2,96,128]{3,2,1,0:T(8,128)(2,1)} %bitcast.17, ...), custom_call_target="tpu_custom_call" | custom-call | bytes 1199104 | tf_op jit(solution)/shard_map/pallas_call | solution.py:29
  2.4 2.6 %collective-permute-start.1 = (bf16[400,128]{1,0:T(8,128)(2,1)S(1)}, bf16[400,128]{1,0:T(8,128)(2,1)S(1)}, u32[]{:S(2)}, u32[]{:S(2)}) collective-permute-start(bf16[400,128]{1,0:T(8,128)(2,1)S(1)} %get-tuple-element.41), channel_id=1, source_target_pairs={{0,12},{4,8},{8,4},{12,0},{1,13},{5,9},{9,5},{13,1},{2,14},{6,10},... | collective-permute-start | bytes 307208 | tf_op jit(solution)/shard_map/ppermute | solution.py:415
  5.1 2.0 %collective-permute-start.2 = (bf16[16,128]{1,0:T(8,128)(2,1)S(1)}, bf16[16,128]{1,0:T(8,128)(2,1)S(1)}, u32[]{:S(2)}, u32[]{:S(2)}) collective-permute-start(bf16[16,128]{1,0:T(8,128)(2,1)S(1)} %get-tuple-element.43.refs_5_), channel_id=1, source_target_pairs={{0,8},{4,12},{8,0},{12,4},{1,9},{5,13},{9,1},{13,5},{2,10},{6,14},... | collective-permute-start | bytes 12296 | tf_op jit(solution)/shard_map/ppermute | solution.py:382
  7.1 2.0 %shard_map.123.refs_4_.weights = bf16[9,384,512]{2,1,0:T(8,128)(2,1)S(1)} custom-call(bf16[9,384,512]{2,1,0:T(8,128)(2,1)} %bitcast.16), custom_call_target="tpu_custom_call" | custom-call | bytes 7077888 | tf_op jit(solution)/shard_map/pallas_call | solution.py:29
  9.2 1.5 %collective-permute-done.2.refs_6_ = bf16[16,128]{1,0:T(8,128)(2,1)S(1)} collective-permute-done((bf16[16,128]{1,0:T(8,128)(2,1)S(1)}, bf16[16,128]{1,0:T(8,128)(2,1)S(1)}, u32[]{:S(2)}, u32[]{:S(2)}) %collective-permute-start.2) | collective-permute-done | bytes 4128 | tf_op jit(solution)/shard_map/ppermute | solution.py:382
  10.6 1.4 %shard_map.124 = (bf16[3,4,4,96,128]{4,3,2,1,0:T(8,128)(2,1)S(1)}, bf16[384,128]{1,0:T(8,128)(2,1)S(1)}, bf16[384,128]{1,0:T(8,128)(2,1)S(1)}) custom-call(bf16[4,2,96,128]{3,2,1,0:T(8,128)(2,1)S(1)} %get-tuple-element.39.refs_0_, bf16[400,128]{1,0:T(8,128)(2,1)S(1)} %collective-permute-done.refs_1_, bf16[400,128]{1,0:T(8,128)(2,1)S(1)} %collective-permute-done.1.refs_2_, ...), custom_call_target="tpu_custom_call" | custom-call | flops 679477248 | bytes 5328896 | tf_op jit(solution)/shard_map/pallas_call | solution.py:29
  12.0 3.8 %collective-permute-start.9 = (bf16[384,128]{1,0:T(8,128)(2,1)S(1)}, bf16[384,128]{1,0:T(8,128)(2,1)S(1)}, u32[]{:S(2)}, u32[]{:S(2)}) collective-permute-start(bf16[384,128]{1,0:T(8,128)(2,1)S(1)} %get-tuple-element.53), channel_id=1, source_target_pairs={{0,3},{1,2},{2,1},{3,0},{4,7},{5,6},{6,5},{7,4},{8,11},{9,10},{10,... | collective-permute-start | bytes 294920 | tf_op jit(solution)/shard_map/ppermute | solution.py:382
  15.8 1.1 %shard_map.125 = (bf16[3,2,4,96,128]{4,3,2,1,0:T(8,128)(2,1)S(1)}, bf16[384,128]{1,0:T(8,128)(2,1)S(1)}, f32[384,128]{1,0:T(8,128)S(1)}) custom-call(bf16[2,2,96,128]{3,2,1,0:T(8,128)(2,1)S(1)} %get-tuple-element.38.cache, bf16[3,4,4,96,128]{4,3,2,1,0:T(8,128)(2,1)S(1)} %get-tuple-element.44.after, bf16[9,384,512]{2,1,0:T(8,128)(2,1)S(1)} %shard_map.123.refs_4_.weights, ...), custom_call_target="tpu_custom_call" | custom-call | flops 679477248 | bytes 5898240 | tf_op jit(solution)/shard_map/pallas_call | solution.py:29
  17.7 2.0 %shard_map.126 = (bf16[384,128]{1,0:T(8,128)(2,1)S(1)}, bf16[384,128]{1,0:T(8,128)(2,1)S(1)}, f32[768,128]{1,0:T(8,128)S(1)}) custom-call(bf16[3,2,4,96,128]{4,3,2,1,0:T(8,128)(2,1)S(1)} %get-tuple-element.47.before, bf16[3,4,4,96,128]{4,3,2,1,0:T(8,128)(2,1)S(1)} %get-tuple-element.44.after, bf16[9,384,512]{2,1,0:T(8,128)(2,1)S(1)} %shard_map.123.refs_4_.weights), custom_call_target="tpu_custom_call" | custom-call | flops 1358954496 | bytes 5898240 | tf_op jit(solution)/shard_map/pallas_call | solution.py:29
  19.7 1.5 %collective-permute-start.5 = (bf16[384,128]{1,0:T(8,128)(2,1)S(1)}, bf16[384,128]{1,0:T(8,128)(2,1)S(1)}, u32[]{:S(2)}, u32[]{:S(2)}) collective-permute-start(bf16[384,128]{1,0:T(8,128)(2,1)S(1)} %get-tuple-element.49), channel_id=1, source_target_pairs={{0,1},{1,0},{2,3},{3,2},{4,5},{5,4},{6,7},{7,6},{8,9},{9,8},{10,11... | collective-permute-start | bytes 294920 | tf_op jit(solution)/shard_map/ppermute | solution.py:382
  21.8 3.8 %collective-permute-done.6 = bf16[384,128]{1,0:T(8,128)(2,1)S(1)} collective-permute-done((bf16[384,128]{1,0:T(8,128)(2,1)S(1)}, bf16[384,128]{1,0:T(8,128)(2,1)S(1)}, u32[]{:S(2)}, u32[]{:S(2)}) %collective-permute-start.6) | collective-permute-done | bytes 98336 | tf_op jit(solution)/shard_map/ppermute | solution.py:382
  25.7 3.4 %collective-permute-done.8.refs_0_ = bf16[384,128]{1,0:T(8,128)(2,1)S(1)} collective-permute-done((bf16[384,128]{1,0:T(8,128)(2,1)S(1)}, bf16[384,128]{1,0:T(8,128)(2,1)S(1)}, u32[]{:S(2)}, u32[]{:S(2)}) %collective-permute-start.8) | collective-permute-done | bytes 98336 | tf_op jit(solution)/shard_map/ppermute | solution.py:382
  29.2 2.6 %collective-permute-done.7.refs_1_ = bf16[384,128]{1,0:T(8,128)(2,1)S(1)} collective-permute-done((bf16[384,128]{1,0:T(8,128)(2,1)S(1)}, bf16[384,128]{1,0:T(8,128)(2,1)S(1)}, u32[]{:S(2)}, u32[]{:S(2)}) %collective-permute-start.7) | collective-permute-done | bytes 98336 | tf_op jit(solution)/shard_map/ppermute | solution.py:382
  32.0 1.6 %collective-permute-start.13 = (bf16[208,128]{1,0:T(8,128)(2,1)S(1)}, bf16[208,128]{1,0:T(8,128)(2,1)S(1)}, u32[]{:S(2)}, u32[]{:S(2)}) collective-permute-start(bf16[208,128]{1,0:T(8,128)(2,1)S(1)} %get-tuple-element.60), channel_id=1, source_target_pairs={{0,12},{4,8},{8,4},{12,0},{1,13},{5,9},{9,5},{13,1},{2,14},{6,10},... | collective-permute-start | bytes 159752 | tf_op jit(solution)/shard_map/ppermute | solution.py:415
  34.2 1.5 %collective-permute-start.15 = (bf16[16,128]{1,0:T(8,128)(2,1)S(1)}, bf16[16,128]{1,0:T(8,128)(2,1)S(1)}, u32[]{:S(2)}, u32[]{:S(2)}) collective-permute-start(bf16[16,128]{1,0:T(8,128)(2,1)S(1)} %get-tuple-element.62.refs_8_), channel_id=1, source_target_pairs={{0,8},{4,12},{8,0},{12,4},{1,9},{5,13},{9,1},{13,5},{2,10},{6,14},... | collective-permute-start | bytes 12296 | tf_op jit(solution)/shard_map/ppermute | solution.py:382
  35.7 1.4 %collective-permute-done.14.refs_5_ = bf16[192,128]{1,0:T(8,128)(2,1)S(1)} collective-permute-done((bf16[192,128]{1,0:T(8,128)(2,1)S(1)}, bf16[192,128]{1,0:T(8,128)(2,1)S(1)}, u32[]{:S(2)}, u32[]{:S(2)}) %collective-permute-start.14) | collective-permute-done | bytes 49184 | tf_op jit(solution)/shard_map/ppermute | solution.py:415
  37.9 1.3 %shard_map.129 = (bf16[3,4,4,96,128]{4,3,2,1,0:T(8,128)(2,1)S(1)}, bf16[384,128]{1,0:T(8,128)(2,1)S(1)}, bf16[384,128]{1,0:T(8,128)(2,1)S(1)}) custom-call(bf16[2,2,96,128]{3,2,1,0:T(8,128)(2,1)S(1)} %get-tuple-element.56.refs_0_, bf16[2,2,96,128]{3,2,1,0:T(8,128)(2,1)S(1)} %get-tuple-element.57.refs_1_, ...), custom_call_target="tpu_custom_call" | custom-call | flops 679477248 | bytes 5328896 | tf_op jit(solution)/shard_map/pallas_call | solution.py:29
  41.5 3.4 %collective-permute-start.18 = (bf16[384,128]{1,0:T(8,128)(2,1)S(1)}, bf16[384,128]{1,0:T(8,128)(2,1)S(1)}, u32[]{:S(2)}, u32[]{:S(2)}) collective-permute-start(bf16[384,128]{1,0:T(8,128)(2,1)S(1)} %get-tuple-element.69), channel_id=1, source_target_pairs={{0,1},{1,0},{2,3},{3,2},{4,5},{5,4},{6,7},{7,6},{8,9},{9,8},{10,11... | collective-permute-start | bytes 294920 | tf_op jit(solution)/shard_map/ppermute | solution.py:382
  44.9 2.0 %shard_map.131 = (bf16[384,128]{1,0:T(8,128)(2,1)S(1)}, bf16[384,128]{1,0:T(8,128)(2,1)S(1)}, f32[768,128]{1,0:T(8,128)S(1)}) custom-call(bf16[3,2,4,96,128]{4,3,2,1,0:T(8,128)(2,1)S(1)} %get-tuple-element.64.before, bf16[3,4,4,96,128]{4,3,2,1,0:T(8,128)(2,1)S(1)} %get-tuple-element.63.after, bf16[9,384,512]{2,1,0:T(8,128)(2,1)S(1)} %bitcast.15), custom_call_target="tpu_custom_call" | custom-call | flops 1358954496 | bytes 5898240 | tf_op jit(solution)/shard_map/pallas_call | solution.py:29
  46.9 2.0 %collective-permute-start.17 = (bf16[384,128]{1,0:T(8,128)(2,1)S(1)}, bf16[384,128]{1,0:T(8,128)(2,1)S(1)}, u32[]{:S(2)}, u32[]{:S(2)}) collective-permute-start(bf16[384,128]{1,0:T(8,128)(2,1)S(1)} %get-tuple-element.67), channel_id=1, source_target_pairs={{0,1},{1,0},{2,3},{3,2},{4,5},{5,4},{6,7},{7,6},{8,9},{9,8},{10,11... | collective-permute-start | bytes 294920 | tf_op jit(solution)/shard_map/ppermute | solution.py:382
  50.0 1.6 %collective-permute-start.19 = (bf16[384,128]{1,0:T(8,128)(2,1)S(1)}, bf16[384,128]{1,0:T(8,128)(2,1)S(1)}, u32[]{:S(2)}, u32[]{:S(2)}) collective-permute-start(bf16[384,128]{1,0:T(8,128)(2,1)S(1)} %add_convert_fusion), channel_id=1, source_target_pairs={{0,2},{1,3},{2,0},{3,1},{4,6},{5,7},{6,4},{7,5},{8,10},{9,11},{10,... | collective-permute-start | bytes 294920 | tf_op jit(solution)/shard_map/ppermute | solution.py:382
  52.3 1.4 %collective-permute-done.16.refs_0_ = bf16[384,128]{1,0:T(8,128)(2,1)S(1)} collective-permute-done((bf16[384,128]{1,0:T(8,128)(2,1)S(1)}, bf16[384,128]{1,0:T(8,128)(2,1)S(1)}, u32[]{:S(2)}, u32[]{:S(2)}) %collective-permute-start.16) | collective-permute-done | bytes 98336 | tf_op jit(solution)/shard_map/ppermute | solution.py:382
  53.6 1.4 %collective-permute-done.17.refs_1_ = bf16[384,128]{1,0:T(8,128)(2,1)S(1)} collective-permute-done((bf16[384,128]{1,0:T(8,128)(2,1)S(1)}, bf16[384,128]{1,0:T(8,128)(2,1)S(1)}, u32[]{:S(2)}, u32[]{:S(2)}) %collective-permute-start.17) | collective-permute-done | bytes 98336 | tf_op jit(solution)/shard_map/ppermute | solution.py:382
  55.1 1.8 %collective-permute-done.19.refs_2_ = bf16[384,128]{1,0:T(8,128)(2,1)S(1)} collective-permute-done((bf16[384,128]{1,0:T(8,128)(2,1)S(1)}, bf16[384,128]{1,0:T(8,128)(2,1)S(1)}, u32[]{:S(2)}, u32[]{:S(2)}) %collective-permute-start.19) | collective-permute-done | bytes 98336 | tf_op jit(solution)/shard_map/ppermute | solution.py:382
  (36 shorter events, 8.5 us)
Async XLA Ops:
  1.8 8.8 %collective-permute-start = (bf16[400,128]{1,0:T(8,128)(2,1)S(1)}, bf16[400,128]{1,0:T(8,128)(2,1)S(1)}, u32[]{:S(2)}, u32[]{:S(2)}) collective-permute-start(bf16[400,128]{1,0:T(8,128)(2,1)S(1)} %get-tuple-element.40), channel_id=1, source_target_pairs={{0,4},{4,0},{8,12},{12,8},{1,5},{5,1},{9,13},{13,9},{2,6},{6,2},{1... | collective-permute-start | bytes 307208 | tf_op jit(solution)/shard_map/ppermute | solution.py:382
  2.4 8.3 %collective-permute-start.1 = (bf16[400,128]{1,0:T(8,128)(2,1)S(1)}, bf16[400,128]{1,0:T(8,128)(2,1)S(1)}, u32[]{:S(2)}, u32[]{:S(2)}) collective-permute-start(bf16[400,128]{1,0:T(8,128)(2,1)S(1)} %get-tuple-element.41), channel_id=1, source_target_pairs={{0,12},{4,8},{8,4},{12,0},{1,13},{5,9},{9,5},{13,1},{2,14},{6,10},... | collective-permute-start | bytes 307208 | tf_op jit(solution)/shard_map/ppermute | solution.py:415
  5.0 10.8 %collective-permute-start.3 = (bf16[384,128]{1,0:T(8,128)(2,1)S(1)}, bf16[384,128]{1,0:T(8,128)(2,1)S(1)}, u32[]{:S(2)}, u32[]{:S(2)}) collective-permute-start(bf16[384,128]{1,0:T(8,128)(2,1)S(1)} %get-tuple-element.45), channel_id=1, source_target_pairs={{0,4},{4,0},{8,12},{12,8},{1,5},{5,1},{9,13},{13,9},{2,6},{6,2},{1... | collective-permute-start | bytes 294920 | tf_op jit(solution)/shard_map/ppermute | solution.py:382
  5.1 10.7 %collective-permute-start.4 = (bf16[384,128]{1,0:T(8,128)(2,1)S(1)}, bf16[384,128]{1,0:T(8,128)(2,1)S(1)}, u32[]{:S(2)}, u32[]{:S(2)}) collective-permute-start(bf16[384,128]{1,0:T(8,128)(2,1)S(1)} %get-tuple-element.46), channel_id=1, source_target_pairs={{0,12},{4,8},{8,4},{12,0},{1,13},{5,9},{9,5},{13,1},{2,14},{6,10},... | collective-permute-start | bytes 294920 | tf_op jit(solution)/shard_map/ppermute | solution.py:415
  5.1 5.5 %collective-permute-start.2 = (bf16[16,128]{1,0:T(8,128)(2,1)S(1)}, bf16[16,128]{1,0:T(8,128)(2,1)S(1)}, u32[]{:S(2)}, u32[]{:S(2)}) collective-permute-start(bf16[16,128]{1,0:T(8,128)(2,1)S(1)} %get-tuple-element.43.refs_5_), channel_id=1, source_target_pairs={{0,8},{4,12},{8,0},{12,4},{1,9},{5,13},{9,1},{13,5},{2,10},{6,14},... | collective-permute-start | bytes 12296 | tf_op jit(solution)/shard_map/ppermute | solution.py:382
  12.0 13.7 %collective-permute-start.9 = (bf16[384,128]{1,0:T(8,128)(2,1)S(1)}, bf16[384,128]{1,0:T(8,128)(2,1)S(1)}, u32[]{:S(2)}, u32[]{:S(2)}) collective-permute-start(bf16[384,128]{1,0:T(8,128)(2,1)S(1)} %get-tuple-element.53), channel_id=1, source_target_pairs={{0,3},{1,2},{2,1},{3,0},{4,7},{5,6},{6,5},{7,4},{8,11},{9,10},{10,... | collective-permute-start | bytes 294920 | tf_op jit(solution)/shard_map/ppermute | solution.py:382
  15.8 9.9 %collective-permute-start.10 = (bf16[384,128]{1,0:T(8,128)(2,1)S(1)}, bf16[384,128]{1,0:T(8,128)(2,1)S(1)}, u32[]{:S(2)}, u32[]{:S(2)}) collective-permute-start(bf16[384,128]{1,0:T(8,128)(2,1)S(1)} %get-tuple-element.54), channel_id=1, source_target_pairs={{0,2},{1,3},{2,0},{3,1},{4,6},{5,7},{6,4},{7,5},{8,10},{9,11},{10,... | collective-permute-start | bytes 294920 | tf_op jit(solution)/shard_map/ppermute | solution.py:382
  17.0 20.9 %copy-start = (bf16[3,3,3,128,512]{4,3,2,1,0:T(8,128)(2,1)S(1)}, bf16[3,3,3,128,512]{4,3,2,1,0:T(8,128)(2,1)}, u32[]{:S(2)}) copy-start(bf16[3,3,3,128,512]{4,3,2,1,0:T(8,128)(2,1)} %param.20) | copy-start | bytes 10616836
  17.0 8.6 %collective-permute-start.6 = (bf16[384,128]{1,0:T(8,128)(2,1)S(1)}, bf16[384,128]{1,0:T(8,128)(2,1)S(1)}, u32[]{:S(2)}, u32[]{:S(2)}) collective-permute-start(bf16[384,128]{1,0:T(8,128)(2,1)S(1)} %get-tuple-element.51), channel_id=1, source_target_pairs={{0,1},{1,0},{2,3},{3,2},{4,5},{5,4},{6,7},{7,6},{8,9},{9,8},{10,11... | collective-permute-start | bytes 294920 | tf_op jit(solution)/shard_map/ppermute | solution.py:382
  19.7 9.5 %collective-permute-start.5 = (bf16[384,128]{1,0:T(8,128)(2,1)S(1)}, bf16[384,128]{1,0:T(8,128)(2,1)S(1)}, u32[]{:S(2)}, u32[]{:S(2)}) collective-permute-start(bf16[384,128]{1,0:T(8,128)(2,1)S(1)} %get-tuple-element.49), channel_id=1, source_target_pairs={{0,1},{1,0},{2,3},{3,2},{4,5},{5,4},{6,7},{7,6},{8,9},{9,8},{10,11... | collective-permute-start | bytes 294920 | tf_op jit(solution)/shard_map/ppermute | solution.py:382
  21.1 7.9 %collective-permute-start.8 = (bf16[384,128]{1,0:T(8,128)(2,1)S(1)}, bf16[384,128]{1,0:T(8,128)(2,1)S(1)}, u32[]{:S(2)}, u32[]{:S(2)}) collective-permute-start(bf16[384,128]{1,0:T(8,128)(2,1)S(1)} %get-tuple-element.52), channel_id=1, source_target_pairs={{0,1},{1,0},{2,3},{3,2},{4,5},{5,4},{6,7},{7,6},{8,9},{9,8},{10,11... | collective-permute-start | bytes 294920 | tf_op jit(solution)/shard_map/ppermute | solution.py:382
  25.6 6.2 %collective-permute-start.7 = (bf16[384,128]{1,0:T(8,128)(2,1)S(1)}, bf16[384,128]{1,0:T(8,128)(2,1)S(1)}, u32[]{:S(2)}, u32[]{:S(2)}) collective-permute-start(bf16[384,128]{1,0:T(8,128)(2,1)S(1)} %add_convert_fusion.1), channel_id=1, source_target_pairs={{0,2},{1,3},{2,0},{3,1},{4,6},{5,7},{6,4},{7,5},{8,10},{9,11},{10,... | collective-permute-start | bytes 294920 | tf_op jit(solution)/shard_map/ppermute | solution.py:382
  31.9 5.9 %collective-permute-start.11 = (bf16[208,128]{1,0:T(8,128)(2,1)S(1)}, bf16[208,128]{1,0:T(8,128)(2,1)S(1)}, u32[]{:S(2)}, u32[]{:S(2)}) collective-permute-start(bf16[208,128]{1,0:T(8,128)(2,1)S(1)} %get-tuple-element.58), channel_id=1, source_target_pairs={{0,4},{4,0},{8,12},{12,8},{1,5},{5,1},{9,13},{13,9},{2,6},{6,2},{1... | collective-permute-start | bytes 159752 | tf_op jit(solution)/shard_map/ppermute | solution.py:382
  32.0 5.9 %collective-permute-start.13 = (bf16[208,128]{1,0:T(8,128)(2,1)S(1)}, bf16[208,128]{1,0:T(8,128)(2,1)S(1)}, u32[]{:S(2)}, u32[]{:S(2)}) collective-permute-start(bf16[208,128]{1,0:T(8,128)(2,1)S(1)} %get-tuple-element.60), channel_id=1, source_target_pairs={{0,12},{4,8},{8,4},{12,0},{1,13},{5,9},{9,5},{13,1},{2,14},{6,10},... | collective-permute-start | bytes 159752 | tf_op jit(solution)/shard_map/ppermute | solution.py:415
  33.6 2.1 %collective-permute-start.12 = (bf16[192,128]{1,0:T(8,128)(2,1)S(1)}, bf16[192,128]{1,0:T(8,128)(2,1)S(1)}, u32[]{:S(2)}, u32[]{:S(2)}) collective-permute-start(bf16[192,128]{1,0:T(8,128)(2,1)S(1)} %get-tuple-element.59), channel_id=1, source_target_pairs={{0,4},{4,0},{8,12},{12,8},{1,5},{5,1},{9,13},{13,9},{2,6},{6,2},{1... | collective-permute-start | bytes 147464 | tf_op jit(solution)/shard_map/ppermute | solution.py:382
  33.7 3.5 %collective-permute-start.14 = (bf16[192,128]{1,0:T(8,128)(2,1)S(1)}, bf16[192,128]{1,0:T(8,128)(2,1)S(1)}, u32[]{:S(2)}, u32[]{:S(2)}) collective-permute-start(bf16[192,128]{1,0:T(8,128)(2,1)S(1)} %get-tuple-element.61), channel_id=1, source_target_pairs={{0,12},{4,8},{8,4},{12,0},{1,13},{5,9},{9,5},{13,1},{2,14},{6,10},... | collective-permute-start | bytes 147464 | tf_op jit(solution)/shard_map/ppermute | solution.py:415
  34.2 3.6 %collective-permute-start.15 = (bf16[16,128]{1,0:T(8,128)(2,1)S(1)}, bf16[16,128]{1,0:T(8,128)(2,1)S(1)}, u32[]{:S(2)}, u32[]{:S(2)}) collective-permute-start(bf16[16,128]{1,0:T(8,128)(2,1)S(1)} %get-tuple-element.62.refs_8_), channel_id=1, source_target_pairs={{0,8},{4,12},{8,0},{12,4},{1,9},{5,13},{9,1},{13,5},{2,10},{6,14},... | collective-permute-start | bytes 12296 | tf_op jit(solution)/shard_map/ppermute | solution.py:382
  39.2 13.1 %collective-permute-start.20 = (bf16[384,128]{1,0:T(8,128)(2,1)S(1)}, bf16[384,128]{1,0:T(8,128)(2,1)S(1)}, u32[]{:S(2)}, u32[]{:S(2)}) collective-permute-start(bf16[384,128]{1,0:T(8,128)(2,1)S(1)} %get-tuple-element.70), channel_id=1, source_target_pairs={{0,3},{1,2},{2,1},{3,0},{4,7},{5,6},{6,5},{7,4},{8,11},{9,10},{10,... | collective-permute-start | bytes 294920 | tf_op jit(solution)/shard_map/ppermute | solution.py:382
  40.0 12.2 %collective-permute-start.21 = (bf16[384,128]{1,0:T(8,128)(2,1)S(1)}, bf16[384,128]{1,0:T(8,128)(2,1)S(1)}, u32[]{:S(2)}, u32[]{:S(2)}) collective-permute-start(bf16[384,128]{1,0:T(8,128)(2,1)S(1)} %get-tuple-element.71), channel_id=1, source_target_pairs={{0,2},{1,3},{2,0},{3,1},{4,6},{5,7},{6,4},{7,5},{8,10},{9,11},{10,... | collective-permute-start | bytes 294920 | tf_op jit(solution)/shard_map/ppermute | solution.py:382
  41.5 8.5 %collective-permute-start.18 = (bf16[384,128]{1,0:T(8,128)(2,1)S(1)}, bf16[384,128]{1,0:T(8,128)(2,1)S(1)}, u32[]{:S(2)}, u32[]{:S(2)}) collective-permute-start(bf16[384,128]{1,0:T(8,128)(2,1)S(1)} %get-tuple-element.69), channel_id=1, source_target_pairs={{0,1},{1,0},{2,3},{3,2},{4,5},{5,4},{6,7},{7,6},{8,9},{9,8},{10,11... | collective-permute-start | bytes 294920 | tf_op jit(solution)/shard_map/ppermute | solution.py:382
  46.9 6.8 %collective-permute-start.16 = (bf16[384,128]{1,0:T(8,128)(2,1)S(1)}, bf16[384,128]{1,0:T(8,128)(2,1)S(1)}, u32[]{:S(2)}, u32[]{:S(2)}) collective-permute-start(bf16[384,128]{1,0:T(8,128)(2,1)S(1)} %get-tuple-element.66), channel_id=1, source_target_pairs={{0,1},{1,0},{2,3},{3,2},{4,5},{5,4},{6,7},{7,6},{8,9},{9,8},{10,11... | collective-permute-start | bytes 294920 | tf_op jit(solution)/shard_map/ppermute | solution.py:382
  46.9 8.1 %collective-permute-start.17 = (bf16[384,128]{1,0:T(8,128)(2,1)S(1)}, bf16[384,128]{1,0:T(8,128)(2,1)S(1)}, u32[]{:S(2)}, u32[]{:S(2)}) collective-permute-start(bf16[384,128]{1,0:T(8,128)(2,1)S(1)} %get-tuple-element.67), channel_id=1, source_target_pairs={{0,1},{1,0},{2,3},{3,2},{4,5},{5,4},{6,7},{7,6},{8,9},{9,8},{10,11... | collective-permute-start | bytes 294920 | tf_op jit(solution)/shard_map/ppermute | solution.py:382
  50.0 6.9 %collective-permute-start.19 = (bf16[384,128]{1,0:T(8,128)(2,1)S(1)}, bf16[384,128]{1,0:T(8,128)(2,1)S(1)}, u32[]{:S(2)}, u32[]{:S(2)}) collective-permute-start(bf16[384,128]{1,0:T(8,128)(2,1)S(1)} %add_convert_fusion), channel_id=1, source_target_pairs={{0,2},{1,3},{2,0},{3,1},{4,6},{5,7},{6,4},{7,5},{8,10},{9,11},{10,... | collective-permute-start | bytes 294920 | tf_op jit(solution)/shard_map/ppermute | solution.py:382
